TPU v7x, 256 devices: a whole 4x4x8 slice. The times are simulated.
256 devices in a mesh: section: 2 (over core), expert: 64 (over y, z, x_lo), dp: 2 (over x_hi).
Axes of the slice: x: 4 (x_hi: 2, x_lo: 2; x = x_hi * 2 + x_lo), y: 4, z: 8, core: 2. Of those that a mesh axis runs over, the one named last changes fastest.
Arguments:
- activations: bfloat16 [2, 2048, 1024], P(None, ('expert', 'dp')), may hold values from -60 to 60
- cotangent: bfloat16 [2, 2048, 1024], P(None, ('expert', 'dp')), may hold values from -6 to 6
- norm_gain: float32 [2, 1024], P('section'), may hold values from 0.1 to 1.9
- w_gate: bfloat16 [2, 64, 1024, 768], P('section', 'expert', 'dp'), may hold values from -0.1875 to 0.1875
- w_up: bfloat16 [2, 64, 1024, 768], P('section', 'expert', 'dp'), may hold values from -0.1875 to 0.1875
- w_down: bfloat16 [2, 64, 768, 1024], P('section', 'expert', None, 'dp'), may hold values from -0.21875 to 0.21875
- routes: int32 [2, 2, 2048, 6], P('section', None, ('expert', 'dp')), may hold values from 0 to 63, all different within a row; in each aligned block of 16 rows (0 to 15, 16 to 31, ..., all dimensions but the last counted through in order) at most 2 rows name the same one
- gate_weights: float32 [2, 2, 2048, 6], P('section', None, ('expert', 'dp')), may hold values from 0.05 to 0.6
Outputs:
- hidden_out: bfloat16 [2, 2, 2048, 1024], P('section', None, ('expert', 'dp'))
- input_grads: bfloat16 [2, 2, 2048, 1024], P('section', None, ('expert', 'dp'))
- grad_gain: float32 [2, 1024], P('section')
- grad_gate: float32 [2, 64, 1024, 768], P('section', 'expert', 'dp')
- grad_up: float32 [2, 64, 1024, 768], P('section', 'expert', 'dp')
- grad_down: float32 [2, 64, 768, 1024], P('section', 'expert', None, 'dp')
Inputs may be any that keep to these rules, and one draw needn't show every extreme that they name: `routes`: each token names 6 different experts. Among the rows of one device (16 tokens of one layer and micro-batch) no expert is named more than 2 times, and in some blocks one is named exactly 2 times.
All inputs are finite; a program needn't handle non-finite values.
Results may differ from a plain program's by a relative error of at most 0.012.
Values may be sent and summed in bfloat16 or wider, within the bound.
No kernel may reach another device: no remote copies, remote signals or barrier semaphores. Data moves between devices by JAX's collectives and lax.ppermute only.
A program may use at most 128 MiB of HBM per device.

v0:
```python
import jax
import jax.numpy as jnp
from jax import lax
from jax.experimental import pallas as pl
from jax.experimental.pallas import tpu as pltpu
from jax.sharding import PartitionSpec as P

epsilon = 1e-06
f32 = jnp.float32
bf16 = jnp.bfloat16
every = ("section", "expert", "dp")
vmem = pl.BlockSpec(memory_space=pltpu.VMEM)
smem = pl.BlockSpec(memory_space=pltpu.SMEM)
anywhere = pl.BlockSpec(memory_space=pl.ANY)


def dot(left, right):
    return jnp.dot(left, right, preferred_element_type=f32)


def dot_nt(left, right):
    return lax.dot_general(left, right, (((1,), (1,)), ((), ())), preferred_element_type=f32)


def dot_tn(left, right):
    return lax.dot_general(left, right, (((0,), (0,)), ((), ())), preferred_element_type=f32)


def call(body, in_specs, outs, scratch=(), flops=0, moved=0, grant=16, out_spec=vmem):
    return pl.pallas_call(
        body,
        in_specs=in_specs,
        out_shape=[jax.ShapeDtypeStruct(shape, dtype) for shape, dtype in outs],
        out_specs=[out_spec] * len(outs),
        scratch_shapes=list(scratch),
        cost_estimate=pl.CostEstimate(flops=flops, bytes_accessed=moved, transcendentals=0),
        compiler_params=pltpu.CompilerParams(vmem_limit_bytes=grant * 2**20),
    )


def token_rows(block, wide):
    values = block.astype(f32)
    for j in range(8):
        wide[pl.ds(j, 16, stride=8), :] = values[:, 128 * j : 128 * (j + 1)]
    return wide[...].astype(bf16)


def token_matrix(rows, wide):
    wide[...] = rows.astype(f32)
    return [wide[pl.ds(j, 16, stride=8), :].astype(bf16) for j in range(8)]


def token_stats(block):
    values = block.astype(f32).reshape(-1, 8, 128)
    mean = jnp.sum(jnp.sum(values * values, axis=2, keepdims=True), axis=1, keepdims=True) / 1024.0
    return (values, lax.rsqrt(mean + epsilon))


def normalized(block, gain):
    values, scaling = token_stats(block)
    return (values * scaling * gain[None]).astype(bf16).reshape(block.shape)


def chunked(rows):
    return rows.astype(bf16).reshape(64, -1, 128)


def fill_tables(ids, gates, pick, high, low):
    token = lax.broadcasted_iota(jnp.int32, (16, 128), 0)
    lane = lax.broadcasted_iota(jnp.int32, (16, 128), 1)
    spread = jnp.where(lax.shift_right_logical(lane, 3) == token, 1.0, 0.0).astype(bf16)
    names = dot(ids.astype(f32).astype(bf16), spread)
    gates_high = gates.astype(bf16)
    gates_low = (gates - gates_high.astype(f32)).astype(bf16)
    upper = dot(gates_high, spread)
    lower = dot(gates_low, spread)
    expert = lax.broadcasted_iota(jnp.int32, (64, 128), 0).astype(f32)
    named = jnp.zeros((64, 128), f32)
    first = jnp.zeros((64, 128), f32)
    second = jnp.zeros((64, 128), f32)
    for k in range(ids.shape[0]):
        match = expert == names[k : k + 1, :]
        named = jnp.where(match, 1.0, named)
        first = jnp.where(match, upper[k : k + 1, :], first)
        second = jnp.where(match, lower[k : k + 1, :], second)
    row = lax.broadcasted_iota(jnp.int32, (128, 128), 0)
    column = lax.broadcasted_iota(jnp.int32, (128, 128), 1)
    earlier = ((row & 7) == 0) & (
        lax.shift_right_logical(row, 3) < lax.shift_right_logical(column, 3)
    )
    before = dot(named.astype(bf16), jnp.where(earlier, 1.0, 0.0).astype(bf16))
    code = jnp.where(named > 0.0, before + 1.0, 0.0)
    slot_row = lax.broadcasted_iota(jnp.int32, (1, 16, 128), 1)
    slot_lane = lax.broadcasted_iota(jnp.int32, (1, 16, 128), 2)
    wanted = lax.shift_right_logical(slot_row, 3).astype(f32) + 1.0
    wanted = jnp.where((slot_row & 7) == (slot_lane & 7), wanted, 9.0)
    shape = (64, 16, 128)
    match = jnp.broadcast_to(code[:, None, :], shape) == jnp.broadcast_to(wanted, shape)
    zero = jnp.zeros(shape, f32)
    pick[...] = jnp.where(match, 1.0, zero).astype(bf16).reshape(1024, 128)
    first = jnp.broadcast_to(first[:, None, :], shape)
    high[...] = jnp.where(match, first, zero).astype(bf16).reshape(1024, 128)
    second = jnp.broadcast_to(second[:, None, :], shape)
    low[...] = jnp.where(match, second, zero).astype(bf16).reshape(1024, 128)


def start_body(*refs):
    place_ref, own_routes, got_routes, own_gates, got_gates = refs[0:5]
    x_ref, grad_ref, own_gain, got_gain = refs[5:9]
    out, x_rows, grad_rows = refs[9:12]
    pick0, high0, low0, pick1, high1, low1 = refs[12:18]
    wide = refs[18]
    section = place_ref[0]
    ids = (own_routes[:, section, :], got_routes[:, section, :])
    gates = (own_gates[:, section, :], got_gates[:, section, :])
    lower = section == 0
    fill_tables(
        jnp.where(lower, ids[0], ids[1]),
        jnp.where(lower, gates[0], gates[1]),
        pick0,
        high0,
        low0,
    )
    fill_tables(
        jnp.where(lower, ids[1], ids[0]),
        jnp.where(lower, gates[1], gates[0]),
        pick1,
        high1,
        low1,
    )
    x_block = token_rows(x_ref[section], wide)
    x_rows[...] = x_block
    gain = jnp.where(lower, own_gain[...], got_gain[...])
    out[:, :16, :] = chunked(dot(pick0[...], normalized(x_block, gain)))
    grad = token_rows(grad_ref[section], wide)
    grad_rows[...] = grad
    out[:, 16:, :] = chunked(dot(high1[...], grad) + dot(low1[...], grad))


def flip_body(*refs):
    for source, target in zip(refs[:6], refs[6:]):
        target[...] = source[...].astype(f32).T.astype(bf16)


def pack_body(*refs):
    place_ref = refs[0]
    own, swapped = refs[1:4], refs[4:7]
    outs = refs[7:11]
    sems = refs[11]
    section = place_ref[0]
    start = pl.multiple_of(section * 256, 256)
    start_down = pl.multiple_of(section * 384, 128)

    def copies(sources):
        found = []
        for layer, (gate, up, down) in enumerate(sources):
            both, last = outs[2 * layer], outs[2 * layer + 1]
            found.append(
                pltpu.make_async_copy(
                    gate.at[pl.ds(start, 256), :], both.at[0:256, :], sems.at[layer, 0]
                )
            )
            found.append(
                pltpu.make_async_copy(
                    up.at[pl.ds(start, 256), :], both.at[256:512, :], sems.at[layer, 1]
                )
            )
            found.append(
                pltpu.make_async_copy(
                    down.at[pl.ds(start_down, 384), :], last, sems.at[layer, 2]
                )
            )
        return found

    @pl.when(section == 0)
    def _():
        for copy in copies((own, swapped)):
            copy.start()

    @pl.when(section != 0)
    def _():
        for copy in copies((swapped, own)):
            copy.start()

    for copy in copies((own, swapped)):
        copy.wait()


def to_matrix(rows, wide, target):
    wide[...] = rows
    slots = rows.shape[0] // 8
    for j in range(8):
        target[:, 128 * j : 128 * (j + 1)] = wide[pl.ds(j, slots, stride=8), :].astype(bf16)


def to_rows(matrix, wide):
    slots = matrix.shape[0]
    for j in range(8):
        wide[pl.ds(j, slots, stride=8), :] = matrix[:, 128 * j : 128 * (j + 1)]
    return wide[...].astype(bf16)


def fetch(place_ref, layer, sources, targets, sems):
    own, swapped = sources[0:3], sources[3:6]
    portions = (sources[6:8], sources[8:10])
    section, part = place_ref[0], place_ref[1]
    mine = pl.multiple_of(part * 512, 512)
    rest = pl.multiple_of((1 - part) * 512, 512)

    def near(group):
        found = []
        for n in range(3):
            if n < 2:
                target = targets[n].at[pl.ds(mine, 512), :]
            else:
                target = targets[n].at[:, pl.ds(mine, 512)]
            found.append(pltpu.make_async_copy(group[n], target, sems.at[n, 0]))
        return found

    def far():
        found = []
        for n in range(3):
            for p, (both, down) in enumerate(portions):
                index = section if p == 0 else 1 - section
                if n < 2:
                    start = pl.multiple_of(rest + index * 256, 256)
                    source = both.at[256 * n : 256 * (n + 1), :]
                    target = targets[n].at[pl.ds(start, 256), :]
                else:
                    start = pl.multiple_of(index * 384, 128)
                    source = down
                    target = targets[n].at[pl.ds(start, 384), pl.ds(rest, 512)]
                found.append(pltpu.make_async_copy(source, target, sems.at[n, 1 + p]))
        return found

    @pl.when(section == layer)
    def _():
        for copy in near(own):
            copy.start()

    @pl.when(section != layer)
    def _():
        for copy in near(swapped):
            copy.start()

    others = far()
    for copy in others:
        copy.start()
    waits = near(own)
    return [[waits[n], others[2 * n], others[2 * n + 1]] for n in range(3)]


def finish(group):
    for copy in group:
        copy.wait()


def gated(pre_gate, pre_up):
    return pre_gate / (1.0 + jnp.exp(-pre_gate)) * pre_up


def halves(place_ref, source, near, far):
    mine = pl.multiple_of(place_ref[1] * 512, 512)
    rest = pl.multiple_of((1 - place_ref[1]) * 512, 512)
    near[:, :512] = source[:, pl.ds(mine, 512)]
    far[:, :512] = source[:, pl.ds(rest, 512)]


def first_forward_body(*refs):
    place_ref, arrived = refs[0:2]
    sources = refs[2:12]
    result, early, early_far, gate_out, up_out = refs[12:17]
    w_gate, w_up, w_down, wide, rows, sems = refs[17:]
    waits = fetch(place_ref, 0, sources, (w_gate, w_up, w_down), sems)
    to_matrix(arrived[:, :16, :].reshape(1024, 128).astype(f32), wide, rows)
    halves(place_ref, rows, early, early_far)
    finish(waits[0])
    pre_gate = dot(rows[...], w_gate[...])
    gate_out[...] = pre_gate
    finish(waits[1])
    pre_up = dot(rows[...], w_up[...])
    up_out[...] = pre_up
    acts = gated(pre_gate, pre_up).astype(bf16)
    early[:, 512:] = acts
    early_far[:, 512:] = acts
    finish(waits[2])
    result[...] = to_rows(dot(acts, w_down[...]), wide).reshape(64, 16, 128)


def expert_grads(act_grad, pre_gate, pre_up):
    sigma = 1.0 / (1.0 + jnp.exp(-pre_gate))
    gate_grad = (act_grad * pre_up * sigma * (1.0 + pre_gate * (1.0 - sigma))).astype(bf16)
    up_grad = (act_grad * pre_gate * sigma).astype(bf16)
    return (gate_grad, up_grad)


def gain_part(pick_rows, normed_rows):
    product = pick_rows.astype(f32) * normed_rows.astype(f32)
    return jnp.sum(product.reshape(-1, 8, 128), axis=0)


def second_body(*refs):
    place_ref, arrived, cot, early0, early0_far = refs[0:5]
    sources = refs[5:15]
    picked, result, kept, beside, straight, cross, late, late_far, gain_out = refs[15:24]
    w_gate, w_up, w_down, wide, rows, grads, early, early_far, sems = refs[24:]
    waits = fetch(place_ref, 1, sources, (w_gate, w_up, w_down), sems)
    normed_rows = arrived[...].reshape(1024, 128)
    to_matrix(normed_rows.astype(f32), wide, rows)
    halves(place_ref, rows, early, early_far)
    to_matrix(cot[:, 16:, :].reshape(1024, 128).astype(f32), wide, grads)
    halves(place_ref, grads, late, late_far)
    finish(waits[0])
    pre_gate = dot(rows[...], w_gate[...])
    finish(waits[1])
    pre_up = dot(rows[...], w_up[...])
    acts = gated(pre_gate, pre_up).astype(bf16)
    early[:, 512:] = acts
    early_far[:, 512:] = acts
    finish(waits[2])
    act_grad = dot_nt(grads[...], w_down[...])
    gate_grad, up_grad = expert_grads(act_grad, pre_gate, pre_up)
    for target in (late, late_far):
        target[:, 512:1280] = gate_grad
        target[:, 1280:] = up_grad
    pick_rows = to_rows(dot_nt(gate_grad, w_gate[...]) + dot_nt(up_grad, w_up[...]), wide)
    picked[...] = pick_rows.reshape(64, 16, 128)
    gain_out[...] = gain_part(pick_rows, normed_rows)
    result[...] = to_rows(dot(acts, w_down[...]), wide).reshape(64, 16, 128)

    @pl.when(place_ref[0] == 0)
    def _():
        kept[...] = early0[...]
        beside[...] = early[...]
        straight[...] = early0_far[...]
        cross[...] = early_far[...]

    @pl.when(place_ref[0] != 0)
    def _():
        kept[...] = early[...]
        beside[...] = early0[...]
        straight[...] = early_far[...]
        cross[...] = early0_far[...]


def first_backward_body(*refs):
    place_ref, arrived, normed, pre_gate, pre_up, gain_second = refs[0:6]
    sources = refs[6:16]
    picked, late, late_far = refs[16:19]
    w_gate, w_up, w_down, wide, grads, sems = refs[19:]
    waits = fetch(place_ref, 0, sources, (w_gate, w_up, w_down), sems)
    to_matrix(arrived[:, :16, :].reshape(1024, 128).astype(f32), wide, grads)
    halves(place_ref, grads, late, late_far)
    finish(waits[2])
    act_grad = dot_nt(grads[...], w_down[...])
    gate_grad, up_grad = expert_grads(act_grad, pre_gate[...], pre_up[...])
    for target in (late, late_far):
        target[:, 512:1280] = gate_grad
        target[:, 1280:] = up_grad
    finish(waits[0])
    finish(waits[1])
    pick_rows = to_rows(dot_nt(gate_grad, w_gate[...]) + dot_nt(up_grad, w_up[...]), wide)
    picked[:, :16, :] = pick_rows.reshape(64, 16, 128)
    gain_first = gain_part(pick_rows, normed[:, :16, :].reshape(1024, 128))
    both = jnp.concatenate([gain_first, gain_second[...]], axis=0).astype(bf16)
    picked[:, 16:, :] = jnp.broadcast_to(both[None], (64, 16, 128))


def combined(high_t, low_t, rows):
    return dot(high_t[...], rows) + dot(low_t[...], rows)


def between_body(returned, x_ref, gain_ref, high_t, low_t, pick, hidden, out):
    rows = returned[...].reshape(1024, 128)
    result = (x_ref[...].astype(f32) + combined(high_t, low_t, rows)).astype(bf16)
    hidden[...] = result
    out[...] = chunked(dot(pick[...], normalized(result, gain_ref[...])))


def input_gradient(rows, upstream, x_block, gain, pick_t):
    normed_grad = dot(pick_t, rows).reshape(-1, 8, 128)
    values, scaling = token_stats(x_block)
    weighted = normed_grad * gain[None]
    mean = (
        jnp.sum(jnp.sum(weighted * values, axis=2, keepdims=True), axis=1, keepdims=True) / 1024.0
    )
    change = scaling * (weighted - values * scaling * scaling * mean)
    return (upstream.astype(f32) + change.reshape(upstream.shape)).astype(bf16)


def turn_body(returned, result, x_ref, grad_ref, gain_ref, pick_t, high, low, grad_out, out):
    rows = returned[...].reshape(1024, 128)
    grad = input_gradient(rows, grad_ref[...], x_ref[...], gain_ref[...], pick_t[...])
    grad_out[...] = grad
    out[:, :16, :] = chunked(dot(high[...], grad) + dot(low[...], grad))
    out[:, 16:, :] = result[...]


def second_output_body(place_ref, arrived, x_ref, high_t, low_t, hidden, sent):
    rows = arrived[:, 16:, :].reshape(1024, 128)
    before = x_ref[...].astype(f32)
    result = before + combined(high_t, low_t, rows)
    hidden[...] = result.astype(bf16)
    sent[...] = jnp.where(place_ref[0] == 0, result, before).astype(bf16)


def arrange(section, first, second, got, wide, out):
    mine = jnp.where(section == 0, first.astype(f32), second.astype(f32))
    for index, rows in ((section, mine), (1 - section, got)):
        for j, piece in enumerate(token_matrix(rows, wide)):
            out[index, :, 128 * j : 128 * (j + 1)] = piece


def hidden_body(place_ref, first, second, got, out, wide):
    arrange(place_ref[0], first[...], second[...], got[...], wide, out)


def last_body(place_ref, returned, x_ref, grad_ref, gain_ref, pick_t, grad_out, sent, gain_out):
    rows = returned[:, :16, :].reshape(1024, 128)
    grad = input_gradient(rows, grad_ref[...], x_ref[...], gain_ref[...], pick_t[...])
    grad_out[...] = grad
    sent[...] = jnp.where(
        place_ref[0] == 0, grad_ref[...].astype(f32), grad.astype(f32)
    ).astype(bf16)
    gain_out[...] = jnp.sum(returned[:, 16:, :].astype(f32), axis=0)


def final_body(*refs):
    place_ref, first, second, got = refs[0:4]
    gain_rows, gain_beside, gain_straight, gain_cross, own_gain = refs[4:9]
    out, gain_out, wide = refs[9:]
    arrange(place_ref[0], first[...], second[...], got[...], wide, out)
    total = (gain_rows[...] + gain_beside[...]) + (gain_straight[...] + gain_cross[...])
    gain_out[...] = jnp.where(place_ref[0] == 0, total[:8], total[8:]) / own_gain[...]


def weight_body(*refs):
    place_ref = refs[0]
    early_parts, first, second = refs[1:5], refs[5:9], refs[9:13]
    outs = refs[13:16]
    early, late, gate, up, down, sems, out_sems = refs[16:]

    def copies(target, group, row):
        return [
            pltpu.make_async_copy(group[n], target.at[pl.ds(128 * n, 128), :], sems.at[row, n])
            for n in range(4)
        ]

    @pl.when(place_ref[0] == 0)
    def _():
        for copy in copies(late, first, 1):
            copy.start()

    @pl.when(place_ref[0] != 0)
    def _():
        for copy in copies(late, second, 1):
            copy.start()

    for copy in copies(early, early_parts, 0):
        copy.start()
    for copy in copies(early, early_parts, 0) + copies(late, first, 1):
        copy.wait()
    normed = early[:, :512]
    done = []
    for n, target in enumerate((gate, up, down)):
        if n < 2:
            target[...] = dot_tn(normed, late[:, 512 + 768 * n : 1280 + 768 * n])
        else:
            target[...] = dot_tn(early[:, 512:], late[:, :512])
        copy = pltpu.make_async_copy(target, outs[n], out_sems.at[n])
        copy.start()
        done.append(copy)
    for copy in done:
        copy.wait()


def after(block, other):
    return lax.optimization_barrier((block, other))[0]


def window(activations, cotangent, norm_gain, w_gate, w_up, w_down, routes, gate_weights):
    section = lax.axis_index("section")
    part = lax.axis_index("dp")
    experts = lax.axis_size("expert")
    place = jnp.stack([section, part]).astype(jnp.int32)
    micro_count, tokens, width = activations.shape
    swap = [(0, 1), (1, 0)]

    def flat(s, e, d):
        return (s * experts + e) * 2 + d

    def pairs(layer, cross):
        found = []
        for s in range(2):
            target = 1 - s if cross else s
            if layer is None or target == layer:
                found += [
                    (flat(s, e, d), flat(target, e, 1 - d))
                    for e in range(experts)
                    for d in range(2)
                ]
        return found

    def beside(block, route=swap):
        return lax.ppermute(block, "section", route)

    def away(block, layer=None, cross=False):
        return lax.ppermute(block, every, pairs(layer, cross))

    def exchange(block):
        return lax.all_to_all(block, "expert", split_axis=0, concat_axis=0, tiled=True)

    own = (w_gate[0, 0], w_up[0, 0], w_down[0, 0])
    own_gain = norm_gain.reshape(8, 128)
    own_routes = routes[0].transpose(2, 0, 1)
    own_gates = gate_weights[0].transpose(2, 0, 1)
    got_routes = beside(own_routes)
    got_gates = beside(own_gates)
    got_gain = beside(own_gain)
    swapped = tuple(beside(w) for w in own)

    big = ((64, 32, 128), bf16)
    small = ((64, 16, 128), bf16)
    block = ((128, 128), bf16)
    early_shape = ((128, 1280), bf16)
    late_shape = ((128, 2048), bf16)
    down = ((1024, 128), bf16)
    across = ((128, 1024), bf16)
    weight_scratch = [
        pltpu.VMEM((1024, 768), bf16),
        pltpu.VMEM((1024, 768), bf16),
        pltpu.VMEM((768, 1024), bf16),
    ]
    wide = pltpu.VMEM((1024, 128), f32)
    narrow = pltpu.VMEM((128, 128), f32)
    matrix = pltpu.VMEM((128, 1024), bf16)
    sems = pltpu.SemaphoreType.DMA((3, 3))

    out_first, x_first, grad_last, *maps = call(
        start_body,
        [smem] + [vmem] * 8,
        [big, block, block] + [down] * 6,
        [narrow],
        flops=10**8,
        moved=2 * 10**6,
    )(
        place,
        own_routes,
        got_routes,
        own_gates,
        got_gates,
        activations,
        cotangent,
        own_gain,
        got_gain,
    )
    _, high0, low0, pick1, _, _ = maps
    first_gain = jnp.where(section == 0, own_gain, got_gain)
    second_gain = jnp.where(section == 0, got_gain, own_gain)

    packed = call(
        pack_body,
        [smem] + [anywhere] * 6,
        [((512, 768), bf16), ((384, 512), bf16)] * 2,
        [pltpu.SemaphoreType.DMA((2, 3))],
        flops=1,
        moved=5 * 10**6,
    )(place, *own, *swapped)
    portions0 = [away(w) for w in packed[:2]]
    portions0 += [beside(w) for w in portions0]
    arrived_first = exchange(out_first)

    flipped = call(flip_body, [vmem] * 6, [across] * 6, flops=10**6, moved=3 * 10**6)(*maps)
    pick0_t, high0_t, low0_t, pick1_t, high1_t, low1_t = flipped

    result, early0, early0_far, pre_gate, pre_up = call(
        first_forward_body,
        [smem, vmem] + [anywhere] * 10,
        [small, early_shape, early_shape, ((128, 768), f32), ((128, 768), f32)],
        weight_scratch + [wide, matrix, sems],
        flops=6 * 10**8,
        moved=6 * 10**6,
    )(place, arrived_first, *own, *swapped, *portions0)
    returned = exchange(result)

    portions1 = [away(after(w, other)) for w, other in zip(packed[2:], portions0)]
    portions1 += [beside(w) for w in portions1]

    hidden_first, out_second = call(
        between_body, [vmem] * 6, [block, small], flops=10**8, moved=2 * 10**6
    )(returned, x_first, second_gain, high0_t, low0_t, pick1)
    arrived_second = exchange(out_second)

    picked, result_second, kept, sent, straight, cross, late1, late1_far, gain_second = call(
        second_body,
        [smem] + [vmem] * 4 + [anywhere] * 10,
        [small, small] + [early_shape] * 4 + [late_shape] * 2 + [((8, 128), f32)],
        weight_scratch
        + [wide, matrix, matrix, pltpu.VMEM((128, 1280), bf16), pltpu.VMEM((128, 1280), bf16), sems],
        flops=12 * 10**8,
        moved=8 * 10**6,
        grant=20,
    )(place, arrived_second, arrived_first, early0, early0_far, *own, *swapped, *portions1)
    returned = exchange(picked)

    early_parts = (kept, beside(sent), away(straight), away(cross, cross=True))
    late1_parts = (late1, beside(late1, [(0, 1)]), away(late1_far, 1), away(late1_far, 1, True))

    grad_middle, out_third = call(
        turn_body, [vmem] * 8, [block, big], flops=10**8, moved=2 * 10**6
    )(
        returned,
        result_second,
        hidden_first,
        grad_last,
        second_gain,
        pick1_t,
        high0,
        low0,
    )
    arrived_third = exchange(out_third)

    picked, late0, late0_far = call(
        first_backward_body,
        [smem] + [vmem] * 5 + [anywhere] * 10,
        [big, late_shape, late_shape],
        weight_scratch + [wide, matrix, sems],
        flops=6 * 10**8,
        moved=8 * 10**6,
    )(
        place,
        arrived_third,
        arrived_first,
        pre_gate,
        pre_up,
        gain_second,
        *own,
        *swapped,
        *portions0,
    )
    late0_parts = (late0, beside(late0, [(1, 0)]), away(late0_far, 0), away(late0_far, 0, True))
    returned = exchange(picked)

    hidden_second, hidden_sent = call(
        second_output_body, [smem] + [vmem] * 4, [block, block], flops=10**8, moved=10**6
    )(place, arrived_third, hidden_first, high1_t, low1_t)
    both = ((micro_count, tokens, width), bf16)
    hidden = call(
        hidden_body, [smem] + [vmem] * 3, [both], [narrow], flops=10**5, moved=10**5
    )(place, hidden_first, hidden_second, beside(hidden_sent))[0]

    weight_grads = call(
        weight_body,
        [smem] + [anywhere] * 12,
        [((512, 768), f32), ((512, 768), f32), ((768, 512), f32)],
        [
            pltpu.VMEM((512, 1280), bf16),
            pltpu.VMEM((512, 2048), bf16),
            pltpu.VMEM((512, 768), f32),
            pltpu.VMEM((512, 768), f32),
            pltpu.VMEM((768, 512), f32),
            pltpu.SemaphoreType.DMA((2, 4)),
            pltpu.SemaphoreType.DMA((3,)),
        ],
        flops=12 * 10**8,
        moved=8 * 10**6,
        grant=24,
        out_spec=anywhere,
    )(place, *early_parts, *late0_parts, *late1_parts)

    grad_first, grad_sent, gain_rows = call(
        last_body, [smem] + [vmem] * 5, [block, block, ((16, 128), f32)], flops=10**8, moved=10**6
    )(place, returned, x_first, grad_middle, first_gain, pick0_t)
    grads, gain_grad = call(
        final_body, [smem] + [vmem] * 8, [both, ((8, 128), f32)], [narrow], flops=10**5, moved=10**5
    )(
        place,
        grad_first,
        grad_middle,
        beside(grad_sent),
        gain_rows,
        beside(gain_rows),
        away(gain_rows),
        away(gain_rows, cross=True),
        own_gain,
    )
    return (
        hidden[None],
        grads[None],
        gain_grad.reshape(1, width),
        weight_grads[0][None, None],
        weight_grads[1][None, None],
        weight_grads[2][None, None],
    )


def solution(mesh):
    placed = (
        P(None, ("expert", "dp"), None),
        P(None, ("expert", "dp"), None),
        P("section", None),
        P("section", "expert", "dp", None),
        P("section", "expert", "dp", None),
        P("section", "expert", None, "dp"),
        P("section", None, ("expert", "dp"), None),
        P("section", None, ("expert", "dp"), None),
    )
    return jax.shard_map(
        window,
        mesh=mesh,
        in_specs=placed,
        out_specs=(
            P("section", None, ("expert", "dp"), None),
            P("section", None, ("expert", "dp"), None),
            P("section", None),
            P("section", "expert", "dp", None),
            P("section", "expert", "dp", None),
            P("section", "expert", None, "dp"),
        ),
        check_vma=False,
    )
```

profile of v0, /device:TPU:4, one launch (start us, length us, event | category | flops | bytes accessed | tf_op | source)
XLA Modules:
  0.0 258.0 jit_solution(17204723388014169369)
XLA Ops:
  1.4 1.8 collective-permute-done.3.refs_4_.refs_5_.refs_8_.refs_9_
  3.2 1.1 collective-permute-done.4.refs_5_.refs_6_.refs_9_.refs_10_
  6.3 1.1 copy-done
  7.5 1.1 copy-done.2
  8.6 1.1 copy-done.4
  9.7 1.1 copy-done.11
  10.9 2.6 %shard_map.128 = (bf16[512,768]{1,0:T(8,128)(2,1)}, bf16[384,512]{1,0:T(8,128)(2,1)S(1)}, bf16[512,768]{1,0:T(8,128)(2,1)S(1)}, bf16[384,512]{1,0:T(8,128)(2,1)S(1)}) custom-call(s32[2]{0:T(128)S(1)} %pad_add_fusion.refs_0_.place_ref, bf16[512,768]{1,0:T(8,128)(2,1)S(1)} %bitcast.19, bf16[512,768]{1,0:T(8,128)(2,1)S(1)} %bitcast.24, ...), custom_call_target="tpu_custom_call" | custom-call | flops 1 | bytes 5000000 | tf_op jit(solution)/shard_map/pallas_call | solution.py:561
  16.9 2.2 collective-permute-start.6
  20.9 1.4 shard_map.127
  28.7 12.2 %all-to-all-start = ((bf16[64,32,128]{2,1,0:T(8,128)(2,1)}), bf16[64,32,128]{2,1,0:T(8,128)(2,1)}, u32[]{:S(2)}, u32[]{:S(2)}) async-start(bf16[64,32,128]{2,1,0:T(8,128)(2,1)} %copy-done.25), calls=%async_computation | async-start | bytes 1048576 | tf_op jit(solution)/shard_map/all_to_all | solution.py:511
  40.9 1.6 collective-permute-start.7
  42.5 2.0 collective-permute-start.10
  44.5 14.4 %collective-permute-done.7.refs_9_.refs_13_ = bf16[384,512]{1,0:T(8,128)(2,1)S(1)} collective-permute-done((bf16[384,512]{1,0:T(8,128)(2,1)}, bf16[384,512]{1,0:T(8,128)(2,1)S(1)}, u32[]{:S(2)}, u32[]{:S(2)}) %collective-permute-start.7) | collective-permute-done | bytes 393248 | tf_op jit(solution)/shard_map/ppermute | solution.py:508
  58.9 1.8 collective-permute-done.9.refs_11_.refs_15_
  61.9 1.1 copy-done.12
  63.0 3.8 %shard_map.129 = (bf16[64,16,128]{2,1,0:T(8,128)(2,1)S(1)}, bf16[128,1280]{1,0:T(8,128)(2,1)S(1)}, bf16[128,1280]{1,0:T(8,128)(2,1)S(1)}, f32[128,768]{1,0:T(8,128)S(1)}, f32[128,768]{1,0:T(8,128)S(1)}) custom-call(s32[2]{0:T(128)S(1)} %pad_add_fusion.refs_0_.place_ref, bf16[64,32,128]{2,1,0:T(8,128)(2,1)} %all-to-all-done.refs_1_.refs_2_, ...), custom_call_target="tpu_custom_call" | custom-call | flops 600000000 | bytes 6000000 | tf_op jit(solution)/shard_map/pallas_call | solution.py:576
  70.4 10.6 %all-to-all-start.1 = ((bf16[64,16,128]{2,1,0:T(8,128)(2,1)}), bf16[64,16,128]{2,1,0:T(8,128)(2,1)}, u32[]{:S(2)}, u32[]{:S(2)}) async-start(bf16[64,16,128]{2,1,0:T(8,128)(2,1)} %copy-done.59), calls=%async_computation.1 | async-start | bytes 524288 | tf_op jit(solution)/shard_map/all_to_all | solution.py:511
  81.1 1.3 collective-permute-start.11
  97.2 1.5 shard_map.131
  100.1 12.0 %all-to-all-start.2 = ((bf16[64,16,128]{2,1,0:T(8,128)(2,1)}), bf16[64,16,128]{2,1,0:T(8,128)(2,1)}, u32[]{:S(2)}, u32[]{:S(2)}) async-start(bf16[64,16,128]{2,1,0:T(8,128)(2,1)} %copy-done.60), calls=%async_computation.2 | async-start | bytes 524288 | tf_op jit(solution)/shard_map/all_to_all | solution.py:511
  112.4 1.7 collective-permute-done.13.refs_14_
  114.9 9.8 %all-to-all-done.2.refs_1_ = bf16[64,16,128]{2,1,0:T(8,128)(2,1)} async-done(((bf16[64,16,128]{2,1,0:T(8,128)(2,1)}), bf16[64,16,128]{2,1,0:T(8,128)(2,1)}, u32[]{:S(2)}, u32[]{:S(2)}) %all-to-all-start.2) | async-done | bytes 262176 | tf_op jit(solution)/shard_map/all_to_all | solution.py:511
  124.7 1.1 copy-done.8
  125.8 1.1 copy-done.13
  129.9 5.8 %shard_map.132 = (bf16[64,16,128]{2,1,0:T(8,128)(2,1)S(1)}, bf16[64,16,128]{2,1,0:T(8,128)(2,1)S(1)}, bf16[128,1280]{1,0:T(8,128)(2,1)S(1)}, bf16[128,1280]{1,0:...) custom-call(s32[2]{0:T(128)S(1)} %pad_add_fusion.refs_0_.place_ref, ...), custom_call_target="tpu_custom_call" | custom-call | flops 1200000000 | bytes 8000000 | tf_op jit(solution)/shard_map/pallas_call | solution.py:594
  137.2 17.7 %all_to_all.30.returned = bf16[64,16,128]{2,1,0:T(8,128)(2,1)S(1)} all-to-all(bf16[64,16,128]{2,1,0:T(8,128)(2,1)S(1)} %get-tuple-element.79), channel_id=1, replica_groups=mesh['section'=2,'expert'=64,'dp'=2] {'expert'}, dimensions={0} | all-to-all | bytes 524288 | tf_op jit(solution)/shard_map/all_to_all | solution.py:511
  157.0 6.2 %all-to-all-start.4 = ((bf16[64,32,128]{2,1,0:T(8,128)(2,1)}), bf16[64,32,128]{2,1,0:T(8,128)(2,1)}, u32[]{:S(2)}, u32[]{:S(2)}) async-start(bf16[64,32,128]{2,1,0:T(8,128)(2,1)} %copy-done.26), calls=%async_computation.4 | async-start | bytes 1048576 | tf_op jit(solution)/shard_map/all_to_all | solution.py:511
  163.3 2.1 collective-permute-start.25
  165.4 14.8 %all-to-all-done.4.arrived.refs_1_ = bf16[64,32,128]{2,1,0:T(8,128)(2,1)} async-done(((bf16[64,32,128]{2,1,0:T(8,128)(2,1)}), bf16[64,32,128]{2,1,0:T(8,128)(2,1)}, u32[]{:S(2)}, u32[]{:S(2)}) %all-to-all-start.4) | async-done | bytes 524320 | tf_op jit(solution)/shard_map/all_to_all | solution.py:511
  180.2 1.1 copy-done.9
  181.4 1.1 copy-done.14
  185.2 5.6 %shard_map.136 = (bf16[64,32,128]{2,1,0:T(8,128)(2,1)S(1)}, bf16[128,2048]{1,0:T(8,128)(2,1)S(1)}, bf16[128,2048]{1,0:T(8,128)(2,1)S(1)}) custom-call(s32[2]{0:T(128)S(1)} %pad_add_fusion.refs_0_.place_ref, bf16[64,32,128]{2,1,0:T(8,128)(2,1)} %all-to-all-done.4.arrived.refs_1_, bf16[64,32,128]{2,1,0:T(8,128)(2,1)} %all-to-all-done.refs_1_.refs_2_, ...), custom_call_target="tpu_custom_call" | custom-call | flops 600000000 | bytes 8000000 | tf_op jit(solution)/shard_map/pallas_call | solution.py:623
  193.2 6.1 %all-to-all-start.5 = ((bf16[64,32,128]{2,1,0:T(8,128)(2,1)}), bf16[64,32,128]{2,1,0:T(8,128)(2,1)S(1)}, u32[]{:S(2)}, u32[]{:S(2)}) async-start(bf16[64,32,128]{2,1,0:T(8,128)(2,1)} %copy-done.24), calls=%async_computation.5 | async-start | bytes 1048576 | tf_op jit(solution)/shard_map/all_to_all | solution.py:511
  199.4 1.4 collective-permute-start.20
  200.8 2.0 collective-permute-start.21
  205.4 1.3 shard_map.134
  208.2 2.6 %collective-permute-start.27 = (bf16[128,2048]{1,0:T(8,128)(2,1)}, bf16[128,2048]{1,0:T(8,128)(2,1)S(1)}, u32[]{:S(2)}, u32[]{:S(2)}) collective-permute-start(bf16[128,2048]{1,0:T(8,128)(2,1)} %copy-done.89), channel_id=1, source_target_pairs={{0,129},{1,128},{2,131},{3,130},{4,133},{5,132},{6,135},{7,134},{8... | collective-permute-start | bytes 1572872 | tf_op jit(solution)/shard_map/ppermute | solution.py:508
  210.8 4.7 %collective-permute-done.20.refs_3_ = bf16[128,1280]{1,0:T(8,128)(2,1)S(1)} collective-permute-done((bf16[128,1280]{1,0:T(8,128)(2,1)}, bf16[128,1280]{1,0:T(8,128)(2,1)S(1)}, u32[]{:S(2)}, u32[]{:S(2)}) %collective-permute-start.20) | collective-permute-done | bytes 327712 | tf_op jit(solution)/shard_map/ppermute | solution.py:508
  216.9 4.4 %collective-permute-done.21.refs_4_ = bf16[128,1280]{1,0:T(8,128)(2,1)S(1)} collective-permute-done((bf16[128,1280]{1,0:T(8,128)(2,1)}, bf16[128,1280]{1,0:T(8,128)(2,1)S(1)}, u32[]{:S(2)}, u32[]{:S(2)}) %collective-permute-start.21) | collective-permute-done | bytes 327712 | tf_op jit(solution)/shard_map/ppermute | solution.py:508
  222.1 1.3 collective-permute-start.22
  223.4 1.3 collective-permute-start.24
  224.7 4.2 %collective-permute-start.23 = (bf16[128,2048]{1,0:T(8,128)(2,1)}, bf16[128,2048]{1,0:T(8,128)(2,1)}, u32[]{:S(2)}, u32[]{:S(2)}) collective-permute-start(bf16[128,2048]{1,0:T(8,128)(2,1)} %copy-done.90), channel_id=1, source_target_pairs={{0,1},{1,0},{2,3},{3,2},{4,5},{5,4},{6,7},{7,6},{8,9},{9,8},{10,11... | collective-permute-start | bytes 1572872 | tf_op jit(solution)/shard_map/ppermute | solution.py:508
  228.9 1.2 shard_map.135
  232.7 3.3 %collective-permute-start.18 = (f32[16,128]{1,0:T(8,128)S(1)}, f32[16,128]{1,0:T(8,128)S(1)}, u32[]{:S(2)}, u32[]{:S(2)}) collective-permute-start(f32[16,128]{1,0:T(8,128)S(1)} %get-tuple-element.96.refs_4_), channel_id=1, source_target_pairs={{0,129},{1,128},{2,131},{3,130},{4,133},{5,132},{6,135},{7,134},{8... | collective-permute-start | bytes 24584 | tf_op jit(solution)/shard_map/ppermute | solution.py:508
  236.8 2.0 collective-permute-start.17
  238.8 5.1 %collective-permute-done.24.refs_8_ = bf16[128,2048]{1,0:T(8,128)(2,1)} collective-permute-done((bf16[128,2048]{1,0:T(8,128)(2,1)}, bf16[128,2048]{1,0:T(8,128)(2,1)}, u32[]{:S(2)}, u32[]{:S(2)}) %collective-permute-start.24) | collective-permute-done | bytes 524320 | tf_op jit(solution)/shard_map/ppermute | solution.py:508
  251.8 4.9 %shard_map.139 = (f32[512,768]{1,0:T(8,128)}, f32[512,768]{1,0:T(8,128)}, f32[768,512]{1,0:T(8,128)}) custom-call(s32[2]{0:T(128)S(1)} %pad_add_fusion.refs_0_.place_ref, bf16[128,1280]{1,0:T(8,128)(2,1)S(1)} %copy-done.43, bf16[128,1280]{1,0:T(8,128)(2,1)S(1)} %copy-done.45, bf16[128,1280]{1,0:T(8,128)(2,1)S(1)} %copy-done.47, ...), custom_call_target="tpu_custom_call" | custom-call | flops 1200000000 | bytes 8000000 | tf_op jit(solution)/shard_map/pallas_call | solution.py:652
  256.8 1.2 shard_map.138
  (234 shorter events, 65.4 us)
Async XLA Ops:
  0.6 2.6 %collective-permute-start.3 = (bf16[512,768]{1,0:T(8,128)(2,1)}, bf16[512,768]{1,0:T(8,128)(2,1)S(1)}, u32[]{:S(2)}, u32[]{:S(2)}) collective-permute-start(bf16[512,768]{1,0:T(8,128)(2,1)} %bitcast.18), channel_id=1, source_target_pairs={{0,128},{128,0},{1,129},{129,1},{2,130},{130,2},{3,131},{131,3},{4... | collective-permute-start | bytes 2359304 | tf_op jit(solution)/shard_map/ppermute | solution.py:505
  0.7 3.6 %collective-permute-start.4 = (bf16[512,768]{1,0:T(8,128)(2,1)}, bf16[512,768]{1,0:T(8,128)(2,1)S(1)}, u32[]{:S(2)}, u32[]{:S(2)}) collective-permute-start(bf16[512,768]{1,0:T(8,128)(2,1)} %bitcast.23), channel_id=1, source_target_pairs={{0,128},{128,0},{1,129},{129,1},{2,130},{130,2},{3,131},{131,3},{4... | collective-permute-start | bytes 2359304 | tf_op jit(solution)/shard_map/ppermute | solution.py:505
  1.2 4.2 %collective-permute-start.5 = (bf16[768,512]{1,0:T(8,128)(2,1)}, bf16[768,512]{1,0:T(8,128)(2,1)S(1)}, u32[]{:S(2)}, u32[]{:S(2)}) collective-permute-start(bf16[768,512]{1,0:T(8,128)(2,1)} %bitcast.28), channel_id=1, source_target_pairs={{0,128},{128,0},{1,129},{129,1},{2,130},{130,2},{3,131},{131,3},{4... | collective-permute-start | bytes 2359304 | tf_op jit(solution)/shard_map/ppermute | solution.py:505
  10.9 49.8 %copy-start.3 = (bf16[1,1,512,768]{3,2,1,0:T(8,128)(2,1)S(1)}, bf16[1,1,512,768]{3,2,1,0:T(8,128)(2,1)}, u32[]{:S(2)}) copy-start(bf16[1,1,512,768]{3,2,1,0:T(8,128)(2,1)} %param.12) | copy-start | bytes 2359300
  10.9 49.8 %copy-start.5 = (bf16[1,1,768,512]{3,2,1,0:T(8,128)(2,1)S(1)}, bf16[1,1,768,512]{3,2,1,0:T(8,128)(2,1)}, u32[]{:S(2)}) copy-start(bf16[1,1,768,512]{3,2,1,0:T(8,128)(2,1)} %param.13) | copy-start | bytes 2359300
  16.9 43.8 %copy-start.1 = (bf16[1,1,512,768]{3,2,1,0:T(8,128)(2,1)S(1)}, bf16[1,1,512,768]{3,2,1,0:T(8,128)(2,1)}, u32[]{:S(2)}) copy-start(bf16[1,1,512,768]{3,2,1,0:T(8,128)(2,1)} %param.11) | copy-start | bytes 2359300
  16.9 25.5 %collective-permute-start.6 = (bf16[512,768]{1,0:T(8,128)(2,1)}, bf16[512,768]{1,0:T(8,128)(2,1)}, u32[]{:S(2)}, u32[]{:S(2)}) collective-permute-start(bf16[512,768]{1,0:T(8,128)(2,1)} %get-tuple-element.59), channel_id=1, source_target_pairs={{0,1},{1,0},{2,3},{3,2},{4,5},{5,4},{6,7},{7,6},{8,9},{9,8},{10,11... | collective-permute-start | bytes 2359304 | tf_op jit(solution)/shard_map/ppermute | solution.py:508
  19.1 1.7 collective-permute-start.2
  19.2 1.3 collective-permute-start
  19.7 1.2 collective-permute-start.1
  28.7 30.3 %all-to-all-start = ((bf16[64,32,128]{2,1,0:T(8,128)(2,1)}), bf16[64,32,128]{2,1,0:T(8,128)(2,1)}, u32[]{:S(2)}, u32[]{:S(2)}) async-start(bf16[64,32,128]{2,1,0:T(8,128)(2,1)} %copy-done.25), calls=%async_computation | async-start | bytes 1048576 | tf_op jit(solution)/shard_map/all_to_all | solution.py:511
  40.9 18.0 %collective-permute-start.7 = (bf16[384,512]{1,0:T(8,128)(2,1)}, bf16[384,512]{1,0:T(8,128)(2,1)S(1)}, u32[]{:S(2)}, u32[]{:S(2)}) collective-permute-start(bf16[384,512]{1,0:T(8,128)(2,1)} %copy-done.92), channel_id=1, source_target_pairs={{0,1},{1,0},{2,3},{3,2},{4,5},{5,4},{6,7},{7,6},{8,9},{9,8},{10,11... | collective-permute-start | bytes 1179656 | tf_op jit(solution)/shard_map/ppermute | solution.py:508
  42.5 18.2 %collective-permute-start.8 = (bf16[512,768]{1,0:T(8,128)(2,1)}, bf16[512,768]{1,0:T(8,128)(2,1)}, u32[]{:S(2)}, u32[]{:S(2)}) collective-permute-start(bf16[512,768]{1,0:T(8,128)(2,1)} %collective-permute-done.6.refs_8_.refs_12_), channel_id=1, source_target_pairs={{0,128},{128,0},{1,129},{129,1},{2,130},{130,2},{3,131},{131,3},{4... | collective-permute-start | bytes 2359304 | tf_op jit(solution)/shard_map/ppermute | solution.py:505
  42.5 39.9 %collective-permute-start.10 = (bf16[512,768]{1,0:T(8,128)(2,1)}, bf16[512,768]{1,0:T(8,128)(2,1)}, u32[]{:S(2)}, u32[]{:S(2)}) collective-permute-start(bf16[512,768]{1,0:T(8,128)(2,1)} %copy-done.88), channel_id=1, source_target_pairs={{0,1},{1,0},{2,3},{3,2},{4,5},{5,4},{6,7},{7,6},{8,9},{9,8},{10,11... | collective-permute-start | bytes 2359304 | tf_op jit(solution)/shard_map/ppermute | solution.py:508
  58.8 1.9 collective-permute-start.9
  70.4 23.2 %all-to-all-start.1 = ((bf16[64,16,128]{2,1,0:T(8,128)(2,1)}), bf16[64,16,128]{2,1,0:T(8,128)(2,1)}, u32[]{:S(2)}, u32[]{:S(2)}) async-start(bf16[64,16,128]{2,1,0:T(8,128)(2,1)} %copy-done.59), calls=%async_computation.1 | async-start | bytes 524288 | tf_op jit(solution)/shard_map/all_to_all | solution.py:511
  81.1 31.0 %collective-permute-start.11 = (bf16[384,512]{1,0:T(8,128)(2,1)}, bf16[384,512]{1,0:T(8,128)(2,1)}, u32[]{:S(2)}, u32[]{:S(2)}) collective-permute-start(bf16[384,512]{1,0:T(8,128)(2,1)} %copy-done.91), channel_id=1, source_target_pairs={{0,1},{1,0},{2,3},{3,2},{4,5},{5,4},{6,7},{7,6},{8,9},{9,8},{10,11... | collective-permute-start | bytes 1179656 | tf_op jit(solution)/shard_map/ppermute | solution.py:508
  82.4 32.5 %collective-permute-start.12 = (bf16[512,768]{1,0:T(8,128)(2,1)}, bf16[512,768]{1,0:T(8,128)(2,1)}, u32[]{:S(2)}, u32[]{:S(2)}) collective-permute-start(bf16[512,768]{1,0:T(8,128)(2,1)} %collective-permute-done.10.refs_11_), channel_id=1, source_target_pairs={{0,128},{128,0},{1,129},{129,1},{2,130},{130,2},{3,131},{131,3},{4... | collective-permute-start | bytes 2359304 | tf_op jit(solution)/shard_map/ppermute | solution.py:505
  100.1 24.6 %all-to-all-start.2 = ((bf16[64,16,128]{2,1,0:T(8,128)(2,1)}), bf16[64,16,128]{2,1,0:T(8,128)(2,1)}, u32[]{:S(2)}, u32[]{:S(2)}) async-start(bf16[64,16,128]{2,1,0:T(8,128)(2,1)} %copy-done.60), calls=%async_computation.2 | async-start | bytes 524288 | tf_op jit(solution)/shard_map/all_to_all | solution.py:511
  112.1 2.0 collective-permute-start.13
  129.9 25.1 %copy-start.17 = (bf16[1024,128]{1,0:T(8,128)(2,1)S(1)}, bf16[1024,128]{1,0:T(8,128)(2,1)}, u32[]{:S(2)}) copy-start(bf16[1024,128]{1,0:T(8,128)(2,1)} %copy-done.15) | copy-start | bytes 786436
  129.9 25.1 %copy-start.20 = (bf16[1024,128]{1,0:T(8,128)(2,1)S(1)}, bf16[1024,128]{1,0:T(8,128)(2,1)}, u32[]{:S(2)}) copy-start(bf16[1024,128]{1,0:T(8,128)(2,1)} %copy-done.18) | copy-start | bytes 786436
  129.9 25.1 %copy-start.55 = (bf16[128,128]{1,0:T(8,128)(2,1)S(1)}, bf16[128,128]{1,0:T(8,128)(2,1)}, u32[]{:S(2)}) copy-start(bf16[128,128]{1,0:T(8,128)(2,1)} %copy-done.54) | copy-start | bytes 98308
  129.9 25.1 %copy-start.72 = (bf16[128,1024]{1,0:T(8,128)(2,1)S(1)}, bf16[128,1024]{1,0:T(8,128)(2,1)}, u32[]{:S(2)}) copy-start(bf16[128,1024]{1,0:T(8,128)(2,1)} %copy-done.71) | copy-start | bytes 786436
  129.9 25.1 %copy-start.83 = (bf16[128,128]{1,0:T(8,128)(2,1)S(1)}, bf16[128,128]{1,0:T(8,128)(2,1)}, u32[]{:S(2)}) copy-start(bf16[128,128]{1,0:T(8,128)(2,1)} %copy-done.82) | copy-start | bytes 98308
  137.2 18.4 %copy-start.85 = (f32[8,128]{1,0:T(8,128)}, f32[8,128]{1,0:T(8,128)S(1)}, u32[]{:S(2)}) copy-start(f32[8,128]{1,0:T(8,128)S(1)} %get-tuple-element.90.refs_5_) | copy-start | bytes 12292
  137.2 18.4 %copy-start.89 = (bf16[128,2048]{1,0:T(8,128)(2,1)}, bf16[128,2048]{1,0:T(8,128)(2,1)S(1)}, u32[]{:S(2)}) copy-start(bf16[128,2048]{1,0:T(8,128)(2,1)S(1)} %get-tuple-element.106) | copy-start | bytes 1572868
  137.2 18.4 %copy-start.93 = (bf16[128,1280]{1,0:T(8,128)(2,1)}, bf16[128,1280]{1,0:T(8,128)(2,1)S(1)}, u32[]{:S(2)}) copy-start(bf16[128,1280]{1,0:T(8,128)(2,1)S(1)} %get-tuple-element.102) | copy-start | bytes 983044
  157.0 23.2 %all-to-all-start.4 = ((bf16[64,32,128]{2,1,0:T(8,128)(2,1)}), bf16[64,32,128]{2,1,0:T(8,128)(2,1)}, u32[]{:S(2)}, u32[]{:S(2)}) async-start(bf16[64,32,128]{2,1,0:T(8,128)(2,1)} %copy-done.26), calls=%async_computation.4 | async-start | bytes 1048576 | tf_op jit(solution)/shard_map/all_to_all | solution.py:511
  163.3 60.1 %collective-permute-start.25 = (bf16[128,2048]{1,0:T(8,128)(2,1)}, bf16[128,2048]{1,0:T(8,128)(2,1)}, u32[]{:S(2)}, u32[]{:S(2)}) collective-permute-start(bf16[128,2048]{1,0:T(8,128)(2,1)} %copy-done.27), channel_id=1, source_target_pairs={{0,128},{1,129},{2,130},{3,131},{4,132},{5,133},{6,134},{7,135},{8... | collective-permute-start | bytes 1572872 | tf_op jit(solution)/shard_map/ppermute | solution.py:505
  193.2 36.9 %copy-start.79 = (bf16[128,128]{1,0:T(8,128)(2,1)S(1)}, bf16[128,128]{1,0:T(8,128)(2,1)}, u32[]{:S(2)}) copy-start(bf16[128,128]{1,0:T(8,128)(2,1)} %copy-done.77) | copy-start | bytes 98308
  193.2 36.9 %copy-start.81 = (bf16[128,128]{1,0:T(8,128)(2,1)S(1)}, bf16[128,128]{1,0:T(8,128)(2,1)}, u32[]{:S(2)}) copy-start(bf16[128,128]{1,0:T(8,128)(2,1)} %copy-done.80) | copy-start | bytes 98308
  193.2 28.9 %copy-start.30 = (bf16[128,2048]{1,0:T(8,128)(2,1)S(1)}, bf16[128,2048]{1,0:T(8,128)(2,1)}, u32[]{:S(2)}) copy-start(bf16[128,2048]{1,0:T(8,128)(2,1)} %copy-done.29) | copy-start | bytes 1572868
  193.2 51.5 %copy-start.43 = (bf16[128,1280]{1,0:T(8,128)(2,1)S(1)}, bf16[128,1280]{1,0:T(8,128)(2,1)}, u32[]{:S(2)}) copy-start(bf16[128,1280]{1,0:T(8,128)(2,1)} %copy-done.42) | copy-start | bytes 983044
  193.2 36.9 %all-to-all-start.5 = ((bf16[64,32,128]{2,1,0:T(8,128)(2,1)}), bf16[64,32,128]{2,1,0:T(8,128)(2,1)S(1)}, u32[]{:S(2)}, u32[]{:S(2)}) async-start(bf16[64,32,128]{2,1,0:T(8,128)(2,1)} %copy-done.24), calls=%async_computation.5 | async-start | bytes 1048576 | tf_op jit(solution)/shard_map/all_to_all | solution.py:511
  199.3 8.1 %collective-permute-start.19 = (bf16[128,1280]{1,0:T(8,128)(2,1)}, bf16[128,1280]{1,0:T(8,128)(2,1)S(1)}, u32[]{:S(2)}, u32[]{:S(2)}) collective-permute-start(bf16[128,1280]{1,0:T(8,128)(2,1)} %copy-done.95), channel_id=1, source_target_pairs={{0,128},{128,0},{1,129},{129,1},{2,130},{130,2},{3,131},{131,3},{4... | collective-permute-start | bytes 983048 | tf_op jit(solution)/shard_map/ppermute | solution.py:505
  199.4 16.1 %collective-permute-start.20 = (bf16[128,1280]{1,0:T(8,128)(2,1)}, bf16[128,1280]{1,0:T(8,128)(2,1)S(1)}, u32[]{:S(2)}, u32[]{:S(2)}) collective-permute-start(bf16[128,1280]{1,0:T(8,128)(2,1)} %copy-done.94), channel_id=1, source_target_pairs={{0,1},{1,0},{2,3},{3,2},{4,5},{5,4},{6,7},{7,6},{8,9},{9,8},{10,11... | collective-permute-start | bytes 983048 | tf_op jit(solution)/shard_map/ppermute | solution.py:508
  200.8 20.6 %collective-permute-start.21 = (bf16[128,1280]{1,0:T(8,128)(2,1)}, bf16[128,1280]{1,0:T(8,128)(2,1)S(1)}, u32[]{:S(2)}, u32[]{:S(2)}) collective-permute-start(bf16[128,1280]{1,0:T(8,128)(2,1)} %copy-done.93), channel_id=1, source_target_pairs={{0,129},{1,128},{2,131},{3,130},{4,133},{5,132},{6,135},{7,134},{8... | collective-permute-start | bytes 983048 | tf_op jit(solution)/shard_map/ppermute | solution.py:508
  206.8 17.9 %collective-permute-start.14 = (bf16[128,128]{1,0:T(8,128)(2,1)S(1)}, bf16[128,128]{1,0:T(8,128)(2,1)S(1)}, u32[]{:S(2)}, u32[]{:S(2)}) collective-permute-start(bf16[128,128]{1,0:T(8,128)(2,1)S(1)} %get-tuple-element.87), channel_id=1, source_target_pairs={{0,128},{128,0},{1,129},{129,1},{2,130},{130,2},{3,131},{131,3},{4... | collective-permute-start | bytes 98312 | tf_op jit(solution)/shard_map/ppermute | solution.py:505
  208.2 23.7 %collective-permute-start.27 = (bf16[128,2048]{1,0:T(8,128)(2,1)}, bf16[128,2048]{1,0:T(8,128)(2,1)S(1)}, u32[]{:S(2)}, u32[]{:S(2)}) collective-permute-start(bf16[128,2048]{1,0:T(8,128)(2,1)} %copy-done.89), channel_id=1, source_target_pairs={{0,129},{1,128},{2,131},{3,130},{4,133},{5,132},{6,135},{7,134},{8... | collective-permute-start | bytes 1572872 | tf_op jit(solution)/shard_map/ppermute | solution.py:508
  216.2 19.8 %collective-permute-start.26 = (bf16[128,2048]{1,0:T(8,128)(2,1)}, bf16[128,2048]{1,0:T(8,128)(2,1)S(1)}, u32[]{:S(2)}, u32[]{:S(2)}) collective-permute-start(bf16[128,2048]{1,0:T(8,128)(2,1)} %copy-done.89), channel_id=1, source_target_pairs={{128,129},{129,128},{130,131},{131,130},{132,133},{133,132},{134,1... | collective-permute-start | bytes 1572872 | tf_op jit(solution)/shard_map/ppermute | solution.py:508
  222.1 16.7 %collective-permute-start.22 = (bf16[128,2048]{1,0:T(8,128)(2,1)S(1)}, bf16[128,2048]{1,0:T(8,128)(2,1)}, u32[]{:S(2)}, u32[]{:S(2)}) collective-permute-start(bf16[128,2048]{1,0:T(8,128)(2,1)S(1)} %copy-done.30), channel_id=1, source_target_pairs={{128,0},{129,1},{130,2},{131,3},{132,4},{133,5},{134,6},{135,7},{1... | collective-permute-start | bytes 1572872 | tf_op jit(solution)/shard_map/ppermute | solution.py:505
  223.4 20.5 %collective-permute-start.24 = (bf16[128,2048]{1,0:T(8,128)(2,1)}, bf16[128,2048]{1,0:T(8,128)(2,1)}, u32[]{:S(2)}, u32[]{:S(2)}) collective-permute-start(bf16[128,2048]{1,0:T(8,128)(2,1)} %copy-done.90), channel_id=1, source_target_pairs={{128,1},{129,0},{130,3},{131,2},{132,5},{133,4},{134,7},{135,6},{1... | collective-permute-start | bytes 1572872 | tf_op jit(solution)/shard_map/ppermute | solution.py:508
  224.7 20.0 %collective-permute-start.23 = (bf16[128,2048]{1,0:T(8,128)(2,1)}, bf16[128,2048]{1,0:T(8,128)(2,1)}, u32[]{:S(2)}, u32[]{:S(2)}) collective-permute-start(bf16[128,2048]{1,0:T(8,128)(2,1)} %copy-done.90), channel_id=1, source_target_pairs={{0,1},{1,0},{2,3},{3,2},{4,5},{5,4},{6,7},{7,6},{8,9},{9,8},{10,11... | collective-permute-start | bytes 1572872 | tf_op jit(solution)/shard_map/ppermute | solution.py:508
  232.7 24.1 %collective-permute-start.18 = (f32[16,128]{1,0:T(8,128)S(1)}, f32[16,128]{1,0:T(8,128)S(1)}, u32[]{:S(2)}, u32[]{:S(2)}) collective-permute-start(f32[16,128]{1,0:T(8,128)S(1)} %get-tuple-element.96.refs_4_), channel_id=1, source_target_pairs={{0,129},{1,128},{2,131},{3,130},{4,133},{5,132},{6,135},{7,134},{8... | collective-permute-start | bytes 24584 | tf_op jit(solution)/shard_map/ppermute | solution.py:508
  236.8 20.0 %collective-permute-start.17 = (f32[16,128]{1,0:T(8,128)S(1)}, f32[16,128]{1,0:T(8,128)S(1)}, u32[]{:S(2)}, u32[]{:S(2)}) collective-permute-start(f32[16,128]{1,0:T(8,128)S(1)} %get-tuple-element.96.refs_4_), channel_id=1, source_target_pairs={{0,1},{1,0},{2,3},{3,2},{4,5},{5,4},{6,7},{7,6},{8,9},{9,8},{10,11... | collective-permute-start | bytes 24584 | tf_op jit(solution)/shard_map/ppermute | solution.py:508
  238.8 18.0 %collective-permute-start.16 = (f32[16,128]{1,0:T(8,128)S(1)}, f32[16,128]{1,0:T(8,128)S(1)}, u32[]{:S(2)}, u32[]{:S(2)}) collective-permute-start(f32[16,128]{1,0:T(8,128)S(1)} %get-tuple-element.96.refs_4_), channel_id=1, source_target_pairs={{0,128},{128,0},{1,129},{129,1},{2,130},{130,2},{3,131},{131,3},{4... | collective-permute-start | bytes 24584 | tf_op jit(solution)/shard_map/ppermute | solution.py:505
  243.9 12.9 %collective-permute-start.15 = (bf16[128,128]{1,0:T(8,128)(2,1)S(1)}, bf16[128,128]{1,0:T(8,128)(2,1)S(1)}, u32[]{:S(2)}, u32[]{:S(2)}) collective-permute-start(bf16[128,128]{1,0:T(8,128)(2,1)S(1)} %get-tuple-element.95), channel_id=1, source_target_pairs={{0,128},{128,0},{1,129},{129,1},{2,130},{130,2},{3,131},{131,3},{4... | collective-permute-start | bytes 98312 | tf_op jit(solution)/shard_map/ppermute | solution.py:505
  (85 other events, 150.1 us)
where the time goes:
time: 263 us; the launch traced here: 258 us
  starting transfers between devices  77.5 us (29%)
  local copies, waits for them, and re-layouts  66.7 us (25%)
  waiting for transfers between devices  62.7 us (24%)
  Pallas kernels  31.3 us (12%)
  blocking collectives  17.7 us (7%)
    unnamed x200, local copies, waits for them, and re-layouts  66.7 us
    all_to_all x5, starting transfers between devices, exchange(): lax.all_to_all(block, 'expert', split_axis=0, concat_axis=0, tiled=True)  47.2 us
    ppermute x12, waiting for transfers between devices, away(): return lax.ppermute(block, every, pairs(layer, cross))  29.4 us
    all_to_all x5, waiting for transfers between devices, exchange(): lax.all_to_all(block, 'expert', split_axis=0, concat_axis=0, tiled=True)  24.7 us
    ppermute x12, starting transfers between devices, away(): return lax.ppermute(block, every, pairs(layer, cross))  24.5 us
    all_to_all x1, blocking collectives, exchange(): lax.all_to_all(block, 'expert', split_axis=0, concat_axis=0, tiled=True)  17.7 us
    ppermute x16, waiting for transfers between devices, beside(): return lax.ppermute(block, 'section', route)  8.63 us
    ppermute x16, starting transfers between devices, beside(): return lax.ppermute(block, 'section', route)  5.79 us
  transfers between devices with their start and end apart: 33, of which 15 were waited for; matrix products, arithmetic and copies ran while one was open for 0% of the time, Pallas kernels for 8%

commit v1 on v0

--- a/solution.py
+++ b/solution.py
@@ -1,3 +1,4 @@
+import functools
 import jax
 import jax.numpy as jnp
 from jax import lax
@@ -26,7 +27,7 @@
     return lax.dot_general(left, right, (((0,), (0,)), ((), ())), preferred_element_type=f32)
 
 
-def call(body, in_specs, outs, scratch=(), flops=0, moved=0, grant=16, out_spec=vmem):
+def call(body, in_specs, outs, scratch=(), flops=0, moved=0, grant=None, out_spec=vmem):
     return pl.pallas_call(
         body,
         in_specs=in_specs,
@@ -34,7 +35,7 @@
         out_specs=[out_spec] * len(outs),
         scratch_shapes=list(scratch),
         cost_estimate=pl.CostEstimate(flops=flops, bytes_accessed=moved, transcendentals=0),
-        compiler_params=pltpu.CompilerParams(vmem_limit_bytes=grant * 2**20),
+        compiler_params=pltpu.CompilerParams(vmem_limit_bytes=grant and grant * 2**20),
     )
 
 
@@ -142,47 +143,33 @@
         target[...] = source[...].astype(f32).T.astype(bf16)
 
 
-def pack_body(*refs):
+def pack_body(layer, *refs):
     place_ref = refs[0]
     own, swapped = refs[1:4], refs[4:7]
-    outs = refs[7:11]
-    sems = refs[11]
+    both, last, sems = refs[7:10]
     section = place_ref[0]
     start = pl.multiple_of(section * 256, 256)
     start_down = pl.multiple_of(section * 384, 128)
 
-    def copies(sources):
-        found = []
-        for layer, (gate, up, down) in enumerate(sources):
-            both, last = outs[2 * layer], outs[2 * layer + 1]
-            found.append(
-                pltpu.make_async_copy(
-                    gate.at[pl.ds(start, 256), :], both.at[0:256, :], sems.at[layer, 0]
-                )
-            )
-            found.append(
-                pltpu.make_async_copy(
-                    up.at[pl.ds(start, 256), :], both.at[256:512, :], sems.at[layer, 1]
-                )
-            )
-            found.append(
-                pltpu.make_async_copy(
-                    down.at[pl.ds(start_down, 384), :], last, sems.at[layer, 2]
-                )
-            )
-        return found
-
-    @pl.when(section == 0)
+    def copies(group):
+        gate, up, down = group
+        return [
+            pltpu.make_async_copy(gate.at[pl.ds(start, 256), :], both.at[0:256, :], sems.at[0]),
+            pltpu.make_async_copy(up.at[pl.ds(start, 256), :], both.at[256:512, :], sems.at[1]),
+            pltpu.make_async_copy(down.at[pl.ds(start_down, 384), :], last, sems.at[2]),
+        ]
+
+    @pl.when(section == layer)
     def _():
-        for copy in copies((own, swapped)):
+        for copy in copies(own):
             copy.start()
 
-    @pl.when(section != 0)
+    @pl.when(section != layer)
     def _():
-        for copy in copies((swapped, own)):
+        for copy in copies(swapped):
             copy.start()
 
-    for copy in copies((own, swapped)):
+    for copy in copies(own):
         copy.wait()
 
 
@@ -558,15 +545,17 @@
     first_gain = jnp.where(section == 0, own_gain, got_gain)
     second_gain = jnp.where(section == 0, got_gain, own_gain)
 
-    packed = call(
-        pack_body,
-        [smem] + [anywhere] * 6,
-        [((512, 768), bf16), ((384, 512), bf16)] * 2,
-        [pltpu.SemaphoreType.DMA((2, 3))],
-        flops=1,
-        moved=5 * 10**6,
-    )(place, *own, *swapped)
-    portions0 = [away(w) for w in packed[:2]]
+    def packed(layer):
+        return call(
+            functools.partial(pack_body, layer),
+            [smem] + [anywhere] * 6,
+            [((512, 768), bf16), ((384, 512), bf16)],
+            [pltpu.SemaphoreType.DMA((3,))],
+            flops=1,
+            moved=25 * 10**5,
+        )(place, *own, *swapped)
+
+    portions0 = [away(w) for w in packed(0)]
     portions0 += [beside(w) for w in portions0]
     arrived_first = exchange(out_first)
 
@@ -583,7 +572,7 @@
     )(place, arrived_first, *own, *swapped, *portions0)
     returned = exchange(result)
 
-    portions1 = [away(after(w, other)) for w, other in zip(packed[2:], portions0)]
+    portions1 = [away(after(w, other)) for w, other in zip(packed(1), portions0)]
     portions1 += [beside(w) for w in portions1]
 
     hidden_first, out_second = call(
@@ -599,7 +588,6 @@
         + [wide, matrix, matrix, pltpu.VMEM((128, 1280), bf16), pltpu.VMEM((128, 1280), bf16), sems],
         flops=12 * 10**8,
         moved=8 * 10**6,
-        grant=20,
     )(place, arrived_second, arrived_first, early0, early0_far, *own, *swapped, *portions1)
     returned = exchange(picked)
 
@@ -646,7 +634,7 @@
     )(place, arrived_third, hidden_first, high1_t, low1_t)
     both = ((micro_count, tokens, width), bf16)
     hidden = call(
-        hidden_body, [smem] + [vmem] * 3, [both], [narrow], flops=10**5, moved=10**5
+        hidden_body, [smem] + [vmem] * 3, [both], [narrow], flops=10**5, moved=10**5, grant=16
     )(place, hidden_first, hidden_second, beside(hidden_sent))[0]
 
     weight_grads = call(
@@ -664,7 +652,6 @@
         ],
         flops=12 * 10**8,
         moved=8 * 10**6,
-        grant=24,
         out_spec=anywhere,
     )(place, *early_parts, *late0_parts, *late1_parts)
 
@@ -672,7 +659,13 @@
         last_body, [smem] + [vmem] * 5, [block, block, ((16, 128), f32)], flops=10**8, moved=10**6
     )(place, returned, x_first, grad_middle, first_gain, pick0_t)
     grads, gain_grad = call(
-        final_body, [smem] + [vmem] * 8, [both, ((8, 128), f32)], [narrow], flops=10**5, moved=10**5
+        final_body,
+        [smem] + [vmem] * 8,
+        [both, ((8, 128), f32)],
+        [narrow],
+        flops=10**5,
+        moved=10**5,
+        grant=16,
     )(
         place,
         grad_first,

time: 263 us -> 222 us (0.84)
  local copies, waits for them, and re-layouts: 66.7 us -> 7.62 us
  Pallas kernels: 31.3 us -> 49.3 us
  waiting for transfers between devices: 62.7 us -> 73.8 us
  starting transfers between devices: 77.5 us -> 67.4 us
    unnamed x200 -> x80, local copies, waits for them, and re-layouts: 66.7 us -> 7.62 us
    all_to_all x5, waiting for transfers between devices: 24.7 us -> 33.8 us  [exchange(): lax.all_to_all(block, 'expert', split_axis=0, concat_axis=0, tiled=True)]
    all_to_all x5, starting transfers between devices: 47.2 us -> 40.2 us  [exchange(): lax.all_to_all(block, 'expert', split_axis=0, concat_axis=0, tiled=True)]
    pallas_call x1 -> x2, Pallas kernels: 2.62 us -> 5.95 us  [packed(): call(functools.partial(pack_body, layer), [smem] + [anywhere] * 6, [((512...]
    ppermute x12, waiting for transfers between devices: 29.4 us -> 32.1 us  [away(): return lax.ppermute(block, every, pairs(layer, cross))]
  transfers between devices with their start and end apart: 33 -> 33, of which waited for: 15 -> 16; matrix products, arithmetic and copies ran while one was open for 0% -> 1% of each run, Pallas kernels for 8% -> 16%
where the time goes in v1:
time: 222 us; the launch traced here: 219 us
  waiting for transfers between devices  73.8 us (33%)
  starting transfers between devices  67.4 us (30%)
  Pallas kernels  49.3 us (22%)
  blocking collectives  18 us (8%)
  local copies, waits for them, and re-layouts  7.62 us (3%)
    all_to_all x5, starting transfers between devices, exchange(): lax.all_to_all(block, 'expert', split_axis=0, concat_axis=0, tiled=True)  40.2 us
    all_to_all x5, waiting for transfers between devices, exchange(): lax.all_to_all(block, 'expert', split_axis=0, concat_axis=0, tiled=True)  33.8 us
    ppermute x12, waiting for transfers between devices, away(): return lax.ppermute(block, every, pairs(layer, cross))  32.1 us
    ppermute x12, starting transfers between devices, away(): return lax.ppermute(block, every, pairs(layer, cross))  22.8 us
    all_to_all x1, blocking collectives, exchange(): lax.all_to_all(block, 'expert', split_axis=0, concat_axis=0, tiled=True)  18 us
    pallas_call x1, Pallas kernels, window(): call(second_body, [smem] + [vmem] * 4 + [anywhere] * 10, [small, small] +...  7.96 us
    ppermute x16, waiting for transfers between devices, beside(): return lax.ppermute(block, 'section', route)  7.9 us
    unnamed x80, local copies, waits for them, and re-layouts  7.62 us
  transfers between devices with their start and end apart: 33, of which 16 were waited for; matrix products, arithmetic and copies ran while one was open for 1% of the time, Pallas kernels for 16%

profile of v1, /device:TPU:4, one launch (start us, length us, event | category | flops | bytes accessed | tf_op | source)
XLA Modules:
  0.0 218.5 jit_solution(10344430651303276768)
XLA Ops:
  2.0 1.2 collective-permute-done.3.refs_4_.refs_5_.refs_8_.refs_9_
  3.2 1.1 collective-permute-done.4.refs_5_.refs_6_.refs_9_.refs_10_
  4.3 1.1 collective-permute-done.5.refs_6_.refs_7_.refs_10_.refs_11_
  5.5 0.9 copy-done.11
  6.3 3.0 %shard_map.128 = (bf16[512,768]{1,0:T(8,128)(2,1)}, bf16[384,512]{1,0:T(8,128)(2,1)}) custom-call(s32[2]{0:T(128)} %pad_add_fusion.refs_0_.place_ref, bf16[512,768]{1,0:T(8,128)(2,1)} %bitcast.23, bf16[512,768]{1,0:T(8,128)(2,1)} %bitcast.29, bf16[768,512]{1,0:T(8,128)(2,1)} %bitcast.35, bf16[512,768]{1,0:T(8,128)(2,1)} %copy-done.9, ...), custom_call_target="tpu_custom_call" | custom-call | flops 1 | bytes 2500000 | tf_op jit(solution)/shard_map/pallas_call | solution.py:549
  9.4 2.3 %collective-permute-start.6 = (bf16[512,768]{1,0:T(8,128)(2,1)}, bf16[512,768]{1,0:T(8,128)(2,1)S(1)}, u32[]{:S(2)}, u32[]{:S(2)}) collective-permute-start(bf16[512,768]{1,0:T(8,128)(2,1)} %get-tuple-element.59), channel_id=1, source_target_pairs={{0,1},{1,0},{2,3},{3,2},{4,5},{5,4},{6,7},{7,6},{8,9},{9,8},{10,11... | collective-permute-start | bytes 2359304 | tf_op jit(solution)/shard_map/ppermute | solution.py:495
  14.5 2.7 %shard_map.127 = (bf16[64,32,128]{2,1,0:T(8,128)(2,1)}, bf16[128,128]{1,0:T(8,128)(2,1)}, bf16[128,128]{1,0:T(8,128)(2,1)}, bf16[1024,128]{1,0:T(8,128)(2,1)}, b...) custom-call(s32[2]{0:T(128)} %pad_add_fusion.refs_0_.place_ref, ...), custom_call_target="tpu_custom_call" | custom-call | flops 100000000 | bytes 2000000 | tf_op jit(solution)/shard_map/pallas_call | solution.py:526
  17.2 11.9 %all-to-all-start = ((bf16[64,32,128]{2,1,0:T(8,128)(2,1)}), bf16[64,32,128]{2,1,0:T(8,128)(2,1)S(1)}, u32[]{:S(2)}, u32[]{:S(2)}) async-start(bf16[64,32,128]{2,1,0:T(8,128)(2,1)} %get-tuple-element.58), calls=%async_computation | async-start | bytes 1048576 | tf_op jit(solution)/shard_map/all_to_all | solution.py:498
  29.2 1.6 collective-permute-start.7
  30.8 2.9 %shard_map.132 = (bf16[512,768]{1,0:T(8,128)(2,1)}, bf16[384,512]{1,0:T(8,128)(2,1)}) custom-call(s32[2]{0:T(128)} %pad_add_fusion.refs_0_.place_ref, bf16[512,768]{1,0:T(8,128)(2,1)} %bitcast.24, bf16[512,768]{1,0:T(8,128)(2,1)} %bitcast.30, bf16[768,512]{1,0:T(8,128)(2,1)} %bitcast.36, bf16[512,768]{1,0:T(8,128)(2,1)} %copy-done.9, ...), custom_call_target="tpu_custom_call" | custom-call | flops 1 | bytes 2500000 | tf_op jit(solution)/shard_map/pallas_call | solution.py:549
  33.8 2.3 %collective-permute-start.10 = (bf16[512,768]{1,0:T(8,128)(2,1)}, bf16[512,768]{1,0:T(8,128)(2,1)}, u32[]{:S(2)}, u32[]{:S(2)}) collective-permute-start(bf16[512,768]{1,0:T(8,128)(2,1)} %get-tuple-element.76), channel_id=1, source_target_pairs={{0,1},{1,0},{2,3},{3,2},{4,5},{5,4},{6,7},{7,6},{8,9},{9,8},{10,11... | collective-permute-start | bytes 2359304 | tf_op jit(solution)/shard_map/ppermute | solution.py:495
  36.0 11.3 %collective-permute-done.7.refs_9_.refs_13_ = bf16[384,512]{1,0:T(8,128)(2,1)S(1)} collective-permute-done((bf16[384,512]{1,0:T(8,128)(2,1)}, bf16[384,512]{1,0:T(8,128)(2,1)S(1)}, u32[]{:S(2)}, u32[]{:S(2)}) %collective-permute-start.7) | collective-permute-done | bytes 393248 | tf_op jit(solution)/shard_map/ppermute | solution.py:495
  47.4 1.6 collective-permute-done.9.refs_11_.refs_15_
  49.8 0.9 copy-done.15
  50.7 5.1 %shard_map.129 = (bf16[64,16,128]{2,1,0:T(8,128)(2,1)}, bf16[128,1280]{1,0:T(8,128)(2,1)}, bf16[128,1280]{1,0:T(8,128)(2,1)}, f32[128,768]{1,0:T(8,128)}, f32[128,768]{1,0:T(8,128)}) custom-call(s32[2]{0:T(128)} %pad_add_fusion.refs_0_.place_ref, bf16[64,32,128]{2,1,0:T(8,128)(2,1)} %copy-done.12, bf16[512,768]{1,0:T(8,128)(2,1)} %bitcast.25, ...), custom_call_target="tpu_custom_call" | custom-call | flops 600000000 | bytes 6000000 | tf_op jit(solution)/shard_map/pallas_call | solution.py:565
  55.8 10.7 %all-to-all-start.1 = ((bf16[64,16,128]{2,1,0:T(8,128)(2,1)}), bf16[64,16,128]{2,1,0:T(8,128)(2,1)S(1)}, u32[]{:S(2)}, u32[]{:S(2)}) async-start(bf16[64,16,128]{2,1,0:T(8,128)(2,1)} %get-tuple-element.61), calls=%async_computation.1 | async-start | bytes 524288 | tf_op jit(solution)/shard_map/all_to_all | solution.py:498
  66.5 1.0 collective-permute-start.11
  67.5 2.7 %shard_map.130 = (bf16[128,1024]{1,0:T(8,128)(2,1)}, bf16[128,1024]{1,0:T(8,128)(2,1)}, bf16[128,1024]{1,0:T(8,128)(2,1)}, bf16[128,1024]{1,0:T(8,128)(2,1)}, bf...) custom-call(bf16[1024,128]{1,0:T(8,128)(2,1)} %get-tuple-element.63.refs_0_, ...), custom_call_target="tpu_custom_call" | custom-call | flops 1000000 | bytes 3000000 | tf_op jit(solution)/shard_map/pallas_call | solution.py:562
  70.8 8.0 %all-to-all-done.1.returned = bf16[64,16,128]{2,1,0:T(8,128)(2,1)S(1)} async-done(((bf16[64,16,128]{2,1,0:T(8,128)(2,1)}), bf16[64,16,128]{2,1,0:T(8,128)(2,1)S(1)}, u32[]{:S(2)}, u32[]{:S(2)}) %all-to-all-start.1) | async-done | bytes 262176 | tf_op jit(solution)/shard_map/all_to_all | solution.py:498
  79.5 2.5 %shard_map.131 = (bf16[128,128]{1,0:T(8,128)(2,1)}, bf16[64,16,128]{2,1,0:T(8,128)(2,1)}) custom-call(bf16[64,16,128]{2,1,0:T(8,128)(2,1)} %copy-done.20, bf16[128,128]{1,0:T(8,128)(2,1)} %get-tuple-element.62.x_ref, f32[8,128]{1,0:T(8,128)} %get-tuple-element.111.gain_ref, bf16[128,1024]{1,0:T(8,128)(2,1)} %get-tuple-element.69.high_t, ...), custom_call_target="tpu_custom_call" | custom-call | flops 100000000 | bytes 2000000 | tf_op jit(solution)/shard_map/pallas_call | solution.py:578
  82.0 6.0 %all-to-all-start.2 = ((bf16[64,16,128]{2,1,0:T(8,128)(2,1)}), bf16[64,16,128]{2,1,0:T(8,128)(2,1)S(1)}, u32[]{:S(2)}, u32[]{:S(2)}) async-start(bf16[64,16,128]{2,1,0:T(8,128)(2,1)} %get-tuple-element.72), calls=%async_computation.2 | async-start | bytes 524288 | tf_op jit(solution)/shard_map/all_to_all | solution.py:498
  88.1 1.7 collective-permute-done.13.refs_14_
  89.9 10.0 %all-to-all-done.2.refs_1_ = bf16[64,16,128]{2,1,0:T(8,128)(2,1)S(1)} async-done(((bf16[64,16,128]{2,1,0:T(8,128)(2,1)}), bf16[64,16,128]{2,1,0:T(8,128)(2,1)S(1)}, u32[]{:S(2)}, u32[]{:S(2)}) %all-to-all-start.2) | async-done | bytes 262176 | tf_op jit(solution)/shard_map/all_to_all | solution.py:498
  100.5 8.0 %shard_map.133 = (bf16[64,16,128]{2,1,0:T(8,128)(2,1)}, bf16[64,16,128]{2,1,0:T(8,128)(2,1)}, bf16[128,1280]{1,0:T(8,128)(2,1)}, bf16[128,1280]{1,0:T(8,128)(2,1...) custom-call(s32[2]{0:T(128)} %pad_add_fusion.refs_0_.place_ref, ...), custom_call_target="tpu_custom_call" | custom-call | flops 1200000000 | bytes 8000000 | tf_op jit(solution)/shard_map/pallas_call | solution.py:583
  108.5 18.0 %all_to_all.30.returned = bf16[64,16,128]{2,1,0:T(8,128)(2,1)} all-to-all(bf16[64,16,128]{2,1,0:T(8,128)(2,1)} %get-tuple-element.79), channel_id=1, replica_groups=mesh['section'=2,'expert'=64,'dp'=2] {'expert'}, dimensions={0} | all-to-all | bytes 524288 | tf_op jit(solution)/shard_map/all_to_all | solution.py:498
  126.5 2.7 %shard_map.134 = (bf16[128,128]{1,0:T(8,128)(2,1)}, bf16[64,32,128]{2,1,0:T(8,128)(2,1)}) custom-call(bf16[64,16,128]{2,1,0:T(8,128)(2,1)} %all_to_all.30.returned, bf16[64,16,128]{2,1,0:T(8,128)(2,1)} %get-tuple-element.80.result, bf16[128,128]{1,0:T(8,128)(2,1)} %get-tuple-element.71.x_ref.first, bf16[128,128]{1,0:T(8,128)(2,1)} %get-tuple-element.81.grad_ref, ...), custom_call_target="tpu_custom_call" | custom-call | flops 100000000 | bytes 2000000 | tf_op jit(solution)/shard_map/pallas_call | solution.py:597
  129.2 5.5 %all-to-all-start.4 = ((bf16[64,32,128]{2,1,0:T(8,128)(2,1)}), bf16[64,32,128]{2,1,0:T(8,128)(2,1)S(1)}, u32[]{:S(2)}, u32[]{:S(2)}) async-start(bf16[64,32,128]{2,1,0:T(8,128)(2,1)} %get-tuple-element.83), calls=%async_computation.4 | async-start | bytes 1048576 | tf_op jit(solution)/shard_map/all_to_all | solution.py:498
  134.8 1.3 collective-permute-start.25
  136.1 15.7 %all-to-all-done.4.arrived.refs_1_ = bf16[64,32,128]{2,1,0:T(8,128)(2,1)S(1)} async-done(((bf16[64,32,128]{2,1,0:T(8,128)(2,1)}), bf16[64,32,128]{2,1,0:T(8,128)(2,1)S(1)}, u32[]{:S(2)}, u32[]{:S(2)}) %all-to-all-start.4) | async-done | bytes 524320 | tf_op jit(solution)/shard_map/all_to_all | solution.py:498
  151.8 0.8 copy-done.13
  152.6 7.4 %shard_map.137 = (bf16[64,32,128]{2,1,0:T(8,128)(2,1)}, bf16[128,2048]{1,0:T(8,128)(2,1)}, bf16[128,2048]{1,0:T(8,128)(2,1)}) custom-call(s32[2]{0:T(128)} %pad_add_fusion.refs_0_.place_ref, bf16[64,32,128]{2,1,0:T(8,128)(2,1)} %copy-done.13, bf16[64,32,128]{2,1,0:T(8,128)(2,1)} %copy-done.12, f32[128,768]{1,0:T(8,128)} %get-tuple-element.88.refs_3_, ...), custom_call_target="tpu_custom_call" | custom-call | flops 600000000 | bytes 8000000 | tf_op jit(solution)/shard_map/pallas_call | solution.py:611
  160.0 6.1 %all-to-all-start.5 = ((bf16[64,32,128]{2,1,0:T(8,128)(2,1)}), bf16[64,32,128]{2,1,0:T(8,128)(2,1)S(1)}, u32[]{:S(2)}, u32[]{:S(2)}) async-start(bf16[64,32,128]{2,1,0:T(8,128)(2,1)} %get-tuple-element.91), calls=%async_computation.5 | async-start | bytes 1048576 | tf_op jit(solution)/shard_map/all_to_all | solution.py:498
  166.2 1.1 collective-permute-start.20
  167.3 2.3 %collective-permute-start.21 = (bf16[128,1280]{1,0:T(8,128)(2,1)}, bf16[128,1280]{1,0:T(8,128)(2,1)}, u32[]{:S(2)}, u32[]{:S(2)}) collective-permute-start(bf16[128,1280]{1,0:T(8,128)(2,1)} %get-tuple-element.102), channel_id=1, source_target_pairs={{0,129},{1,128},{2,131},{3,130},{4,133},{5,132},{6,135},{7,134},{8... | collective-permute-start | bytes 983048 | tf_op jit(solution)/shard_map/ppermute | solution.py:495
  169.6 2.1 shard_map.135
  172.1 2.6 %collective-permute-start.27 = (bf16[128,2048]{1,0:T(8,128)(2,1)}, bf16[128,2048]{1,0:T(8,128)(2,1)S(1)}, u32[]{:S(2)}, u32[]{:S(2)}) collective-permute-start(bf16[128,2048]{1,0:T(8,128)(2,1)} %get-tuple-element.106), channel_id=1, source_target_pairs={{0,129},{1,128},{2,131},{3,130},{4,133},{5,132},{6,135},{7,134},{8... | collective-permute-start | bytes 1572872 | tf_op jit(solution)/shard_map/ppermute | solution.py:495
  174.7 7.3 %collective-permute-done.20.refs_3_ = bf16[128,1280]{1,0:T(8,128)(2,1)} collective-permute-done((bf16[128,1280]{1,0:T(8,128)(2,1)S(1)}, bf16[128,1280]{1,0:T(8,128)(2,1)}, u32[]{:S(2)}, u32[]{:S(2)}) %collective-permute-start.20) | collective-permute-done | bytes 327712 | tf_op jit(solution)/shard_map/ppermute | solution.py:495
  182.7 5.7 %collective-permute-done.21.refs_4_ = bf16[128,1280]{1,0:T(8,128)(2,1)} collective-permute-done((bf16[128,1280]{1,0:T(8,128)(2,1)}, bf16[128,1280]{1,0:T(8,128)(2,1)}, u32[]{:S(2)}, u32[]{:S(2)}) %collective-permute-start.21) | collective-permute-done | bytes 327712 | tf_op jit(solution)/shard_map/ppermute | solution.py:495
  188.3 1.3 collective-permute-start.22
  189.6 1.3 collective-permute-start.24
  191.0 3.7 %collective-permute-start.23 = (bf16[128,2048]{1,0:T(8,128)(2,1)}, bf16[128,2048]{1,0:T(8,128)(2,1)}, u32[]{:S(2)}, u32[]{:S(2)}) collective-permute-start(bf16[128,2048]{1,0:T(8,128)(2,1)} %get-tuple-element.104), channel_id=1, source_target_pairs={{0,1},{1,0},{2,3},{3,2},{4,5},{5,4},{6,7},{7,6},{8,9},{9,8},{10,11... | collective-permute-start | bytes 1572872 | tf_op jit(solution)/shard_map/ppermute | solution.py:495
  195.4 1.2 shard_map.136
  197.4 2.1 shard_map.138
  199.5 2.2 collective-permute-start.18
  201.7 1.8 collective-permute-start.17
  203.5 7.2 %collective-permute-done.24.refs_8_ = bf16[128,2048]{1,0:T(8,128)(2,1)S(1)} collective-permute-done((bf16[128,2048]{1,0:T(8,128)(2,1)}, bf16[128,2048]{1,0:T(8,128)(2,1)S(1)}, u32[]{:S(2)}, u32[]{:S(2)}) %collective-permute-start.24) | collective-permute-done | bytes 524320 | tf_op jit(solution)/shard_map/ppermute | solution.py:495
  211.5 5.7 %shard_map.140 = (f32[512,768]{1,0:T(8,128)}, f32[512,768]{1,0:T(8,128)}, f32[768,512]{1,0:T(8,128)}) custom-call(s32[2]{0:T(128)} %pad_add_fusion.refs_0_.place_ref, bf16[128,1280]{1,0:T(8,128)(2,1)} %get-tuple-element.99.refs_1_, bf16[128,1280]{1,0:T(8,128)(2,1)} %copy-done.30, bf16[128,1280]{1,0:T(8,128)(2,1)} %collective-permute-done.20.refs_3_, ...), custom_call_target="tpu_custom_call" | custom-call | flops 1200000000 | bytes 8000000 | tf_op jit(solution)/shard_map/pallas_call | solution.py:640
  217.3 1.2 shard_map.139
  (115 shorter events, 10.7 us)
Async XLA Ops:
  0.6 2.6 %collective-permute-start.3 = (bf16[512,768]{1,0:T(8,128)(2,1)}, bf16[512,768]{1,0:T(8,128)(2,1)S(1)}, u32[]{:S(2)}, u32[]{:S(2)}) collective-permute-start(bf16[512,768]{1,0:T(8,128)(2,1)} %bitcast.22), channel_id=1, source_target_pairs={{0,128},{128,0},{1,129},{129,1},{2,130},{130,2},{3,131},{131,3},{4... | collective-permute-start | bytes 2359304 | tf_op jit(solution)/shard_map/ppermute | solution.py:492
  0.7 3.6 %collective-permute-start.4 = (bf16[512,768]{1,0:T(8,128)(2,1)}, bf16[512,768]{1,0:T(8,128)(2,1)S(1)}, u32[]{:S(2)}, u32[]{:S(2)}) collective-permute-start(bf16[512,768]{1,0:T(8,128)(2,1)} %bitcast.28), channel_id=1, source_target_pairs={{0,128},{128,0},{1,129},{129,1},{2,130},{130,2},{3,131},{131,3},{4... | collective-permute-start | bytes 2359304 | tf_op jit(solution)/shard_map/ppermute | solution.py:492
  1.2 4.2 %collective-permute-start.5 = (bf16[768,512]{1,0:T(8,128)(2,1)}, bf16[768,512]{1,0:T(8,128)(2,1)S(1)}, u32[]{:S(2)}, u32[]{:S(2)}) collective-permute-start(bf16[768,512]{1,0:T(8,128)(2,1)} %bitcast.34), channel_id=1, source_target_pairs={{0,128},{128,0},{1,129},{129,1},{2,130},{130,2},{3,131},{131,3},{4... | collective-permute-start | bytes 2359304 | tf_op jit(solution)/shard_map/ppermute | solution.py:492
  2.0 10.2 %copy-start.37 = (f32[1,2,16,6]{2,1,3,0:T(2,128)S(1)}, f32[1,2,16,6]{2,1,3,0:T(2,128)}, u32[]{:S(2)}) copy-start(f32[1,2,16,6]{2,1,3,0:T(2,128)} %param.15) | copy-start | bytes 2308
  9.4 21.4 %collective-permute-start.6 = (bf16[512,768]{1,0:T(8,128)(2,1)}, bf16[512,768]{1,0:T(8,128)(2,1)S(1)}, u32[]{:S(2)}, u32[]{:S(2)}) collective-permute-start(bf16[512,768]{1,0:T(8,128)(2,1)} %get-tuple-element.59), channel_id=1, source_target_pairs={{0,1},{1,0},{2,3},{3,2},{4,5},{5,4},{6,7},{7,6},{8,9},{9,8},{10,11... | collective-permute-start | bytes 2359304 | tf_op jit(solution)/shard_map/ppermute | solution.py:495
  11.7 1.7 collective-permute-start.2
  11.7 1.3 collective-permute-start
  12.2 1.2 collective-permute-start.1
  17.2 30.2 %all-to-all-start = ((bf16[64,32,128]{2,1,0:T(8,128)(2,1)}), bf16[64,32,128]{2,1,0:T(8,128)(2,1)S(1)}, u32[]{:S(2)}, u32[]{:S(2)}) async-start(bf16[64,32,128]{2,1,0:T(8,128)(2,1)} %get-tuple-element.58), calls=%async_computation | async-start | bytes 1048576 | tf_op jit(solution)/shard_map/all_to_all | solution.py:498
  29.2 18.1 %collective-permute-start.7 = (bf16[384,512]{1,0:T(8,128)(2,1)}, bf16[384,512]{1,0:T(8,128)(2,1)S(1)}, u32[]{:S(2)}, u32[]{:S(2)}) collective-permute-start(bf16[384,512]{1,0:T(8,128)(2,1)} %get-tuple-element.60), channel_id=1, source_target_pairs={{0,1},{1,0},{2,3},{3,2},{4,5},{5,4},{6,7},{7,6},{8,9},{9,8},{10,11... | collective-permute-start | bytes 1179656 | tf_op jit(solution)/shard_map/ppermute | solution.py:495
  30.8 18.3 %collective-permute-start.8 = (bf16[512,768]{1,0:T(8,128)(2,1)S(1)}, bf16[512,768]{1,0:T(8,128)(2,1)S(1)}, u32[]{:S(2)}, u32[]{:S(2)}) collective-permute-start(bf16[512,768]{1,0:T(8,128)(2,1)S(1)} %collective-permute-done.6.refs_8_.refs_12_), channel_id=1, source_target_pairs={{0,128},{128,0},{1,129},{129,1},{2,130},{130,2},{3,131},{131,3},{4... | collective-permute-start | bytes 2359304 | tf_op jit(solution)/shard_map/ppermute | solution.py:492
  33.8 32.7 %copy-start.33 = (bf16[384,512]{1,0:T(8,128)(2,1)S(1)}, bf16[384,512]{1,0:T(8,128)(2,1)}, u32[]{:S(2)}) copy-start(bf16[384,512]{1,0:T(8,128)(2,1)} %get-tuple-element.78) | copy-start | bytes 1179652
  33.8 33.7 %collective-permute-start.10 = (bf16[512,768]{1,0:T(8,128)(2,1)}, bf16[512,768]{1,0:T(8,128)(2,1)}, u32[]{:S(2)}, u32[]{:S(2)}) collective-permute-start(bf16[512,768]{1,0:T(8,128)(2,1)} %get-tuple-element.76), channel_id=1, source_target_pairs={{0,1},{1,0},{2,3},{3,2},{4,5},{5,4},{6,7},{7,6},{8,9},{9,8},{10,11... | collective-permute-start | bytes 2359304 | tf_op jit(solution)/shard_map/ppermute | solution.py:495
  47.3 1.7 collective-permute-start.9
  55.8 14.4 %copy-start.7 = (f32[1,1024]{1,0:T(1,128)S(1)}, f32[1,1024]{1,0:T(1,128)}, u32[]{:S(2)}) copy-start(f32[1,1024]{1,0:T(1,128)} %param.10) | copy-start | bytes 12292
  55.8 14.4 %copy-start.32 = (f32[8,128]{1,0:T(8,128)S(1)}, f32[8,128]{1,0:T(8,128)}, u32[]{:S(2)}) copy-start(f32[8,128]{1,0:T(8,128)} %copy-done.31) | copy-start | bytes 12292
  55.8 23.0 %all-to-all-start.1 = ((bf16[64,16,128]{2,1,0:T(8,128)(2,1)}), bf16[64,16,128]{2,1,0:T(8,128)(2,1)S(1)}, u32[]{:S(2)}, u32[]{:S(2)}) async-start(bf16[64,16,128]{2,1,0:T(8,128)(2,1)} %get-tuple-element.61), calls=%async_computation.1 | async-start | bytes 524288 | tf_op jit(solution)/shard_map/all_to_all | solution.py:498
  66.5 21.6 %collective-permute-start.11 = (bf16[384,512]{1,0:T(8,128)(2,1)S(1)}, bf16[384,512]{1,0:T(8,128)(2,1)S(1)}, u32[]{:S(2)}, u32[]{:S(2)}) collective-permute-start(bf16[384,512]{1,0:T(8,128)(2,1)S(1)} %copy-done.33), channel_id=1, source_target_pairs={{0,1},{1,0},{2,3},{3,2},{4,5},{5,4},{6,7},{7,6},{8,9},{9,8},{10,11... | collective-permute-start | bytes 1179656 | tf_op jit(solution)/shard_map/ppermute | solution.py:495
  67.5 22.3 %collective-permute-start.12 = (bf16[512,768]{1,0:T(8,128)(2,1)}, bf16[512,768]{1,0:T(8,128)(2,1)S(1)}, u32[]{:S(2)}, u32[]{:S(2)}) collective-permute-start(bf16[512,768]{1,0:T(8,128)(2,1)} %collective-permute-done.10.refs_11_), channel_id=1, source_target_pairs={{0,128},{128,0},{1,129},{129,1},{2,130},{130,2},{3,131},{131,3},{4... | collective-permute-start | bytes 2359304 | tf_op jit(solution)/shard_map/ppermute | solution.py:492
  82.0 17.8 %all-to-all-start.2 = ((bf16[64,16,128]{2,1,0:T(8,128)(2,1)}), bf16[64,16,128]{2,1,0:T(8,128)(2,1)S(1)}, u32[]{:S(2)}, u32[]{:S(2)}) async-start(bf16[64,16,128]{2,1,0:T(8,128)(2,1)} %get-tuple-element.72), calls=%async_computation.2 | async-start | bytes 524288 | tf_op jit(solution)/shard_map/all_to_all | solution.py:498
  88.0 11.8 %copy-start.28 = (bf16[384,512]{1,0:T(8,128)(2,1)}, bf16[384,512]{1,0:T(8,128)(2,1)S(1)}, u32[]{:S(2)}) copy-start(bf16[384,512]{1,0:T(8,128)(2,1)S(1)} %collective-permute-done.11.refs_12_) | copy-start | bytes 1179652
  88.0 1.8 collective-permute-start.13
  89.8 10.0 %copy-start.29 = (bf16[384,512]{1,0:T(8,128)(2,1)}, bf16[384,512]{1,0:T(8,128)(2,1)S(1)}, u32[]{:S(2)}) copy-start(bf16[384,512]{1,0:T(8,128)(2,1)S(1)} %collective-permute-done.13.refs_14_) | copy-start | bytes 1179652
  108.5 26.3 %copy-start.22 = (bf16[128,2048]{1,0:T(8,128)(2,1)S(1)}, bf16[128,2048]{1,0:T(8,128)(2,1)}, u32[]{:S(2)}) copy-start(bf16[128,2048]{1,0:T(8,128)(2,1)} %get-tuple-element.105.refs_9_) | copy-start | bytes 1572868
  129.2 22.6 %all-to-all-start.4 = ((bf16[64,32,128]{2,1,0:T(8,128)(2,1)}), bf16[64,32,128]{2,1,0:T(8,128)(2,1)S(1)}, u32[]{:S(2)}, u32[]{:S(2)}) async-start(bf16[64,32,128]{2,1,0:T(8,128)(2,1)} %get-tuple-element.83), calls=%async_computation.4 | async-start | bytes 1048576 | tf_op jit(solution)/shard_map/all_to_all | solution.py:498
  134.8 54.9 %collective-permute-start.25 = (bf16[128,2048]{1,0:T(8,128)(2,1)S(1)}, bf16[128,2048]{1,0:T(8,128)(2,1)S(1)}, u32[]{:S(2)}, u32[]{:S(2)}) collective-permute-start(bf16[128,2048]{1,0:T(8,128)(2,1)S(1)} %copy-done.22), channel_id=1, source_target_pairs={{0,128},{1,129},{2,130},{3,131},{4,132},{5,133},{6,134},{7,135},{8... | collective-permute-start | bytes 1572872 | tf_op jit(solution)/shard_map/ppermute | solution.py:492
  152.6 13.5 %copy-start.35 = (bf16[128,1280]{1,0:T(8,128)(2,1)S(1)}, bf16[128,1280]{1,0:T(8,128)(2,1)}, u32[]{:S(2)}) copy-start(bf16[128,1280]{1,0:T(8,128)(2,1)} %get-tuple-element.100) | copy-start | bytes 983044
  152.6 13.6 %copy-start.34 = (bf16[128,1280]{1,0:T(8,128)(2,1)S(1)}, bf16[128,1280]{1,0:T(8,128)(2,1)}, u32[]{:S(2)}) copy-start(bf16[128,1280]{1,0:T(8,128)(2,1)} %get-tuple-element.101) | copy-start | bytes 983044
  160.0 28.4 %copy-start.24 = (bf16[128,2048]{1,0:T(8,128)(2,1)S(1)}, bf16[128,2048]{1,0:T(8,128)(2,1)}, u32[]{:S(2)}) copy-start(bf16[128,2048]{1,0:T(8,128)(2,1)} %get-tuple-element.103.refs_5_) | copy-start | bytes 1572868
  160.0 34.7 %copy-start = (bf16[128,128]{1,0:T(8,128)(2,1)S(1)}, bf16[128,128]{1,0:T(8,128)(2,1)}, u32[]{:S(2)}) copy-start(bf16[128,128]{1,0:T(8,128)(2,1)} %get-tuple-element.71.x_ref.first) | copy-start | bytes 98308
  160.0 34.7 %copy-start.2 = (s32[2]{0:T(128)S(1)}, s32[2]{0:T(128)}, u32[]{:S(2)}) copy-start(s32[2]{0:T(128)} %pad_add_fusion.refs_0_.place_ref) | copy-start | bytes 28
  160.0 36.6 %all-to-all-start.5 = ((bf16[64,32,128]{2,1,0:T(8,128)(2,1)}), bf16[64,32,128]{2,1,0:T(8,128)(2,1)S(1)}, u32[]{:S(2)}, u32[]{:S(2)}) async-start(bf16[64,32,128]{2,1,0:T(8,128)(2,1)} %get-tuple-element.91), calls=%async_computation.5 | async-start | bytes 1048576 | tf_op jit(solution)/shard_map/all_to_all | solution.py:498
  166.1 6.0 %collective-permute-start.19 = (bf16[128,1280]{1,0:T(8,128)(2,1)S(1)}, bf16[128,1280]{1,0:T(8,128)(2,1)S(1)}, u32[]{:S(2)}, u32[]{:S(2)}) collective-permute-start(bf16[128,1280]{1,0:T(8,128)(2,1)S(1)} %copy-done.35), channel_id=1, source_target_pairs={{0,128},{128,0},{1,129},{129,1},{2,130},{130,2},{3,131},{131,3},{4... | collective-permute-start | bytes 983048 | tf_op jit(solution)/shard_map/ppermute | solution.py:492
  166.2 15.8 %collective-permute-start.20 = (bf16[128,1280]{1,0:T(8,128)(2,1)S(1)}, bf16[128,1280]{1,0:T(8,128)(2,1)}, u32[]{:S(2)}, u32[]{:S(2)}) collective-permute-start(bf16[128,1280]{1,0:T(8,128)(2,1)S(1)} %copy-done.34), channel_id=1, source_target_pairs={{0,1},{1,0},{2,3},{3,2},{4,5},{5,4},{6,7},{7,6},{8,9},{9,8},{10,11... | collective-permute-start | bytes 983048 | tf_op jit(solution)/shard_map/ppermute | solution.py:495
  167.3 21.1 %collective-permute-start.21 = (bf16[128,1280]{1,0:T(8,128)(2,1)}, bf16[128,1280]{1,0:T(8,128)(2,1)}, u32[]{:S(2)}, u32[]{:S(2)}) collective-permute-start(bf16[128,1280]{1,0:T(8,128)(2,1)} %get-tuple-element.102), channel_id=1, source_target_pairs={{0,129},{1,128},{2,131},{3,130},{4,133},{5,132},{6,135},{7,134},{8... | collective-permute-start | bytes 983048 | tf_op jit(solution)/shard_map/ppermute | solution.py:495
  171.7 19.3 %collective-permute-start.14 = (bf16[128,128]{1,0:T(8,128)(2,1)}, bf16[128,128]{1,0:T(8,128)(2,1)S(1)}, u32[]{:S(2)}, u32[]{:S(2)}) collective-permute-start(bf16[128,128]{1,0:T(8,128)(2,1)} %get-tuple-element.87), channel_id=1, source_target_pairs={{0,128},{128,0},{1,129},{129,1},{2,130},{130,2},{3,131},{131,3},{4... | collective-permute-start | bytes 98312 | tf_op jit(solution)/shard_map/ppermute | solution.py:492
  172.1 39.3 %copy-start.30 = (bf16[128,1280]{1,0:T(8,128)(2,1)}, bf16[128,1280]{1,0:T(8,128)(2,1)S(1)}, u32[]{:S(2)}) copy-start(bf16[128,1280]{1,0:T(8,128)(2,1)S(1)} %collective-permute-done.19.refs_2_) | copy-start | bytes 983044
  172.1 27.5 %collective-permute-start.27 = (bf16[128,2048]{1,0:T(8,128)(2,1)}, bf16[128,2048]{1,0:T(8,128)(2,1)S(1)}, u32[]{:S(2)}, u32[]{:S(2)}) collective-permute-start(bf16[128,2048]{1,0:T(8,128)(2,1)} %get-tuple-element.106), channel_id=1, source_target_pairs={{0,129},{1,128},{2,131},{3,130},{4,133},{5,132},{6,135},{7,134},{8... | collective-permute-start | bytes 1572872 | tf_op jit(solution)/shard_map/ppermute | solution.py:495
  182.0 19.7 %collective-permute-start.26 = (bf16[128,2048]{1,0:T(8,128)(2,1)}, bf16[128,2048]{1,0:T(8,128)(2,1)S(1)}, u32[]{:S(2)}, u32[]{:S(2)}) collective-permute-start(bf16[128,2048]{1,0:T(8,128)(2,1)} %get-tuple-element.106), channel_id=1, source_target_pairs={{128,129},{129,128},{130,131},{131,130},{132,133},{133,132},{134,1... | collective-permute-start | bytes 1572872 | tf_op jit(solution)/shard_map/ppermute | solution.py:495
  188.3 15.2 %collective-permute-start.22 = (bf16[128,2048]{1,0:T(8,128)(2,1)S(1)}, bf16[128,2048]{1,0:T(8,128)(2,1)}, u32[]{:S(2)}, u32[]{:S(2)}) collective-permute-start(bf16[128,2048]{1,0:T(8,128)(2,1)S(1)} %copy-done.24), channel_id=1, source_target_pairs={{128,0},{129,1},{130,2},{131,3},{132,4},{133,5},{134,6},{135,7},{1... | collective-permute-start | bytes 1572872 | tf_op jit(solution)/shard_map/ppermute | solution.py:492
  189.6 21.7 %copy-start.23 = (bf16[128,2048]{1,0:T(8,128)(2,1)}, bf16[128,2048]{1,0:T(8,128)(2,1)S(1)}, u32[]{:S(2)}) copy-start(bf16[128,2048]{1,0:T(8,128)(2,1)S(1)} %collective-permute-done.25.refs_10_) | copy-start | bytes 1572868
  189.6 21.1 %collective-permute-start.24 = (bf16[128,2048]{1,0:T(8,128)(2,1)}, bf16[128,2048]{1,0:T(8,128)(2,1)S(1)}, u32[]{:S(2)}, u32[]{:S(2)}) collective-permute-start(bf16[128,2048]{1,0:T(8,128)(2,1)} %get-tuple-element.104), channel_id=1, source_target_pairs={{128,1},{129,0},{130,3},{131,2},{132,5},{133,4},{134,7},{135,6},{1... | collective-permute-start | bytes 1572872 | tf_op jit(solution)/shard_map/ppermute | solution.py:495
  191.0 20.4 %collective-permute-start.23 = (bf16[128,2048]{1,0:T(8,128)(2,1)}, bf16[128,2048]{1,0:T(8,128)(2,1)}, u32[]{:S(2)}, u32[]{:S(2)}) collective-permute-start(bf16[128,2048]{1,0:T(8,128)(2,1)} %get-tuple-element.104), channel_id=1, source_target_pairs={{0,1},{1,0},{2,3},{3,2},{4,5},{5,4},{6,7},{7,6},{8,9},{9,8},{10,11... | collective-permute-start | bytes 1572872 | tf_op jit(solution)/shard_map/ppermute | solution.py:495
  199.5 11.8 %copy-start.25 = (bf16[128,2048]{1,0:T(8,128)(2,1)}, bf16[128,2048]{1,0:T(8,128)(2,1)S(1)}, u32[]{:S(2)}) copy-start(bf16[128,2048]{1,0:T(8,128)(2,1)S(1)} %collective-permute-done.27.refs_12_) | copy-start | bytes 1572868
  199.5 17.7 %collective-permute-start.18 = (f32[16,128]{1,0:T(8,128)}, f32[16,128]{1,0:T(8,128)S(1)}, u32[]{:S(2)}, u32[]{:S(2)}) collective-permute-start(f32[16,128]{1,0:T(8,128)} %get-tuple-element.96.refs_4_), channel_id=1, source_target_pairs={{0,129},{1,128},{2,131},{3,130},{4,133},{5,132},{6,135},{7,134},{8... | collective-permute-start | bytes 24584 | tf_op jit(solution)/shard_map/ppermute | solution.py:495
  201.7 15.5 %collective-permute-start.17 = (f32[16,128]{1,0:T(8,128)}, f32[16,128]{1,0:T(8,128)S(1)}, u32[]{:S(2)}, u32[]{:S(2)}) collective-permute-start(f32[16,128]{1,0:T(8,128)} %get-tuple-element.96.refs_4_), channel_id=1, source_target_pairs={{0,1},{1,0},{2,3},{3,2},{4,5},{5,4},{6,7},{7,6},{8,9},{9,8},{10,11... | collective-permute-start | bytes 24584 | tf_op jit(solution)/shard_map/ppermute | solution.py:495
  203.5 13.7 %collective-permute-start.16 = (f32[16,128]{1,0:T(8,128)}, f32[16,128]{1,0:T(8,128)S(1)}, u32[]{:S(2)}, u32[]{:S(2)}) collective-permute-start(f32[16,128]{1,0:T(8,128)} %get-tuple-element.96.refs_4_), channel_id=1, source_target_pairs={{0,128},{128,0},{1,129},{129,1},{2,130},{130,2},{3,131},{131,3},{4... | collective-permute-start | bytes 24584 | tf_op jit(solution)/shard_map/ppermute | solution.py:492
  210.7 6.5 %collective-permute-start.15 = (bf16[128,128]{1,0:T(8,128)(2,1)}, bf16[128,128]{1,0:T(8,128)(2,1)S(1)}, u32[]{:S(2)}, u32[]{:S(2)}) collective-permute-start(bf16[128,128]{1,0:T(8,128)(2,1)} %get-tuple-element.95), channel_id=1, source_target_pairs={{0,128},{128,0},{1,129},{129,1},{2,130},{130,2},{3,131},{131,3},{4... | collective-permute-start | bytes 98312 | tf_op jit(solution)/shard_map/ppermute | solution.py:492
  (25 other events, 80.7 us)

commit v2 on v1

--- a/solution.py
+++ b/solution.py
@@ -32,7 +32,7 @@
         body,
         in_specs=in_specs,
         out_shape=[jax.ShapeDtypeStruct(shape, dtype) for shape, dtype in outs],
-        out_specs=[out_spec] * len(outs),
+        out_specs=out_spec if isinstance(out_spec, list) else [out_spec] * len(outs),
         scratch_shapes=list(scratch),
         cost_estimate=pl.CostEstimate(flops=flops, bytes_accessed=moved, transcendentals=0),
         compiler_params=pltpu.CompilerParams(vmem_limit_bytes=grant and grant * 2**20),
@@ -143,21 +143,23 @@
         target[...] = source[...].astype(f32).T.astype(bf16)
 
 
-def pack_body(layer, *refs):
+def pack_body(layer, tensors, *refs):
     place_ref = refs[0]
-    own, swapped = refs[1:4], refs[4:7]
-    both, last, sems = refs[7:10]
+    own, swapped = refs[1 : 1 + len(tensors)], refs[1 + len(tensors) : 1 + 2 * len(tensors)]
+    outs, sems = refs[1 + 2 * len(tensors) : -1], refs[-1]
     section = place_ref[0]
     start = pl.multiple_of(section * 256, 256)
     start_down = pl.multiple_of(section * 384, 128)
 
     def copies(group):
-        gate, up, down = group
-        return [
-            pltpu.make_async_copy(gate.at[pl.ds(start, 256), :], both.at[0:256, :], sems.at[0]),
-            pltpu.make_async_copy(up.at[pl.ds(start, 256), :], both.at[256:512, :], sems.at[1]),
-            pltpu.make_async_copy(down.at[pl.ds(start_down, 384), :], last, sems.at[2]),
-        ]
+        found = []
+        for n, ref in zip(tensors, group):
+            if n < 2:
+                source, target = ref.at[pl.ds(start, 256), :], outs[0].at[256 * n : 256 * n + 256, :]
+            else:
+                source, target = ref.at[pl.ds(start_down, 384), :], outs[-1]
+            found.append(pltpu.make_async_copy(source, target, sems.at[n]))
+        return found
 
     @pl.when(section == layer)
     def _():
@@ -189,52 +191,69 @@
 
 def fetch(place_ref, layer, sources, targets, sems):
     own, swapped = sources[0:3], sources[3:6]
-    portions = (sources[6:8], sources[8:10])
     section, part = place_ref[0], place_ref[1]
     mine = pl.multiple_of(part * 512, 512)
     rest = pl.multiple_of((1 - part) * 512, 512)
-
-    def near(group):
+    downs = sources[-2:]
+
+    def near(group, others):
         found = []
         for n in range(3):
             if n < 2:
                 target = targets[n].at[pl.ds(mine, 512), :]
             else:
                 target = targets[n].at[:, pl.ds(mine, 512)]
-            found.append(pltpu.make_async_copy(group[n], target, sems.at[n, 0]))
+            found.append([pltpu.make_async_copy(group[n], target, sems.at[n, 0])])
+        for n, source in enumerate(others):
+            target = targets[n].at[pl.ds(rest, 512), :]
+            found[n].append(pltpu.make_async_copy(source, target, sems.at[n, 1]))
         return found
 
-    def far():
+    def far(n):
         found = []
-        for n in range(3):
-            for p, (both, down) in enumerate(portions):
-                index = section if p == 0 else 1 - section
-                if n < 2:
-                    start = pl.multiple_of(rest + index * 256, 256)
-                    source = both.at[256 * n : 256 * (n + 1), :]
-                    target = targets[n].at[pl.ds(start, 256), :]
-                else:
-                    start = pl.multiple_of(index * 384, 128)
-                    source = down
-                    target = targets[n].at[pl.ds(start, 384), pl.ds(rest, 512)]
-                found.append(pltpu.make_async_copy(source, target, sems.at[n, 1 + p]))
+        for p in range(2):
+            index = section if p == 0 else 1 - section
+            if n < 2:
+                start = pl.multiple_of(rest + index * 256, 256)
+                source = sources[6 + p].at[256 * n : 256 * (n + 1), :]
+                target = targets[n].at[pl.ds(start, 256), :]
+            else:
+                start = pl.multiple_of(index * 384, 128)
+                source = downs[p]
+                target = targets[n].at[pl.ds(start, 384), pl.ds(rest, 512)]
+            found.append(pltpu.make_async_copy(source, target, sems.at[n, 1 + p]))
         return found
 
-    @pl.when(section == layer)
+    if layer == 0:
+        gate_far, gate_passed, up_far, up_passed = sources[6:10]
+        lower, upper = (gate_far, up_passed), (gate_passed, up_far)
+        others = [[], [], far(2)]
+    else:
+        lower, upper = (), ()
+        others = [far(0), far(1), far(2)]
+
+    @pl.when(section == 0)
     def _():
-        for copy in near(own):
+        for copies in near(own if layer == 0 else swapped, lower):
+            for copy in copies:
+                copy.start()
+
+    @pl.when(section != 0)
+    def _():
+        for copies in near(swapped if layer == 0 else own, upper):
+            for copy in copies:
+                copy.start()
+
+    for copies in others:
+        for copy in copies:
             copy.start()
-
-    @pl.when(section != layer)
-    def _():
-        for copy in near(swapped):
-            copy.start()
-
-    others = far()
-    for copy in others:
-        copy.start()
-    waits = near(own)
-    return [[waits[n], others[2 * n], others[2 * n + 1]] for n in range(3)]
+    return [first + second for first, second in zip(near(own, lower), others)]
+
+
+def begin(source, target, sem):
+    copy = pltpu.make_async_copy(source, target, sem)
+    copy.start()
+    return copy
 
 
 def finish(group):
@@ -255,23 +274,30 @@
 
 def first_forward_body(*refs):
     place_ref, arrived = refs[0:2]
-    sources = refs[2:12]
-    result, early, early_far, gate_out, up_out = refs[12:17]
-    w_gate, w_up, w_down, wide, rows, sems = refs[17:]
+    sources = refs[2:14]
+    result = refs[14]
+    outs = refs[15:19]
+    w_gate, w_up, w_down, wide, rows = refs[19:24]
+    early, early_far, gate_out, up_out, sems, more = refs[24:]
     waits = fetch(place_ref, 0, sources, (w_gate, w_up, w_down), sems)
     to_matrix(arrived[:, :16, :].reshape(1024, 128).astype(f32), wide, rows)
     halves(place_ref, rows, early, early_far)
     finish(waits[0])
     pre_gate = dot(rows[...], w_gate[...])
     gate_out[...] = pre_gate
+    stores = [begin(gate_out, outs[2], more.at[2])]
     finish(waits[1])
     pre_up = dot(rows[...], w_up[...])
     up_out[...] = pre_up
+    stores.append(begin(up_out, outs[3], more.at[3]))
     acts = gated(pre_gate, pre_up).astype(bf16)
     early[:, 512:] = acts
     early_far[:, 512:] = acts
+    stores.append(begin(early, outs[0], more.at[0]))
+    stores.append(begin(early_far, outs[1], more.at[1]))
     finish(waits[2])
     result[...] = to_rows(dot(acts, w_down[...]), wide).reshape(64, 16, 128)
+    finish(stores)
 
 
 def expert_grads(act_grad, pre_gate, pre_up):
@@ -287,15 +313,23 @@
 
 
 def second_body(*refs):
-    place_ref, arrived, cot, early0, early0_far = refs[0:5]
+    place_ref, arrived, cot_ref, early0_ref, early0_far_ref = refs[0:5]
     sources = refs[5:15]
-    picked, result, kept, beside, straight, cross, late, late_far, gain_out = refs[15:24]
-    w_gate, w_up, w_down, wide, rows, grads, early, early_far, sems = refs[24:]
+    picked, result, gain_out = refs[15:18]
+    outs = refs[18:24]
+    w_gate, w_up, w_down, wide, rows, grads, early, early_far = refs[24:32]
+    cot, early0, early0_far, late, late_far, sems, more = refs[32:]
     waits = fetch(place_ref, 1, sources, (w_gate, w_up, w_down), sems)
+    loads = [
+        begin(cot_ref.at[:, 16:32, :], cot, more.at[0]),
+        begin(early0_ref, early0, more.at[1]),
+        begin(early0_far_ref, early0_far, more.at[2]),
+    ]
     normed_rows = arrived[...].reshape(1024, 128)
     to_matrix(normed_rows.astype(f32), wide, rows)
     halves(place_ref, rows, early, early_far)
-    to_matrix(cot[:, 16:, :].reshape(1024, 128).astype(f32), wide, grads)
+    finish(loads)
+    to_matrix(cot[...].reshape(1024, 128).astype(f32), wide, grads)
     halves(place_ref, grads, late, late_far)
     finish(waits[0])
     pre_gate = dot(rows[...], w_gate[...])
@@ -304,53 +338,72 @@
     acts = gated(pre_gate, pre_up).astype(bf16)
     early[:, 512:] = acts
     early_far[:, 512:] = acts
+
+    def moves(order):
+        return [
+            pltpu.make_async_copy(source, outs[n], more.at[3 + n])
+            for n, source in enumerate(order)
+        ]
+
+    @pl.when(place_ref[0] == 0)
+    def _():
+        for copy in moves((early0, early, early0_far, early_far)):
+            copy.start()
+
+    @pl.when(place_ref[0] != 0)
+    def _():
+        for copy in moves((early, early0, early_far, early0_far)):
+            copy.start()
+
+    stores = moves((early0, early, early0_far, early_far))
     finish(waits[2])
     act_grad = dot_nt(grads[...], w_down[...])
     gate_grad, up_grad = expert_grads(act_grad, pre_gate, pre_up)
     for target in (late, late_far):
         target[:, 512:1280] = gate_grad
         target[:, 1280:] = up_grad
+    stores.append(begin(late, outs[4], more.at[7]))
+    stores.append(begin(late_far, outs[5], more.at[8]))
     pick_rows = to_rows(dot_nt(gate_grad, w_gate[...]) + dot_nt(up_grad, w_up[...]), wide)
     picked[...] = pick_rows.reshape(64, 16, 128)
     gain_out[...] = gain_part(pick_rows, normed_rows)
     result[...] = to_rows(dot(acts, w_down[...]), wide).reshape(64, 16, 128)
-
-    @pl.when(place_ref[0] == 0)
-    def _():
-        kept[...] = early0[...]
-        beside[...] = early[...]
-        straight[...] = early0_far[...]
-        cross[...] = early_far[...]
-
-    @pl.when(place_ref[0] != 0)
-    def _():
-        kept[...] = early[...]
-        beside[...] = early0[...]
-        straight[...] = early_far[...]
-        cross[...] = early0_far[...]
+    finish(stores)
 
 
 def first_backward_body(*refs):
-    place_ref, arrived, normed, pre_gate, pre_up, gain_second = refs[0:6]
-    sources = refs[6:16]
-    picked, late, late_far = refs[16:19]
-    w_gate, w_up, w_down, wide, grads, sems = refs[19:]
+    place_ref, gain_second, arrived_ref, normed_ref, gate_ref, up_ref = refs[0:6]
+    sources = refs[6:18]
+    picked = refs[18]
+    outs = refs[19:21]
+    w_gate, w_up, w_down, wide, grads = refs[21:26]
+    arrived, normed, pre_gate, pre_up, late, late_far, sems, more = refs[26:]
+    load = begin(arrived_ref.at[:, 0:16, :], arrived, more.at[0])
     waits = fetch(place_ref, 0, sources, (w_gate, w_up, w_down), sems)
-    to_matrix(arrived[:, :16, :].reshape(1024, 128).astype(f32), wide, grads)
+    loads = [
+        begin(gate_ref, pre_gate, more.at[1]),
+        begin(up_ref, pre_up, more.at[2]),
+        begin(normed_ref.at[:, 0:16, :], normed, more.at[3]),
+    ]
+    load.wait()
+    to_matrix(arrived[...].reshape(1024, 128).astype(f32), wide, grads)
     halves(place_ref, grads, late, late_far)
     finish(waits[2])
     act_grad = dot_nt(grads[...], w_down[...])
+    finish(loads)
     gate_grad, up_grad = expert_grads(act_grad, pre_gate[...], pre_up[...])
     for target in (late, late_far):
         target[:, 512:1280] = gate_grad
         target[:, 1280:] = up_grad
+    stores = [begin(late, outs[0], more.at[4]), begin(late_far, outs[1], more.at[5])]
     finish(waits[0])
     finish(waits[1])
     pick_rows = to_rows(dot_nt(gate_grad, w_gate[...]) + dot_nt(up_grad, w_up[...]), wide)
     picked[:, :16, :] = pick_rows.reshape(64, 16, 128)
-    gain_first = gain_part(pick_rows, normed[:, :16, :].reshape(1024, 128))
+    gain_first = gain_part(pick_rows, normed[...].reshape(1024, 128))
     both = jnp.concatenate([gain_first, gain_second[...]], axis=0).astype(bf16)
     picked[:, 16:, :] = jnp.broadcast_to(both[None], (64, 16, 128))
+    finish(stores)
 
 
 def combined(high_t, low_t, rows):
@@ -406,18 +459,18 @@
     rows = returned[:, :16, :].reshape(1024, 128)
     grad = input_gradient(rows, grad_ref[...], x_ref[...], gain_ref[...], pick_t[...])
     grad_out[...] = grad
-    sent[...] = jnp.where(
-        place_ref[0] == 0, grad_ref[...].astype(f32), grad.astype(f32)
-    ).astype(bf16)
-    gain_out[...] = jnp.sum(returned[:, 16:, :].astype(f32), axis=0)
+    gain_rows = jnp.sum(returned[:, 16:, :].astype(f32), axis=0)
+    sent[:128, :] = jnp.where(place_ref[0] == 0, grad_ref[...].astype(f32), grad.astype(f32))
+    sent[128:, :] = gain_rows
+    gain_out[...] = gain_rows
 
 
 def final_body(*refs):
     place_ref, first, second, got = refs[0:4]
-    gain_rows, gain_beside, gain_straight, gain_cross, own_gain = refs[4:9]
-    out, gain_out, wide = refs[9:]
-    arrange(place_ref[0], first[...], second[...], got[...], wide, out)
-    total = (gain_rows[...] + gain_beside[...]) + (gain_straight[...] + gain_cross[...])
+    gain_rows, gain_straight, gain_cross, own_gain = refs[4:8]
+    out, gain_out, wide = refs[8:]
+    arrange(place_ref[0], first[...], second[...], got[:128, :], wide, out)
+    total = (gain_rows[...] + got[128:, :]) + (gain_straight[...] + gain_cross[...])
     gain_out[...] = jnp.where(place_ref[0] == 0, total[:8], total[8:]) / own_gain[...]
 
 
@@ -522,6 +575,10 @@
     narrow = pltpu.VMEM((128, 128), f32)
     matrix = pltpu.VMEM((128, 1024), bf16)
     sems = pltpu.SemaphoreType.DMA((3, 3))
+    early_room = pltpu.VMEM((128, 1280), bf16)
+    late_room = pltpu.VMEM((128, 2048), bf16)
+    plain_room = pltpu.VMEM((128, 768), f32)
+    arrival = pltpu.VMEM((64, 16, 128), bf16)
 
     out_first, x_first, grad_last, *maps = call(
         start_body,
@@ -545,49 +602,68 @@
     first_gain = jnp.where(section == 0, own_gain, got_gain)
     second_gain = jnp.where(section == 0, got_gain, own_gain)
 
-    def packed(layer):
+    def packed(layer, tensors):
+        shapes = [((512, 768), bf16), ((384, 512), bf16)][-min(2, len(tensors)) :]
         return call(
-            functools.partial(pack_body, layer),
-            [smem] + [anywhere] * 6,
-            [((512, 768), bf16), ((384, 512), bf16)],
+            functools.partial(pack_body, layer, tensors),
+            [smem] + [anywhere] * (2 * len(tensors)),
+            shapes,
             [pltpu.SemaphoreType.DMA((3,))],
             flops=1,
             moved=25 * 10**5,
-        )(place, *own, *swapped)
-
-    portions0 = [away(w) for w in packed(0)]
-    portions0 += [beside(w) for w in portions0]
+        )(place, *[own[n] for n in tensors], *[swapped[n] for n in tensors])
+
+    gate_far = away(own[0], 0)
+    up_far = away(swapped[1], 1)
+    down_far = away(packed(0, (2,))[0])
+    portions0 = (
+        gate_far,
+        beside(gate_far, [(0, 1)]),
+        up_far,
+        beside(up_far, [(1, 0)]),
+        down_far,
+        beside(down_far),
+    )
     arrived_first = exchange(out_first)
 
     flipped = call(flip_body, [vmem] * 6, [across] * 6, flops=10**6, moved=3 * 10**6)(*maps)
     pick0_t, high0_t, low0_t, pick1_t, high1_t, low1_t = flipped
 
+    portions1 = [
+        away(after(w, other))
+        for w, other in zip(packed(1, (0, 1, 2)), (up_far, down_far))
+    ]
+    portions1 = [w for far in portions1 for w in (far, beside(far))]
+
     result, early0, early0_far, pre_gate, pre_up = call(
         first_forward_body,
-        [smem, vmem] + [anywhere] * 10,
+        [smem, vmem] + [anywhere] * 12,
         [small, early_shape, early_shape, ((128, 768), f32), ((128, 768), f32)],
-        weight_scratch + [wide, matrix, sems],
+        weight_scratch
+        + [wide, matrix, early_room, early_room, plain_room, plain_room, sems]
+        + [pltpu.SemaphoreType.DMA((4,))],
         flops=6 * 10**8,
         moved=6 * 10**6,
+        out_spec=[vmem] + [anywhere] * 4,
     )(place, arrived_first, *own, *swapped, *portions0)
     returned = exchange(result)
-
-    portions1 = [away(after(w, other)) for w, other in zip(packed(1), portions0)]
-    portions1 += [beside(w) for w in portions1]
 
     hidden_first, out_second = call(
         between_body, [vmem] * 6, [block, small], flops=10**8, moved=2 * 10**6
     )(returned, x_first, second_gain, high0_t, low0_t, pick1)
     arrived_second = exchange(out_second)
 
-    picked, result_second, kept, sent, straight, cross, late1, late1_far, gain_second = call(
+    picked, result_second, gain_second, kept, sent, straight, cross, late1, late1_far = call(
         second_body,
-        [smem] + [vmem] * 4 + [anywhere] * 10,
-        [small, small] + [early_shape] * 4 + [late_shape] * 2 + [((8, 128), f32)],
+        [smem, vmem] + [anywhere] * 13,
+        [small, small, ((8, 128), f32)] + [early_shape] * 4 + [late_shape] * 2,
         weight_scratch
-        + [wide, matrix, matrix, pltpu.VMEM((128, 1280), bf16), pltpu.VMEM((128, 1280), bf16), sems],
+        + [wide, matrix, matrix, early_room, early_room]
+        + [arrival, early_room, early_room, late_room, late_room, sems]
+        + [pltpu.SemaphoreType.DMA((9,))],
         flops=12 * 10**8,
         moved=8 * 10**6,
+        out_spec=[vmem] * 3 + [anywhere] * 6,
     )(place, arrived_second, arrived_first, early0, early0_far, *own, *swapped, *portions1)
     returned = exchange(picked)
 
@@ -610,18 +686,21 @@
 
     picked, late0, late0_far = call(
         first_backward_body,
-        [smem] + [vmem] * 5 + [anywhere] * 10,
+        [smem, vmem] + [anywhere] * 16,
         [big, late_shape, late_shape],
-        weight_scratch + [wide, matrix, sems],
+        weight_scratch
+        + [wide, matrix, arrival, arrival, plain_room, plain_room, late_room, late_room, sems]
+        + [pltpu.SemaphoreType.DMA((6,))],
         flops=6 * 10**8,
         moved=8 * 10**6,
+        out_spec=[vmem] + [anywhere] * 2,
     )(
         place,
+        gain_second,
         arrived_third,
         arrived_first,
         pre_gate,
         pre_up,
-        gain_second,
         *own,
         *swapped,
         *portions0,
@@ -630,7 +709,7 @@
     returned = exchange(picked)
 
     hidden_second, hidden_sent = call(
-        second_output_body, [smem] + [vmem] * 4, [block, block], flops=10**8, moved=10**6
+        second_output_body, [smem] + [vmem] * 4, [block, block], flops=10**8, moved=10**6, grant=16
     )(place, arrived_third, hidden_first, high1_t, low1_t)
     both = ((micro_count, tokens, width), bf16)
     hidden = call(
@@ -652,15 +731,21 @@
         ],
         flops=12 * 10**8,
         moved=8 * 10**6,
+        grant=28,
         out_spec=anywhere,
     )(place, *early_parts, *late0_parts, *late1_parts)
 
     grad_first, grad_sent, gain_rows = call(
-        last_body, [smem] + [vmem] * 5, [block, block, ((16, 128), f32)], flops=10**8, moved=10**6
+        last_body,
+        [smem] + [vmem] * 5,
+        [block, ((144, 128), f32), ((16, 128), f32)],
+        flops=10**8,
+        moved=10**6,
+        grant=16,
     )(place, returned, x_first, grad_middle, first_gain, pick0_t)
     grads, gain_grad = call(
         final_body,
-        [smem] + [vmem] * 8,
+        [smem] + [vmem] * 7,
         [both, ((8, 128), f32)],
         [narrow],
         flops=10**5,
@@ -672,7 +757,6 @@
         grad_middle,
         beside(grad_sent),
         gain_rows,
-        beside(gain_rows),
         away(gain_rows),
         away(gain_rows, cross=True),
         own_gain,

time: 222 us -> 223 us (level)
  waiting for transfers between devices: 73.8 us -> 63.6 us
  local copies, waits for them, and re-layouts: 7.62 us -> 16 us
  starting transfers between devices: 67.4 us -> 75.2 us
  Pallas kernels: 49.3 us -> 45.1 us
    ppermute x12 -> x13, waiting for transfers between devices: 32.1 us -> 23.3 us  [away(): return lax.ppermute(block, every, pairs(layer, cross))]
    unnamed x80 -> x74, local copies, waits for them, and re-layouts: 7.62 us -> 16 us
    ppermute x12 -> x13, starting transfers between devices: 22.8 us -> 26.9 us  [away(): return lax.ppermute(block, every, pairs(layer, cross))]
    ppermute x16, starting transfers between devices: 4.48 us -> 8.08 us  [beside(): return lax.ppermute(block, 'section', route)]
  transfers between devices with their start and end apart: 33 -> 34, of which waited for: 16 -> 13; matrix products, arithmetic and copies ran while one was open for 1% -> 1% of each run, Pallas kernels for 16% -> 15%
where the time goes in v2:
time: 223 us; the launch traced here: 220 us
  starting transfers between devices  75.2 us (34%)
  waiting for transfers between devices  63.6 us (29%)
  Pallas kernels  45.1 us (20%)
  blocking collectives  18 us (8%)
  local copies, waits for them, and re-layouts  16 us (7%)
    all_to_all x5, starting transfers between devices, exchange(): lax.all_to_all(block, 'expert', split_axis=0, concat_axis=0, tiled=True)  40.1 us
    all_to_all x5, waiting for transfers between devices, exchange(): lax.all_to_all(block, 'expert', split_axis=0, concat_axis=0, tiled=True)  33.6 us
    ppermute x13, starting transfers between devices, away(): return lax.ppermute(block, every, pairs(layer, cross))  26.9 us
    ppermute x13, waiting for transfers between devices, away(): return lax.ppermute(block, every, pairs(layer, cross))  23.3 us
    all_to_all x1, blocking collectives, exchange(): lax.all_to_all(block, 'expert', split_axis=0, concat_axis=0, tiled=True)  18 us
    unnamed x74, local copies, waits for them, and re-layouts  16 us
    ppermute x16, starting transfers between devices, beside(): return lax.ppermute(block, 'section', route)  8.08 us
    pallas_call x1, Pallas kernels, window(): call(second_body, [smem, vmem] + [anywhere] * 13, [small, small, ((8, 128...  7.72 us
  transfers between devices with their start and end apart: 34, of which 13 were waited for; matrix products, arithmetic and copies ran while one was open for 1% of the time, Pallas kernels for 15%

profile of v2, /device:TPU:4, one launch (start us, length us, event | category | flops | bytes accessed | tf_op | source)
XLA Modules:
  0.0 220.3 jit_solution(15049520783096438007)
XLA Ops:
  1.2 4.1 %collective-permute-start.6 = (bf16[512,768]{1,0:T(8,128)(2,1)}, bf16[512,768]{1,0:T(8,128)(2,1)}, u32[]{:S(2)}, u32[]{:S(2)}) collective-permute-start(bf16[512,768]{1,0:T(8,128)(2,1)} %bitcast.28), channel_id=1, source_target_pairs={{0,1},{1,0},{2,3},{3,2},{4,5},{5,4},{6,7},{7,6},{8,9},{9,8},{10,11... | collective-permute-start | bytes 2359304 | tf_op jit(solution)/shard_map/ppermute | solution.py:548
  5.4 1.6 collective-permute-start.8
  7.4 2.0 collective-permute-done.refs_2_
  9.8 1.0 collective-permute-done.1.refs_4_
  12.8 2.7 %shard_map.127 = (bf16[64,32,128]{2,1,0:T(8,128)(2,1)}, bf16[128,128]{1,0:T(8,128)(2,1)}, bf16[128,128]{1,0:T(8,128)(2,1)}, bf16[1024,128]{1,0:T(8,128)(2,1)}, b...) custom-call(s32[2]{0:T(128)} %pad_add_fusion.refs_0_.place_ref, ...), custom_call_target="tpu_custom_call" | custom-call | flops 100000000 | bytes 2000000 | tf_op jit(solution)/shard_map/pallas_call | solution.py:583
  15.5 11.9 %all-to-all-start = ((bf16[64,32,128]{2,1,0:T(8,128)(2,1)}), bf16[64,32,128]{2,1,0:T(8,128)(2,1)S(1)}, u32[]{:S(2)}, u32[]{:S(2)}) async-start(bf16[64,32,128]{2,1,0:T(8,128)(2,1)} %get-tuple-element.56), calls=%async_computation | async-start | bytes 1048576 | tf_op jit(solution)/shard_map/all_to_all | solution.py:551
  28.3 2.4 %shard_map.128 = bf16[384,512]{1,0:T(8,128)(2,1)} custom-call(s32[2]{0:T(128)} %pad_add_fusion.refs_0_.place_ref, bf16[768,512]{1,0:T(8,128)(2,1)} %bitcast.23, bf16[768,512]{1,0:T(8,128)(2,1)} %copy-done.20), custom_call_target="tpu_custom_call" | custom-call | flops 1 | bytes 2500000 | tf_op jit(solution)/shard_map/pallas_call | solution.py:607
  30.8 1.6 collective-permute-start.10
  32.4 1.7 collective-permute-start.7
  34.2 1.3 collective-permute-start.9
  36.4 3.0 %shard_map.132 = (bf16[512,768]{1,0:T(8,128)(2,1)}, bf16[384,512]{1,0:T(8,128)(2,1)}) custom-call(s32[2]{0:T(128)} %pad_add_fusion.refs_0_.place_ref, bf16[512,768]{1,0:T(8,128)(2,1)} %bitcast.30, bf16[512,768]{1,0:T(8,128)(2,1)} %bitcast.35, bf16[768,512]{1,0:T(8,128)(2,1)} %bitcast.24, bf16[512,768]{1,0:T(8,128)(2,1)} %copy-done.22, ...), custom_call_target="tpu_custom_call" | custom-call | flops 1 | bytes 2500000 | tf_op jit(solution)/shard_map/pallas_call | solution.py:607
  39.3 2.1 collective-permute-start.12
  41.4 6.0 %collective-permute-done.10.refs_12_.refs_16_ = bf16[384,512]{1,0:T(8,128)(2,1)S(1)} collective-permute-done((bf16[384,512]{1,0:T(8,128)(2,1)}, bf16[384,512]{1,0:T(8,128)(2,1)S(1)}, u32[]{:S(2)}, u32[]{:S(2)}) %collective-permute-start.10) | collective-permute-done | bytes 393248 | tf_op jit(solution)/shard_map/ppermute | solution.py:548
  47.4 1.7 collective-permute-done.11.refs_13_.refs_17_
  50.8 5.1 %shard_map.129 = (bf16[64,16,128]{2,1,0:T(8,128)(2,1)}, bf16[128,1280]{1,0:T(8,128)(2,1)}, bf16[128,1280]{1,0:T(8,128)(2,1)}, f32[128,768]{1,0:T(8,128)}, f32[128,768]{1,0:T(8,128)}) custom-call(s32[2]{0:T(128)} %pad_add_fusion.refs_0_.place_ref, bf16[64,32,128]{2,1,0:T(8,128)(2,1)} %copy-done.23, bf16[512,768]{1,0:T(8,128)(2,1)} %bitcast.31, ...), custom_call_target="tpu_custom_call" | custom-call | flops 600000000 | bytes 6000000 | tf_op jit(solution)/shard_map/pallas_call | solution.py:638
  56.0 10.6 %all-to-all-start.1 = ((bf16[64,16,128]{2,1,0:T(8,128)(2,1)}), bf16[64,16,128]{2,1,0:T(8,128)(2,1)S(1)}, u32[]{:S(2)}, u32[]{:S(2)}) async-start(bf16[64,16,128]{2,1,0:T(8,128)(2,1)} %get-tuple-element.57), calls=%async_computation.1 | async-start | bytes 524288 | tf_op jit(solution)/shard_map/all_to_all | solution.py:551
  66.6 1.2 collective-permute-start.14
  67.8 2.7 %shard_map.130 = (bf16[128,1024]{1,0:T(8,128)(2,1)}, bf16[128,1024]{1,0:T(8,128)(2,1)}, bf16[128,1024]{1,0:T(8,128)(2,1)}, bf16[128,1024]{1,0:T(8,128)(2,1)}, bf...) custom-call(bf16[1024,128]{1,0:T(8,128)(2,1)} %get-tuple-element.59.refs_0_, ...), custom_call_target="tpu_custom_call" | custom-call | flops 1000000 | bytes 3000000 | tf_op jit(solution)/shard_map/pallas_call | solution.py:629
  71.1 7.9 %all-to-all-done.1.returned = bf16[64,16,128]{2,1,0:T(8,128)(2,1)S(1)} async-done(((bf16[64,16,128]{2,1,0:T(8,128)(2,1)}), bf16[64,16,128]{2,1,0:T(8,128)(2,1)S(1)}, u32[]{:S(2)}, u32[]{:S(2)}) %all-to-all-start.1) | async-done | bytes 262176 | tf_op jit(solution)/shard_map/all_to_all | solution.py:551
  79.7 2.5 %shard_map.131 = (bf16[128,128]{1,0:T(8,128)(2,1)}, bf16[64,16,128]{2,1,0:T(8,128)(2,1)}) custom-call(bf16[64,16,128]{2,1,0:T(8,128)(2,1)} %copy-done.29, bf16[128,128]{1,0:T(8,128)(2,1)} %get-tuple-element.58.x_ref, f32[8,128]{1,0:T(8,128)} %get-tuple-element.107.gain_ref, bf16[128,1024]{1,0:T(8,128)(2,1)} %get-tuple-element.65.high_t, ...), custom_call_target="tpu_custom_call" | custom-call | flops 100000000 | bytes 2000000 | tf_op jit(solution)/shard_map/pallas_call | solution.py:651
  82.2 6.0 %all-to-all-start.2 = ((bf16[64,16,128]{2,1,0:T(8,128)(2,1)}), bf16[64,16,128]{2,1,0:T(8,128)(2,1)S(1)}, u32[]{:S(2)}, u32[]{:S(2)}) async-start(bf16[64,16,128]{2,1,0:T(8,128)(2,1)} %get-tuple-element.68), calls=%async_computation.2 | async-start | bytes 524288 | tf_op jit(solution)/shard_map/all_to_all | solution.py:551
  88.3 1.7 collective-permute-done.15.refs_14_
  90.0 10.0 %all-to-all-done.2.refs_1_ = bf16[64,16,128]{2,1,0:T(8,128)(2,1)S(1)} async-done(((bf16[64,16,128]{2,1,0:T(8,128)(2,1)}), bf16[64,16,128]{2,1,0:T(8,128)(2,1)S(1)}, u32[]{:S(2)}, u32[]{:S(2)}) %all-to-all-start.2) | async-done | bytes 262176 | tf_op jit(solution)/shard_map/all_to_all | solution.py:551
  100.7 7.7 %shard_map.133 = (bf16[64,16,128]{2,1,0:T(8,128)(2,1)}, bf16[64,16,128]{2,1,0:T(8,128)(2,1)}, f32[8,128]{1,0:T(8,128)}, bf16[128,1280]{1,0:T(8,128)(2,1)}, bf16[...) custom-call(s32[2]{0:T(128)} %pad_add_fusion.refs_0_.place_ref, ...), custom_call_target="tpu_custom_call" | custom-call | flops 1200000000 | bytes 8000000 | tf_op jit(solution)/shard_map/pallas_call | solution.py:656
  108.4 18.0 %all_to_all.30.returned = bf16[64,16,128]{2,1,0:T(8,128)(2,1)} all-to-all(bf16[64,16,128]{2,1,0:T(8,128)(2,1)} %get-tuple-element.75), channel_id=1, replica_groups=mesh['section'=2,'expert'=64,'dp'=2] {'expert'}, dimensions={0} | all-to-all | bytes 524288 | tf_op jit(solution)/shard_map/all_to_all | solution.py:551
  126.4 2.7 %shard_map.134 = (bf16[128,128]{1,0:T(8,128)(2,1)}, bf16[64,32,128]{2,1,0:T(8,128)(2,1)}) custom-call(bf16[64,16,128]{2,1,0:T(8,128)(2,1)} %all_to_all.30.returned, bf16[64,16,128]{2,1,0:T(8,128)(2,1)} %get-tuple-element.76.result, bf16[128,128]{1,0:T(8,128)(2,1)} %get-tuple-element.67.x_ref.first, bf16[128,128]{1,0:T(8,128)(2,1)} %get-tuple-element.77.grad_ref, ...), custom_call_target="tpu_custom_call" | custom-call | flops 100000000 | bytes 2000000 | tf_op jit(solution)/shard_map/pallas_call | solution.py:673
  129.1 5.5 %all-to-all-start.4 = ((bf16[64,32,128]{2,1,0:T(8,128)(2,1)}), bf16[64,32,128]{2,1,0:T(8,128)(2,1)S(1)}, u32[]{:S(2)}, u32[]{:S(2)}) async-start(bf16[64,32,128]{2,1,0:T(8,128)(2,1)} %get-tuple-element.79), calls=%async_computation.4 | async-start | bytes 1048576 | tf_op jit(solution)/shard_map/all_to_all | solution.py:551
  134.7 1.3 collective-permute-start.26
  136.0 15.7 %all-to-all-done.4.arrived.refs_2_ = bf16[64,32,128]{2,1,0:T(8,128)(2,1)S(1)} async-done(((bf16[64,32,128]{2,1,0:T(8,128)(2,1)}), bf16[64,32,128]{2,1,0:T(8,128)(2,1)S(1)}, u32[]{:S(2)}, u32[]{:S(2)}) %all-to-all-start.4) | async-done | bytes 524320 | tf_op jit(solution)/shard_map/all_to_all | solution.py:551
  152.5 7.2 %shard_map.137 = (bf16[64,32,128]{2,1,0:T(8,128)(2,1)}, bf16[128,2048]{1,0:T(8,128)(2,1)}, bf16[128,2048]{1,0:T(8,128)(2,1)}) custom-call(s32[2]{0:T(128)} %pad_add_fusion.refs_0_.place_ref, f32[8,128]{1,0:T(8,128)} %get-tuple-element.84.refs_1_, bf16[64,32,128]{2,1,0:T(8,128)(2,1)} %copy-done, bf16[64,32,128]{2,1,0:T(8,128)(2,1)} %copy-done.23, ...), custom_call_target="tpu_custom_call" | custom-call | flops 600000000 | bytes 8000000 | tf_op jit(solution)/shard_map/pallas_call | solution.py:687
  159.7 6.1 %all-to-all-start.5 = ((bf16[64,32,128]{2,1,0:T(8,128)(2,1)}), bf16[64,32,128]{2,1,0:T(8,128)(2,1)S(1)}, u32[]{:S(2)}, u32[]{:S(2)}) async-start(bf16[64,32,128]{2,1,0:T(8,128)(2,1)} %get-tuple-element.87), calls=%async_computation.5 | async-start | bytes 1048576 | tf_op jit(solution)/shard_map/all_to_all | solution.py:551
  165.9 1.2 collective-permute-start.21
  167.0 2.2 collective-permute-start.22
  169.2 1.0 copy-done.1
  174.2 2.7 %collective-permute-start.28 = (bf16[128,2048]{1,0:T(8,128)(2,1)}, bf16[128,2048]{1,0:T(8,128)(2,1)S(1)}, u32[]{:S(2)}, u32[]{:S(2)}) collective-permute-start(bf16[128,2048]{1,0:T(8,128)(2,1)} %get-tuple-element.102), channel_id=1, source_target_pairs={{0,129},{1,128},{2,131},{3,130},{4,133},{5,132},{6,135},{7,134},{8... | collective-permute-start | bytes 1572872 | tf_op jit(solution)/shard_map/ppermute | solution.py:548
  176.9 4.8 %collective-permute-done.21.refs_3_ = bf16[128,1280]{1,0:T(8,128)(2,1)S(1)} collective-permute-done((bf16[128,1280]{1,0:T(8,128)(2,1)}, bf16[128,1280]{1,0:T(8,128)(2,1)S(1)}, u32[]{:S(2)}, u32[]{:S(2)}) %collective-permute-start.21) | collective-permute-done | bytes 327712 | tf_op jit(solution)/shard_map/ppermute | solution.py:548
  183.2 4.8 %collective-permute-done.22.refs_4_ = bf16[128,1280]{1,0:T(8,128)(2,1)S(1)} collective-permute-done((bf16[128,1280]{1,0:T(8,128)(2,1)}, bf16[128,1280]{1,0:T(8,128)(2,1)S(1)}, u32[]{:S(2)}, u32[]{:S(2)}) %collective-permute-start.22) | collective-permute-done | bytes 327712 | tf_op jit(solution)/shard_map/ppermute | solution.py:548
  188.7 1.3 collective-permute-start.23
  190.0 1.3 collective-permute-start.25
  191.3 4.3 %collective-permute-start.24 = (bf16[128,2048]{1,0:T(8,128)(2,1)}, bf16[128,2048]{1,0:T(8,128)(2,1)}, u32[]{:S(2)}, u32[]{:S(2)}) collective-permute-start(bf16[128,2048]{1,0:T(8,128)(2,1)} %get-tuple-element.100), channel_id=1, source_target_pairs={{0,1},{1,0},{2,3},{3,2},{4,5},{5,4},{6,7},{7,6},{8,9},{9,8},{10,11... | collective-permute-start | bytes 1572872 | tf_op jit(solution)/shard_map/ppermute | solution.py:548
  195.6 1.2 shard_map.136
  199.4 2.2 collective-permute-start.19
  201.5 1.9 collective-permute-start.18
  203.5 7.1 %collective-permute-done.25.refs_8_ = bf16[128,2048]{1,0:T(8,128)(2,1)} collective-permute-done((bf16[128,2048]{1,0:T(8,128)(2,1)}, bf16[128,2048]{1,0:T(8,128)(2,1)}, u32[]{:S(2)}, u32[]{:S(2)}) %collective-permute-start.25) | collective-permute-done | bytes 524320 | tf_op jit(solution)/shard_map/ppermute | solution.py:548
  211.2 1.0 copy-done.6
  212.1 1.0 copy-done.8
  214.1 4.9 %shard_map.140 = (f32[512,768]{1,0:T(8,128)}, f32[512,768]{1,0:T(8,128)}, f32[768,512]{1,0:T(8,128)}) custom-call(s32[2]{0:T(128)S(1)} %copy-done.18, bf16[128,1280]{1,0:T(8,128)(2,1)S(1)} %copy-done.4, bf16[128,1280]{1,0:T(8,128)(2,1)S(1)} %copy-done.6, bf16[128,1280]{1,0:T(8,128)(2,1)S(1)} %copy-done.8, bf16[128,1280]{1,0:T(8,128)(2,1)S(1)} %copy-done.10, ...), custom_call_target="tpu_custom_call" | custom-call | flops 1200000000 | bytes 8000000 | tf_op jit(solution)/shard_map/pallas_call | solution.py:719
  219.1 1.2 shard_map.139
  (111 shorter events, 20.1 us)
Async XLA Ops:
  0.6 4.7 %collective-permute-start.4 = (bf16[512,768]{1,0:T(8,128)(2,1)}, bf16[512,768]{1,0:T(8,128)(2,1)S(1)}, u32[]{:S(2)}, u32[]{:S(2)}) collective-permute-start(bf16[512,768]{1,0:T(8,128)(2,1)} %bitcast.34), channel_id=1, source_target_pairs={{0,128},{128,0},{1,129},{129,1},{2,130},{130,2},{3,131},{131,3},{4... | collective-permute-start | bytes 2359304 | tf_op jit(solution)/shard_map/ppermute | solution.py:545
  0.7 26.7 %collective-permute-start.5 = (bf16[768,512]{1,0:T(8,128)(2,1)}, bf16[768,512]{1,0:T(8,128)(2,1)S(1)}, u32[]{:S(2)}, u32[]{:S(2)}) collective-permute-start(bf16[768,512]{1,0:T(8,128)(2,1)} %bitcast.22), channel_id=1, source_target_pairs={{0,128},{128,0},{1,129},{129,1},{2,130},{130,2},{3,131},{131,3},{4... | collective-permute-start | bytes 2359304 | tf_op jit(solution)/shard_map/ppermute | solution.py:545
  1.2 31.2 %collective-permute-start.6 = (bf16[512,768]{1,0:T(8,128)(2,1)}, bf16[512,768]{1,0:T(8,128)(2,1)}, u32[]{:S(2)}, u32[]{:S(2)}) collective-permute-start(bf16[512,768]{1,0:T(8,128)(2,1)} %bitcast.28), channel_id=1, source_target_pairs={{0,1},{1,0},{2,3},{3,2},{4,5},{5,4},{6,7},{7,6},{8,9},{9,8},{10,11... | collective-permute-start | bytes 2359304 | tf_op jit(solution)/shard_map/ppermute | solution.py:548
  5.4 25.4 %copy-start.21 = (bf16[512,768]{1,0:T(8,128)(2,1)}, bf16[512,768]{1,0:T(8,128)(2,1)S(1)}, u32[]{:S(2)}) copy-start(bf16[512,768]{1,0:T(8,128)(2,1)S(1)} %collective-permute-done.4.refs_6_.refs_5_.refs_9_.refs_10_) | copy-start | bytes 2359300
  5.4 28.8 %collective-permute-start.8 = (bf16[512,768]{1,0:T(8,128)(2,1)S(1)}, bf16[512,768]{1,0:T(8,128)(2,1)}, u32[]{:S(2)}, u32[]{:S(2)}) collective-permute-start(bf16[512,768]{1,0:T(8,128)(2,1)S(1)} %collective-permute-done.4.refs_6_.refs_5_.refs_9_.refs_10_), channel_id=1, source_target_pairs={{128,129},{129,128},{130,131},{131,130},{132,133},{133,132},{134,1... | collective-permute-start | bytes 2359304 | tf_op jit(solution)/shard_map/ppermute | solution.py:548
  6.9 28.5 %collective-permute-start.3 = (bf16[512,768]{1,0:T(8,128)(2,1)}, bf16[512,768]{1,0:T(8,128)(2,1)S(1)}, u32[]{:S(2)}, u32[]{:S(2)}) collective-permute-start(bf16[512,768]{1,0:T(8,128)(2,1)} %bitcast.29), channel_id=1, source_target_pairs={{0,128},{128,0},{1,129},{129,1},{2,130},{130,2},{3,131},{131,3},{4... | collective-permute-start | bytes 2359304 | tf_op jit(solution)/shard_map/ppermute | solution.py:545
  7.3 2.1 collective-permute-start
  9.4 2.8 %copy-start.35 = (s32[6,2,16]{2,1,0:T(2,128)}, s32[6,2,16]{2,1,0:T(2,128)S(1)}, u32[]{:S(2)}) copy-start(s32[6,2,16]{2,1,0:T(2,128)S(1)} %collective-permute-done.refs_2_) | copy-start | bytes 2308
  9.4 1.4 collective-permute-start.1
  10.8 1.4 collective-permute-start.2
  15.5 31.9 %all-to-all-start = ((bf16[64,32,128]{2,1,0:T(8,128)(2,1)}), bf16[64,32,128]{2,1,0:T(8,128)(2,1)S(1)}, u32[]{:S(2)}, u32[]{:S(2)}) async-start(bf16[64,32,128]{2,1,0:T(8,128)(2,1)} %get-tuple-element.56), calls=%async_computation | async-start | bytes 1048576 | tf_op jit(solution)/shard_map/all_to_all | solution.py:551
  30.8 16.6 %collective-permute-start.10 = (bf16[384,512]{1,0:T(8,128)(2,1)}, bf16[384,512]{1,0:T(8,128)(2,1)S(1)}, u32[]{:S(2)}, u32[]{:S(2)}) collective-permute-start(bf16[384,512]{1,0:T(8,128)(2,1)} %shard_map.128), channel_id=1, source_target_pairs={{0,1},{1,0},{2,3},{3,2},{4,5},{5,4},{6,7},{7,6},{8,9},{9,8},{10,11... | collective-permute-start | bytes 1179656 | tf_op jit(solution)/shard_map/ppermute | solution.py:548
  32.4 15.0 %collective-permute-start.7 = (bf16[512,768]{1,0:T(8,128)(2,1)}, bf16[512,768]{1,0:T(8,128)(2,1)S(1)}, u32[]{:S(2)}, u32[]{:S(2)}) collective-permute-start(bf16[512,768]{1,0:T(8,128)(2,1)} %collective-permute-done.6.refs_8_.refs_12_), channel_id=1, source_target_pairs={{0,128},{1,129},{2,130},{3,131},{4,132},{5,133},{6,134},{7,135},{8... | collective-permute-start | bytes 2359304 | tf_op jit(solution)/shard_map/ppermute | solution.py:545
  34.2 15.0 %collective-permute-start.9 = (bf16[512,768]{1,0:T(8,128)(2,1)}, bf16[512,768]{1,0:T(8,128)(2,1)S(1)}, u32[]{:S(2)}, u32[]{:S(2)}) collective-permute-start(bf16[512,768]{1,0:T(8,128)(2,1)} %collective-permute-done.8.refs_10_.refs_14_), channel_id=1, source_target_pairs={{128,0},{129,1},{130,2},{131,3},{132,4},{133,5},{134,6},{135,7},{1... | collective-permute-start | bytes 2359304 | tf_op jit(solution)/shard_map/ppermute | solution.py:545
  39.3 28.4 %collective-permute-start.12 = (bf16[512,768]{1,0:T(8,128)(2,1)}, bf16[512,768]{1,0:T(8,128)(2,1)}, u32[]{:S(2)}, u32[]{:S(2)}) collective-permute-start(bf16[512,768]{1,0:T(8,128)(2,1)} %get-tuple-element.72), channel_id=1, source_target_pairs={{0,1},{1,0},{2,3},{3,2},{4,5},{5,4},{6,7},{7,6},{8,9},{9,8},{10,11... | collective-permute-start | bytes 2359304 | tf_op jit(solution)/shard_map/ppermute | solution.py:548
  47.4 1.7 collective-permute-start.11
  56.0 14.5 %copy-start.19 = (f32[1,1024]{1,0:T(1,128)S(1)}, f32[1,1024]{1,0:T(1,128)}, u32[]{:S(2)}) copy-start(f32[1,1024]{1,0:T(1,128)} %param.10) | copy-start | bytes 12292
  56.0 14.5 %copy-start.34 = (f32[8,128]{1,0:T(8,128)S(1)}, f32[8,128]{1,0:T(8,128)}, u32[]{:S(2)}) copy-start(f32[8,128]{1,0:T(8,128)} %copy-done.33) | copy-start | bytes 12292
  56.0 23.0 %all-to-all-start.1 = ((bf16[64,16,128]{2,1,0:T(8,128)(2,1)}), bf16[64,16,128]{2,1,0:T(8,128)(2,1)S(1)}, u32[]{:S(2)}, u32[]{:S(2)}) async-start(bf16[64,16,128]{2,1,0:T(8,128)(2,1)} %get-tuple-element.57), calls=%async_computation.1 | async-start | bytes 524288 | tf_op jit(solution)/shard_map/all_to_all | solution.py:551
  66.6 21.6 %collective-permute-start.14 = (bf16[384,512]{1,0:T(8,128)(2,1)}, bf16[384,512]{1,0:T(8,128)(2,1)S(1)}, u32[]{:S(2)}, u32[]{:S(2)}) collective-permute-start(bf16[384,512]{1,0:T(8,128)(2,1)} %get-tuple-element.74), channel_id=1, source_target_pairs={{0,1},{1,0},{2,3},{3,2},{4,5},{5,4},{6,7},{7,6},{8,9},{9,8},{10,11... | collective-permute-start | bytes 1179656 | tf_op jit(solution)/shard_map/ppermute | solution.py:548
  67.8 22.3 %collective-permute-start.13 = (bf16[512,768]{1,0:T(8,128)(2,1)}, bf16[512,768]{1,0:T(8,128)(2,1)S(1)}, u32[]{:S(2)}, u32[]{:S(2)}) collective-permute-start(bf16[512,768]{1,0:T(8,128)(2,1)} %collective-permute-done.12.refs_11_), channel_id=1, source_target_pairs={{0,128},{128,0},{1,129},{129,1},{2,130},{130,2},{3,131},{131,3},{4... | collective-permute-start | bytes 2359304 | tf_op jit(solution)/shard_map/ppermute | solution.py:545
  82.2 17.8 %all-to-all-start.2 = ((bf16[64,16,128]{2,1,0:T(8,128)(2,1)}), bf16[64,16,128]{2,1,0:T(8,128)(2,1)S(1)}, u32[]{:S(2)}, u32[]{:S(2)}) async-start(bf16[64,16,128]{2,1,0:T(8,128)(2,1)} %get-tuple-element.68), calls=%async_computation.2 | async-start | bytes 524288 | tf_op jit(solution)/shard_map/all_to_all | solution.py:551
  88.2 11.8 %copy-start.31 = (bf16[384,512]{1,0:T(8,128)(2,1)}, bf16[384,512]{1,0:T(8,128)(2,1)S(1)}, u32[]{:S(2)}) copy-start(bf16[384,512]{1,0:T(8,128)(2,1)S(1)} %collective-permute-done.14.refs_13_) | copy-start | bytes 1179652
  88.2 1.8 collective-permute-start.15
  90.0 10.0 %copy-start.32 = (bf16[384,512]{1,0:T(8,128)(2,1)}, bf16[384,512]{1,0:T(8,128)(2,1)S(1)}, u32[]{:S(2)}) copy-start(bf16[384,512]{1,0:T(8,128)(2,1)S(1)} %collective-permute-done.15.refs_14_) | copy-start | bytes 1179652
  90.0 10.0 %copy-start.30 = (bf16[512,768]{1,0:T(8,128)(2,1)}, bf16[512,768]{1,0:T(8,128)(2,1)S(1)}, u32[]{:S(2)}) copy-start(bf16[512,768]{1,0:T(8,128)(2,1)S(1)} %collective-permute-done.13.refs_12_) | copy-start | bytes 2359300
  108.4 26.3 %copy-start.2 = (bf16[128,2048]{1,0:T(8,128)(2,1)S(1)}, bf16[128,2048]{1,0:T(8,128)(2,1)}, u32[]{:S(2)}) copy-start(bf16[128,2048]{1,0:T(8,128)(2,1)} %get-tuple-element.101.refs_9_) | copy-start | bytes 1572868
  129.1 22.6 %all-to-all-start.4 = ((bf16[64,32,128]{2,1,0:T(8,128)(2,1)}), bf16[64,32,128]{2,1,0:T(8,128)(2,1)S(1)}, u32[]{:S(2)}, u32[]{:S(2)}) async-start(bf16[64,32,128]{2,1,0:T(8,128)(2,1)} %get-tuple-element.79), calls=%async_computation.4 | async-start | bytes 1048576 | tf_op jit(solution)/shard_map/all_to_all | solution.py:551
  134.7 55.3 %collective-permute-start.26 = (bf16[128,2048]{1,0:T(8,128)(2,1)S(1)}, bf16[128,2048]{1,0:T(8,128)(2,1)S(1)}, u32[]{:S(2)}, u32[]{:S(2)}) collective-permute-start(bf16[128,2048]{1,0:T(8,128)(2,1)S(1)} %copy-done.2), channel_id=1, source_target_pairs={{0,128},{1,129},{2,130},{3,131},{4,132},{5,133},{6,134},{7,135},{8... | collective-permute-start | bytes 1572872 | tf_op jit(solution)/shard_map/ppermute | solution.py:545
  152.5 16.7 %copy-start.11 = (bf16[128,128]{1,0:T(8,128)(2,1)S(1)}, bf16[128,128]{1,0:T(8,128)(2,1)}, u32[]{:S(2)}) copy-start(bf16[128,128]{1,0:T(8,128)(2,1)} %get-tuple-element.67.x_ref.first) | copy-start | bytes 98308
  152.5 16.7 %copy-start.18 = (s32[2]{0:T(128)S(1)}, s32[2]{0:T(128)}, u32[]{:S(2)}) copy-start(s32[2]{0:T(128)} %pad_add_fusion.refs_0_.place_ref) | copy-start | bytes 28
  159.6 29.0 %copy-start.3 = (bf16[128,2048]{1,0:T(8,128)(2,1)S(1)}, bf16[128,2048]{1,0:T(8,128)(2,1)}, u32[]{:S(2)}) copy-start(bf16[128,2048]{1,0:T(8,128)(2,1)} %get-tuple-element.99.refs_5_) | copy-start | bytes 1572868
  159.7 37.1 %copy-start.15 = (bf16[128,128]{1,0:T(8,128)(2,1)S(1)}, bf16[128,128]{1,0:T(8,128)(2,1)}, u32[]{:S(2)}) copy-start(bf16[128,128]{1,0:T(8,128)(2,1)} %get-tuple-element.58.x_ref) | copy-start | bytes 98308
  159.7 51.5 %copy-start.4 = (bf16[128,1280]{1,0:T(8,128)(2,1)S(1)}, bf16[128,1280]{1,0:T(8,128)(2,1)}, u32[]{:S(2)}) copy-start(bf16[128,1280]{1,0:T(8,128)(2,1)} %get-tuple-element.95.refs_1_) | copy-start | bytes 983044
  159.7 37.1 %all-to-all-start.5 = ((bf16[64,32,128]{2,1,0:T(8,128)(2,1)}), bf16[64,32,128]{2,1,0:T(8,128)(2,1)S(1)}, u32[]{:S(2)}, u32[]{:S(2)}) async-start(bf16[64,32,128]{2,1,0:T(8,128)(2,1)} %get-tuple-element.87), calls=%async_computation.5 | async-start | bytes 1048576 | tf_op jit(solution)/shard_map/all_to_all | solution.py:551
  165.8 7.7 %collective-permute-start.20 = (bf16[128,1280]{1,0:T(8,128)(2,1)}, bf16[128,1280]{1,0:T(8,128)(2,1)S(1)}, u32[]{:S(2)}, u32[]{:S(2)}) collective-permute-start(bf16[128,1280]{1,0:T(8,128)(2,1)} %get-tuple-element.96), channel_id=1, source_target_pairs={{0,128},{128,0},{1,129},{129,1},{2,130},{130,2},{3,131},{131,3},{4... | collective-permute-start | bytes 983048 | tf_op jit(solution)/shard_map/ppermute | solution.py:545
  165.9 15.9 %collective-permute-start.21 = (bf16[128,1280]{1,0:T(8,128)(2,1)}, bf16[128,1280]{1,0:T(8,128)(2,1)S(1)}, u32[]{:S(2)}, u32[]{:S(2)}) collective-permute-start(bf16[128,1280]{1,0:T(8,128)(2,1)} %get-tuple-element.97), channel_id=1, source_target_pairs={{0,1},{1,0},{2,3},{3,2},{4,5},{5,4},{6,7},{7,6},{8,9},{9,8},{10,11... | collective-permute-start | bytes 983048 | tf_op jit(solution)/shard_map/ppermute | solution.py:548
  167.0 20.9 %collective-permute-start.22 = (bf16[128,1280]{1,0:T(8,128)(2,1)}, bf16[128,1280]{1,0:T(8,128)(2,1)S(1)}, u32[]{:S(2)}, u32[]{:S(2)}) collective-permute-start(bf16[128,1280]{1,0:T(8,128)(2,1)} %get-tuple-element.98), channel_id=1, source_target_pairs={{0,129},{1,128},{2,131},{3,130},{4,133},{5,132},{6,135},{7,134},{8... | collective-permute-start | bytes 983048 | tf_op jit(solution)/shard_map/ppermute | solution.py:548
  173.0 18.3 %collective-permute-start.16 = (bf16[128,128]{1,0:T(8,128)(2,1)S(1)}, bf16[128,128]{1,0:T(8,128)(2,1)S(1)}, u32[]{:S(2)}, u32[]{:S(2)}) collective-permute-start(bf16[128,128]{1,0:T(8,128)(2,1)S(1)} %get-tuple-element.83), channel_id=1, source_target_pairs={{0,128},{128,0},{1,129},{129,1},{2,130},{130,2},{3,131},{131,3},{4... | collective-permute-start | bytes 98312 | tf_op jit(solution)/shard_map/ppermute | solution.py:545
  174.2 25.2 %collective-permute-start.28 = (bf16[128,2048]{1,0:T(8,128)(2,1)}, bf16[128,2048]{1,0:T(8,128)(2,1)S(1)}, u32[]{:S(2)}, u32[]{:S(2)}) collective-permute-start(bf16[128,2048]{1,0:T(8,128)(2,1)} %get-tuple-element.102), channel_id=1, source_target_pairs={{0,129},{1,128},{2,131},{3,130},{4,133},{5,132},{6,135},{7,134},{8... | collective-permute-start | bytes 1572872 | tf_op jit(solution)/shard_map/ppermute | solution.py:548
  182.5 19.1 %collective-permute-start.27 = (bf16[128,2048]{1,0:T(8,128)(2,1)}, bf16[128,2048]{1,0:T(8,128)(2,1)S(1)}, u32[]{:S(2)}, u32[]{:S(2)}) collective-permute-start(bf16[128,2048]{1,0:T(8,128)(2,1)} %get-tuple-element.102), channel_id=1, source_target_pairs={{128,129},{129,128},{130,131},{131,130},{132,133},{133,132},{134,1... | collective-permute-start | bytes 1572872 | tf_op jit(solution)/shard_map/ppermute | solution.py:548
  188.7 14.8 %collective-permute-start.23 = (bf16[128,2048]{1,0:T(8,128)(2,1)S(1)}, bf16[128,2048]{1,0:T(8,128)(2,1)}, u32[]{:S(2)}, u32[]{:S(2)}) collective-permute-start(bf16[128,2048]{1,0:T(8,128)(2,1)S(1)} %copy-done.3), channel_id=1, source_target_pairs={{128,0},{129,1},{130,2},{131,3},{132,4},{133,5},{134,6},{135,7},{1... | collective-permute-start | bytes 1572872 | tf_op jit(solution)/shard_map/ppermute | solution.py:545
  190.0 20.5 %collective-permute-start.25 = (bf16[128,2048]{1,0:T(8,128)(2,1)}, bf16[128,2048]{1,0:T(8,128)(2,1)}, u32[]{:S(2)}, u32[]{:S(2)}) collective-permute-start(bf16[128,2048]{1,0:T(8,128)(2,1)} %get-tuple-element.100), channel_id=1, source_target_pairs={{128,1},{129,0},{130,3},{131,2},{132,5},{133,4},{134,7},{135,6},{1... | collective-permute-start | bytes 1572872 | tf_op jit(solution)/shard_map/ppermute | solution.py:548
  191.3 19.9 %collective-permute-start.24 = (bf16[128,2048]{1,0:T(8,128)(2,1)}, bf16[128,2048]{1,0:T(8,128)(2,1)}, u32[]{:S(2)}, u32[]{:S(2)}) collective-permute-start(bf16[128,2048]{1,0:T(8,128)(2,1)} %get-tuple-element.100), channel_id=1, source_target_pairs={{0,1},{1,0},{2,3},{3,2},{4,5},{5,4},{6,7},{7,6},{8,9},{9,8},{10,11... | collective-permute-start | bytes 1572872 | tf_op jit(solution)/shard_map/ppermute | solution.py:548
  199.4 19.6 %collective-permute-start.19 = (f32[16,128]{1,0:T(8,128)S(1)}, f32[16,128]{1,0:T(8,128)S(1)}, u32[]{:S(2)}, u32[]{:S(2)}) collective-permute-start(f32[16,128]{1,0:T(8,128)S(1)} %get-tuple-element.92.refs_4_), channel_id=1, source_target_pairs={{0,129},{1,128},{2,131},{3,130},{4,133},{5,132},{6,135},{7,134},{8... | collective-permute-start | bytes 24584 | tf_op jit(solution)/shard_map/ppermute | solution.py:548
  201.5 17.5 %collective-permute-start.18 = (f32[16,128]{1,0:T(8,128)S(1)}, f32[16,128]{1,0:T(8,128)S(1)}, u32[]{:S(2)}, u32[]{:S(2)}) collective-permute-start(f32[16,128]{1,0:T(8,128)S(1)} %get-tuple-element.92.refs_4_), channel_id=1, source_target_pairs={{0,1},{1,0},{2,3},{3,2},{4,5},{5,4},{6,7},{7,6},{8,9},{9,8},{10,11... | collective-permute-start | bytes 24584 | tf_op jit(solution)/shard_map/ppermute | solution.py:548
  203.5 15.6 %collective-permute-start.17 = (f32[144,128]{1,0:T(8,128)S(1)}, f32[144,128]{1,0:T(8,128)S(1)}, u32[]{:S(2)}, u32[]{:S(2)}) collective-permute-start(f32[144,128]{1,0:T(8,128)S(1)} %get-tuple-element.91), channel_id=1, source_target_pairs={{0,128},{128,0},{1,129},{129,1},{2,130},{130,2},{3,131},{131,3},{4... | collective-permute-start | bytes 221192 | tf_op jit(solution)/shard_map/ppermute | solution.py:545
  214.1 5.0 %copy-start.17 = (bf16[128,128]{1,0:T(8,128)(2,1)S(1)}, bf16[128,128]{1,0:T(8,128)(2,1)}, u32[]{:S(2)}) copy-start(bf16[128,128]{1,0:T(8,128)(2,1)} %get-tuple-element.88.grad_ref.refs_2_) | copy-start | bytes 98308
  (23 other events, 22.5 us)

commit v3 on v2

--- a/solution.py
+++ b/solution.py
@@ -13,6 +13,7 @@
 vmem = pl.BlockSpec(memory_space=pltpu.VMEM)
 smem = pl.BlockSpec(memory_space=pltpu.SMEM)
 anywhere = pl.BlockSpec(memory_space=pl.ANY)
+hbm = pl.BlockSpec(memory_space=pltpu.HBM)
 
 
 def dot(left, right):
@@ -37,6 +38,52 @@
         cost_estimate=pl.CostEstimate(flops=flops, bytes_accessed=moved, transcendentals=0),
         compiler_params=pltpu.CompilerParams(vmem_limit_bytes=grant and grant * 2**20),
     )
+
+
+def begin(source, target, sem):
+    copy = pltpu.make_async_copy(source, target, sem)
+    copy.start()
+    return copy
+
+
+def finish(group):
+    for copy in group:
+        copy.wait()
+
+
+def staged_body(body, loaded, inputs, outputs, *refs):
+    ins = list(refs[:inputs])
+    outs = refs[inputs : inputs + outputs]
+    rooms = refs[inputs + outputs : 2 * inputs + 2 * outputs - loaded]
+    rest, sems = refs[2 * inputs + 2 * outputs - loaded : -1], refs[-1]
+    copies = []
+    for n in range(loaded, inputs):
+        copies.append(begin(ins[n], rooms[n - loaded], sems.at[n - loaded]))
+        ins[n] = rooms[n - loaded]
+    results = rooms[inputs - loaded :]
+    finish(copies)
+    body(*ins, *results, *rest)
+    finish(
+        [
+            begin(source, target, sems.at[inputs - loaded + n])
+            for n, (source, target) in enumerate(zip(results, outs))
+        ]
+    )
+
+
+def staged(body, in_specs, outs, arrays, scratch=()):
+    loaded = len(in_specs)
+    rooms = [pltpu.VMEM(array.shape, array.dtype) for array in arrays[loaded:]]
+    rooms += [pltpu.VMEM(shape, dtype) for shape, dtype in outs]
+    return call(
+        functools.partial(staged_body, body, loaded, len(arrays), len(outs)),
+        list(in_specs) + [hbm] * (len(arrays) - loaded),
+        outs,
+        rooms + list(scratch) + [pltpu.SemaphoreType.DMA((len(rooms),))],
+        flops=10**8,
+        moved=2 * 10**6,
+        out_spec=hbm,
+    )(*arrays)
 
 
 def token_rows(block, wide):
@@ -189,24 +236,24 @@
     return wide[...].astype(bf16)
 
 
-def fetch(place_ref, layer, sources, targets, sems):
+def fetch(place_ref, layer, sources, targets, sems, order=(0, 1, 2)):
     own, swapped = sources[0:3], sources[3:6]
     section, part = place_ref[0], place_ref[1]
     mine = pl.multiple_of(part * 512, 512)
     rest = pl.multiple_of((1 - part) * 512, 512)
-    downs = sources[-2:]
 
     def near(group, others):
         found = []
         for n in range(3):
-            if n < 2:
-                target = targets[n].at[pl.ds(mine, 512), :]
-            else:
-                target = targets[n].at[:, pl.ds(mine, 512)]
-            found.append([pltpu.make_async_copy(group[n], target, sems.at[n, 0])])
-        for n, source in enumerate(others):
-            target = targets[n].at[pl.ds(rest, 512), :]
-            found[n].append(pltpu.make_async_copy(source, target, sems.at[n, 1]))
+            copies = []
+            for h, (sources_now, start) in enumerate(((group, mine), (others, rest))):
+                if sources_now:
+                    if n < 2:
+                        target = targets[n].at[pl.ds(start, 512), :]
+                    else:
+                        target = targets[n].at[:, pl.ds(start, 512)]
+                    copies.append(pltpu.make_async_copy(sources_now[n], target, sems.at[n, h]))
+            found.append(copies)
         return found
 
     def far(n):
@@ -219,46 +266,37 @@
                 target = targets[n].at[pl.ds(start, 256), :]
             else:
                 start = pl.multiple_of(index * 384, 128)
-                source = downs[p]
+                source = sources[8 + p]
                 target = targets[n].at[pl.ds(start, 384), pl.ds(rest, 512)]
             found.append(pltpu.make_async_copy(source, target, sems.at[n, 1 + p]))
         return found
 
     if layer == 0:
-        gate_far, gate_passed, up_far, up_passed = sources[6:10]
-        lower, upper = (gate_far, up_passed), (gate_passed, up_far)
-        others = [[], [], far(2)]
+        gate, gate_passed, up, up_passed, down, down_passed = sources[6:12]
+        lower, upper = (gate, up_passed, down), (gate_passed, up, down_passed)
+        others = [[], [], []]
     else:
         lower, upper = (), ()
         others = [far(0), far(1), far(2)]
 
     @pl.when(section == 0)
     def _():
-        for copies in near(own if layer == 0 else swapped, lower):
-            for copy in copies:
+        groups = near(own if layer == 0 else swapped, lower)
+        for n in order:
+            for copy in groups[n]:
                 copy.start()
 
     @pl.when(section != 0)
     def _():
-        for copies in near(swapped if layer == 0 else own, upper):
-            for copy in copies:
+        groups = near(swapped if layer == 0 else own, upper)
+        for n in order:
+            for copy in groups[n]:
                 copy.start()
 
-    for copies in others:
-        for copy in copies:
+    for n in order:
+        for copy in others[n]:
             copy.start()
     return [first + second for first, second in zip(near(own, lower), others)]
-
-
-def begin(source, target, sem):
-    copy = pltpu.make_async_copy(source, target, sem)
-    copy.start()
-    return copy
-
-
-def finish(group):
-    for copy in group:
-        copy.wait()
 
 
 def gated(pre_gate, pre_up):
@@ -273,30 +311,32 @@
 
 
 def first_forward_body(*refs):
-    place_ref, arrived = refs[0:2]
+    place_ref, arrived_ref = refs[0:2]
     sources = refs[2:14]
-    result = refs[14]
-    outs = refs[15:19]
+    outs = refs[14:19]
     w_gate, w_up, w_down, wide, rows = refs[19:24]
-    early, early_far, gate_out, up_out, sems, more = refs[24:]
+    early, early_far, gate_out, up_out, arrived, result, sems, more = refs[24:]
+    load = begin(arrived_ref.at[:, 0:16, :], arrived, more.at[4])
     waits = fetch(place_ref, 0, sources, (w_gate, w_up, w_down), sems)
-    to_matrix(arrived[:, :16, :].reshape(1024, 128).astype(f32), wide, rows)
+    load.wait()
+    to_matrix(arrived[...].reshape(1024, 128).astype(f32), wide, rows)
     halves(place_ref, rows, early, early_far)
     finish(waits[0])
     pre_gate = dot(rows[...], w_gate[...])
     gate_out[...] = pre_gate
-    stores = [begin(gate_out, outs[2], more.at[2])]
+    stores = [begin(gate_out, outs[3], more.at[2])]
     finish(waits[1])
     pre_up = dot(rows[...], w_up[...])
     up_out[...] = pre_up
-    stores.append(begin(up_out, outs[3], more.at[3]))
+    stores.append(begin(up_out, outs[4], more.at[3]))
     acts = gated(pre_gate, pre_up).astype(bf16)
     early[:, 512:] = acts
     early_far[:, 512:] = acts
-    stores.append(begin(early, outs[0], more.at[0]))
-    stores.append(begin(early_far, outs[1], more.at[1]))
+    stores.append(begin(early, outs[1], more.at[0]))
+    stores.append(begin(early_far, outs[2], more.at[1]))
     finish(waits[2])
     result[...] = to_rows(dot(acts, w_down[...]), wide).reshape(64, 16, 128)
+    stores.append(begin(result, outs[0], more.at[5]))
     finish(stores)
 
 
@@ -315,10 +355,10 @@
 def second_body(*refs):
     place_ref, arrived, cot_ref, early0_ref, early0_far_ref = refs[0:5]
     sources = refs[5:15]
-    picked, result, gain_out = refs[15:18]
+    ends = refs[15:18]
     outs = refs[18:24]
     w_gate, w_up, w_down, wide, rows, grads, early, early_far = refs[24:32]
-    cot, early0, early0_far, late, late_far, sems, more = refs[32:]
+    cot, early0, early0_far, late, late_far, picked, result, gain_out, sems, more = refs[32:]
     waits = fetch(place_ref, 1, sources, (w_gate, w_up, w_down), sems)
     loads = [
         begin(cot_ref.at[:, 16:32, :], cot, more.at[0]),
@@ -366,20 +406,22 @@
     stores.append(begin(late_far, outs[5], more.at[8]))
     pick_rows = to_rows(dot_nt(gate_grad, w_gate[...]) + dot_nt(up_grad, w_up[...]), wide)
     picked[...] = pick_rows.reshape(64, 16, 128)
+    stores.append(begin(picked, ends[0], more.at[9]))
     gain_out[...] = gain_part(pick_rows, normed_rows)
+    stores.append(begin(gain_out, ends[2], more.at[10]))
     result[...] = to_rows(dot(acts, w_down[...]), wide).reshape(64, 16, 128)
+    stores.append(begin(result, ends[1], more.at[11]))
     finish(stores)
 
 
 def first_backward_body(*refs):
     place_ref, gain_second, arrived_ref, normed_ref, gate_ref, up_ref = refs[0:6]
     sources = refs[6:18]
-    picked = refs[18]
-    outs = refs[19:21]
+    outs = refs[18:21]
     w_gate, w_up, w_down, wide, grads = refs[21:26]
-    arrived, normed, pre_gate, pre_up, late, late_far, sems, more = refs[26:]
+    arrived, normed, pre_gate, pre_up, late, late_far, picked, sems, more = refs[26:]
     load = begin(arrived_ref.at[:, 0:16, :], arrived, more.at[0])
-    waits = fetch(place_ref, 0, sources, (w_gate, w_up, w_down), sems)
+    waits = fetch(place_ref, 0, sources, (w_gate, w_up, w_down), sems, (2, 0, 1))
     loads = [
         begin(gate_ref, pre_gate, more.at[1]),
         begin(up_ref, pre_up, more.at[2]),
@@ -395,7 +437,7 @@
     for target in (late, late_far):
         target[:, 512:1280] = gate_grad
         target[:, 1280:] = up_grad
-    stores = [begin(late, outs[0], more.at[4]), begin(late_far, outs[1], more.at[5])]
+    stores = [begin(late, outs[1], more.at[4]), begin(late_far, outs[2], more.at[5])]
     finish(waits[0])
     finish(waits[1])
     pick_rows = to_rows(dot_nt(gate_grad, w_gate[...]) + dot_nt(up_grad, w_up[...]), wide)
@@ -403,6 +445,7 @@
     gain_first = gain_part(pick_rows, normed[...].reshape(1024, 128))
     both = jnp.concatenate([gain_first, gain_second[...]], axis=0).astype(bf16)
     picked[:, 16:, :] = jnp.broadcast_to(both[None], (64, 16, 128))
+    stores.append(begin(picked, outs[0], more.at[6]))
     finish(stores)
 
 
@@ -455,7 +498,11 @@
     arrange(place_ref[0], first[...], second[...], got[...], wide, out)
 
 
-def last_body(place_ref, returned, x_ref, grad_ref, gain_ref, pick_t, grad_out, sent, gain_out):
+def last_body(*refs):
+    place_ref, returned = refs[0:2]
+    grad_out, sent, gain_out = refs[6:9]
+    x_ref, grad_ref, gain_ref, pick_t, sems = refs[9:]
+    finish([begin(refs[2 + n], refs[9 + n], sems.at[n]) for n in range(4)])
     rows = returned[:, :16, :].reshape(1024, 128)
     grad = input_gradient(rows, grad_ref[...], x_ref[...], gain_ref[...], pick_t[...])
     grad_out[...] = grad
@@ -580,23 +627,13 @@
     plain_room = pltpu.VMEM((128, 768), f32)
     arrival = pltpu.VMEM((64, 16, 128), bf16)
 
-    out_first, x_first, grad_last, *maps = call(
+    out_first, x_first, grad_last, *maps = staged(
         start_body,
         [smem] + [vmem] * 8,
         [big, block, block] + [down] * 6,
+        [place, own_routes, got_routes, own_gates, got_gates]
+        + [activations, cotangent, own_gain, got_gain],
         [narrow],
-        flops=10**8,
-        moved=2 * 10**6,
-    )(
-        place,
-        own_routes,
-        got_routes,
-        own_gates,
-        got_gates,
-        activations,
-        cotangent,
-        own_gain,
-        got_gain,
     )
     _, high0, low0, pick1, _, _ = maps
     first_gain = jnp.where(section == 0, own_gain, got_gain)
@@ -615,14 +652,14 @@
 
     gate_far = away(own[0], 0)
     up_far = away(swapped[1], 1)
-    down_far = away(packed(0, (2,))[0])
+    down_far = away(own[2], 0)
     portions0 = (
         gate_far,
         beside(gate_far, [(0, 1)]),
         up_far,
         beside(up_far, [(1, 0)]),
         down_far,
-        beside(down_far),
+        beside(down_far, [(0, 1)]),
     )
     arrived_first = exchange(out_first)
 
@@ -637,63 +674,60 @@
 
     result, early0, early0_far, pre_gate, pre_up = call(
         first_forward_body,
-        [smem, vmem] + [anywhere] * 12,
+        [smem] + [hbm] * 13,
         [small, early_shape, early_shape, ((128, 768), f32), ((128, 768), f32)],
         weight_scratch
-        + [wide, matrix, early_room, early_room, plain_room, plain_room, sems]
-        + [pltpu.SemaphoreType.DMA((4,))],
+        + [wide, matrix, early_room, early_room, plain_room, plain_room, arrival, arrival, sems]
+        + [pltpu.SemaphoreType.DMA((6,))],
         flops=6 * 10**8,
         moved=6 * 10**6,
-        out_spec=[vmem] + [anywhere] * 4,
+        out_spec=hbm,
     )(place, arrived_first, *own, *swapped, *portions0)
     returned = exchange(result)
 
-    hidden_first, out_second = call(
-        between_body, [vmem] * 6, [block, small], flops=10**8, moved=2 * 10**6
-    )(returned, x_first, second_gain, high0_t, low0_t, pick1)
+    hidden_first, out_second = staged(
+        between_body,
+        [vmem],
+        [block, small],
+        [returned, x_first, second_gain, high0_t, low0_t, pick1],
+    )
     arrived_second = exchange(out_second)
 
     picked, result_second, gain_second, kept, sent, straight, cross, late1, late1_far = call(
         second_body,
-        [smem, vmem] + [anywhere] * 13,
+        [smem, vmem] + [hbm] * 13,
         [small, small, ((8, 128), f32)] + [early_shape] * 4 + [late_shape] * 2,
         weight_scratch
         + [wide, matrix, matrix, early_room, early_room]
-        + [arrival, early_room, early_room, late_room, late_room, sems]
-        + [pltpu.SemaphoreType.DMA((9,))],
+        + [arrival, early_room, early_room, late_room, late_room, arrival, arrival]
+        + [pltpu.VMEM((8, 128), f32), sems, pltpu.SemaphoreType.DMA((12,))],
         flops=12 * 10**8,
         moved=8 * 10**6,
-        out_spec=[vmem] * 3 + [anywhere] * 6,
+        out_spec=hbm,
     )(place, arrived_second, arrived_first, early0, early0_far, *own, *swapped, *portions1)
     returned = exchange(picked)
 
     early_parts = (kept, beside(sent), away(straight), away(cross, cross=True))
     late1_parts = (late1, beside(late1, [(0, 1)]), away(late1_far, 1), away(late1_far, 1, True))
 
-    grad_middle, out_third = call(
-        turn_body, [vmem] * 8, [block, big], flops=10**8, moved=2 * 10**6
-    )(
-        returned,
-        result_second,
-        hidden_first,
-        grad_last,
-        second_gain,
-        pick1_t,
-        high0,
-        low0,
+    grad_middle, out_third = staged(
+        turn_body,
+        [vmem],
+        [block, big],
+        [returned, result_second, hidden_first, grad_last, second_gain, pick1_t, high0, low0],
     )
     arrived_third = exchange(out_third)
 
     picked, late0, late0_far = call(
         first_backward_body,
-        [smem, vmem] + [anywhere] * 16,
+        [smem, vmem] + [hbm] * 16,
         [big, late_shape, late_shape],
         weight_scratch
-        + [wide, matrix, arrival, arrival, plain_room, plain_room, late_room, late_room, sems]
-        + [pltpu.SemaphoreType.DMA((6,))],
+        + [wide, matrix, arrival, arrival, plain_room, plain_room, late_room, late_room]
+        + [pltpu.VMEM((64, 32, 128), bf16), sems, pltpu.SemaphoreType.DMA((7,))],
         flops=6 * 10**8,
         moved=8 * 10**6,
-        out_spec=[vmem] + [anywhere] * 2,
+        out_spec=hbm,
     )(
         place,
         gain_second,
@@ -737,8 +771,15 @@
 
     grad_first, grad_sent, gain_rows = call(
         last_body,
-        [smem] + [vmem] * 5,
+        [smem, vmem] + [hbm] * 4,
         [block, ((144, 128), f32), ((16, 128), f32)],
+        [
+            pltpu.VMEM((128, 128), bf16),
+            pltpu.VMEM((128, 128), bf16),
+            pltpu.VMEM((8, 128), f32),
+            matrix,
+            pltpu.SemaphoreType.DMA((4,)),
+        ],
         flops=10**8,
         moved=10**6,
         grant=16,

time: 223 us -> 226 us (1.013)
  starting transfers between devices: 75.2 us -> 86.8 us
  waiting for transfers between devices: 63.6 us -> 58.1 us
    all_to_all x5, starting transfers between devices: 40.1 us -> 45.3 us  [exchange(): lax.all_to_all(block, 'expert', split_axis=0, concat_axis=0, tiled=True)]
    ppermute x13, waiting for transfers between devices: 23.3 us -> 18.9 us  [away(): return lax.ppermute(block, every, pairs(layer, cross))]
    ppermute x16, starting transfers between devices: 8.08 us -> 12.4 us  [beside(): return lax.ppermute(block, 'section', route)]
    ppermute x16, waiting for transfers between devices: 6.84 us -> 3.82 us  [beside(): return lax.ppermute(block, 'section', route)]
    pallas_call x2 -> x1, Pallas kernels: 5.42 us -> 3 us  [packed(): call(functools.partial(pack_body, layer, tensors), [smem] + [anywhere] *...]
  transfers between devices with their start and end apart: 34 -> 34, of which waited for: 13 -> 12; matrix products, arithmetic and copies ran while one was open for 1% -> 1% of each run, Pallas kernels for 15% -> 14%
where the time goes in v3:
time: 226 us; the launch traced here: 223 us
  starting transfers between devices  86.8 us (38%)
  waiting for transfers between devices  58.1 us (26%)
  Pallas kernels  43.4 us (19%)
  blocking collectives  18.1 us (8%)
  local copies, waits for them, and re-layouts  14.6 us (6%)
    all_to_all x5, starting transfers between devices, exchange(): lax.all_to_all(block, 'expert', split_axis=0, concat_axis=0, tiled=True)  45.3 us
    all_to_all x5, waiting for transfers between devices, exchange(): lax.all_to_all(block, 'expert', split_axis=0, concat_axis=0, tiled=True)  35.4 us
    ppermute x13, starting transfers between devices, away(): return lax.ppermute(block, every, pairs(layer, cross))  29.1 us
    ppermute x13, waiting for transfers between devices, away(): return lax.ppermute(block, every, pairs(layer, cross))  18.9 us
    all_to_all x1, blocking collectives, exchange(): lax.all_to_all(block, 'expert', split_axis=0, concat_axis=0, tiled=True)  18.1 us
    unnamed x74, local copies, waits for them, and re-layouts  14.6 us
    ppermute x16, starting transfers between devices, beside(): return lax.ppermute(block, 'section', route)  12.4 us
    pallas_call x3, Pallas kernels, staged(): call(functools.partial(staged_body, body, loaded, len(arrays), len(outs))...  10.3 us
  transfers between devices with their start and end apart: 34, of which 12 were waited for; matrix products, arithmetic and copies ran while one was open for 1% of the time, Pallas kernels for 14%

profile of v3, /device:TPU:4, one launch (start us, length us, event | category | flops | bytes accessed | tf_op | source)
XLA Modules:
  0.0 223.5 jit_solution(2558813076956940842)
XLA Ops:
  0.7 4.1 %collective-permute-start.6 = (bf16[512,768]{1,0:T(8,128)(2,1)}, bf16[512,768]{1,0:T(8,128)(2,1)}, u32[]{:S(2)}, u32[]{:S(2)}) collective-permute-start(bf16[512,768]{1,0:T(8,128)(2,1)} %bitcast.22), channel_id=1, source_target_pairs={{0,1},{1,0},{2,3},{3,2},{4,5},{5,4},{6,7},{7,6},{8,9},{9,8},{10,11... | collective-permute-start | bytes 2359304 | tf_op jit(solution)/shard_map/ppermute | solution.py:595
  4.9 3.2 %collective-permute-start.10 = (bf16[768,512]{1,0:T(8,128)(2,1)}, bf16[768,512]{1,0:T(8,128)(2,1)}, u32[]{:S(2)}, u32[]{:S(2)}) collective-permute-start(bf16[768,512]{1,0:T(8,128)(2,1)} %bitcast.33), channel_id=1, source_target_pairs={{0,1},{1,0},{2,3},{3,2},{4,5},{5,4},{6,7},{7,6},{8,9},{9,8},{10,11... | collective-permute-start | bytes 2359304 | tf_op jit(solution)/shard_map/ppermute | solution.py:595
  8.1 1.6 collective-permute-start.8
  10.2 1.0 collective-permute-done.refs_2_
  11.6 1.0 collective-permute-done.1.refs_4_
  13.8 3.2 %shard_map.127 = (bf16[64,32,128]{2,1,0:T(8,128)(2,1)}, bf16[128,128]{1,0:T(8,128)(2,1)}, bf16[128,128]{1,0:T(8,128)(2,1)}, bf16[1024,128]{1,0:T(8,128)(2,1)}, b...) custom-call(s32[2]{0:T(128)} %pad_add_fusion.refs_0_.place_ref, ...), custom_call_target="tpu_custom_call" | custom-call | flops 100000000 | bytes 2000000 | tf_op jit(solution)/shard_map/pallas_call | solution.py:78
  17.0 12.8 %all-to-all-start = ((bf16[64,32,128]{2,1,0:T(8,128)(2,1)}), bf16[64,32,128]{2,1,0:T(8,128)(2,1)S(1)}, u32[]{:S(2)}, u32[]{:S(2)}) async-start(bf16[64,32,128]{2,1,0:T(8,128)(2,1)} %get-tuple-element.56), calls=%async_computation | async-start | bytes 1048576 | tf_op jit(solution)/shard_map/all_to_all | solution.py:598
  29.7 2.9 %collective-permute-start.7 = (bf16[512,768]{1,0:T(8,128)(2,1)}, bf16[512,768]{1,0:T(8,128)(2,1)}, u32[]{:S(2)}, u32[]{:S(2)}) collective-permute-start(bf16[512,768]{1,0:T(8,128)(2,1)} %collective-permute-done.6.refs_8_.refs_12_), channel_id=1, source_target_pairs={{0,128},{1,129},{2,130},{3,131},{4,132},{5,133},{6,134},{7,135},{8... | collective-permute-start | bytes 2359304 | tf_op jit(solution)/shard_map/ppermute | solution.py:592
  32.6 1.4 collective-permute-done.10.refs_12_.refs_16_
  34.0 2.2 collective-permute-start.11
  36.3 1.3 collective-permute-start.9
  39.3 3.0 %shard_map.131 = (bf16[512,768]{1,0:T(8,128)(2,1)}, bf16[384,512]{1,0:T(8,128)(2,1)}) custom-call(s32[2]{0:T(128)} %pad_add_fusion.refs_0_.place_ref, bf16[512,768]{1,0:T(8,128)(2,1)} %bitcast.24, bf16[512,768]{1,0:T(8,128)(2,1)} %bitcast.29, bf16[768,512]{1,0:T(8,128)(2,1)} %bitcast.35, bf16[512,768]{1,0:T(8,128)(2,1)} %copy-done.21, ...), custom_call_target="tpu_custom_call" | custom-call | flops 1 | bytes 2500000 | tf_op jit(solution)/shard_map/pallas_call | solution.py:644
  42.3 2.1 collective-permute-start.12
  44.4 3.6 %all-to-all-done.refs_1_.refs_2_.refs_3_ = bf16[64,32,128]{2,1,0:T(8,128)(2,1)S(1)} async-done(((bf16[64,32,128]{2,1,0:T(8,128)(2,1)}), bf16[64,32,128]{2,1,0:T(8,128)(2,1)S(1)}, u32[]{:S(2)}, u32[]{:S(2)}) %all-to-all-start) | async-done | bytes 524320 | tf_op jit(solution)/shard_map/all_to_all | solution.py:598
  48.8 4.3 %shard_map.128 = (bf16[64,16,128]{2,1,0:T(8,128)(2,1)}, bf16[128,1280]{1,0:T(8,128)(2,1)}, bf16[128,1280]{1,0:T(8,128)(2,1)}, f32[128,768]{1,0:T(8,128)}, f32[128,768]{1,0:T(8,128)}) custom-call(s32[2]{0:T(128)} %pad_add_fusion.refs_0_.place_ref, bf16[64,32,128]{2,1,0:T(8,128)(2,1)} %copy-done.23, bf16[512,768]{1,0:T(8,128)(2,1)} %bitcast.25, ...), custom_call_target="tpu_custom_call" | custom-call | flops 600000000 | bytes 6000000 | tf_op jit(solution)/shard_map/pallas_call | solution.py:675
  53.1 10.4 %all-to-all-start.1 = ((bf16[64,16,128]{2,1,0:T(8,128)(2,1)}), bf16[64,16,128]{2,1,0:T(8,128)(2,1)S(1)}, u32[]{:S(2)}, u32[]{:S(2)}) async-start(bf16[64,16,128]{2,1,0:T(8,128)(2,1)} %get-tuple-element.57), calls=%async_computation.1 | async-start | bytes 524288 | tf_op jit(solution)/shard_map/all_to_all | solution.py:598
  63.6 2.7 %collective-permute-start.14 = (bf16[384,512]{1,0:T(8,128)(2,1)S(1)}, bf16[384,512]{1,0:T(8,128)(2,1)S(1)}, u32[]{:S(2)}, u32[]{:S(2)}) collective-permute-start(bf16[384,512]{1,0:T(8,128)(2,1)S(1)} %copy-done.32), channel_id=1, source_target_pairs={{0,1},{1,0},{2,3},{3,2},{4,5},{5,4},{6,7},{7,6},{8,9},{9,8},{10,11... | collective-permute-start | bytes 1179656 | tf_op jit(solution)/shard_map/ppermute | solution.py:595
  66.3 1.1 collective-permute-start.13
  67.4 2.7 %shard_map.129 = (bf16[128,1024]{1,0:T(8,128)(2,1)}, bf16[128,1024]{1,0:T(8,128)(2,1)}, bf16[128,1024]{1,0:T(8,128)(2,1)}, bf16[128,1024]{1,0:T(8,128)(2,1)}, bf...) custom-call(bf16[1024,128]{1,0:T(8,128)(2,1)} %get-tuple-element.59.refs_0_, ...), custom_call_target="tpu_custom_call" | custom-call | flops 1000000 | bytes 3000000 | tf_op jit(solution)/shard_map/pallas_call | solution.py:666
  70.7 5.5 %all-to-all-done.1.refs_0_ = bf16[64,16,128]{2,1,0:T(8,128)(2,1)S(1)} async-done(((bf16[64,16,128]{2,1,0:T(8,128)(2,1)}), bf16[64,16,128]{2,1,0:T(8,128)(2,1)S(1)}, u32[]{:S(2)}, u32[]{:S(2)}) %all-to-all-start.1) | async-done | bytes 262176 | tf_op jit(solution)/shard_map/all_to_all | solution.py:598
  77.0 3.4 %shard_map.130 = (bf16[128,128]{1,0:T(8,128)(2,1)}, bf16[64,16,128]{2,1,0:T(8,128)(2,1)}) custom-call(bf16[64,16,128]{2,1,0:T(8,128)(2,1)} %copy-done.25, bf16[128,128]{1,0:T(8,128)(2,1)} %get-tuple-element.58.refs_1_.refs_2_, f32[8,128]{1,0:T(8,128)} %get-tuple-element.107.refs_2_.refs_4_, bf16[128,1024]{1,0:T(8,128)(2,1)} %get-tuple-element.65.refs_3_, ...), custom_call_target="tpu_custom_call" | custom-call | flops 100000000 | bytes 2000000 | tf_op jit(solution)/shard_map/pallas_call | solution.py:78
  80.4 10.1 %all-to-all-start.2 = ((bf16[64,16,128]{2,1,0:T(8,128)(2,1)}), bf16[64,16,128]{2,1,0:T(8,128)(2,1)S(1)}, u32[]{:S(2)}, u32[]{:S(2)}) async-start(bf16[64,16,128]{2,1,0:T(8,128)(2,1)} %get-tuple-element.68), calls=%async_computation.2 | async-start | bytes 524288 | tf_op jit(solution)/shard_map/all_to_all | solution.py:598
  90.8 1.7 collective-permute-done.15.refs_14_
  92.6 10.5 %all-to-all-done.2.refs_1_ = bf16[64,16,128]{2,1,0:T(8,128)(2,1)S(1)} async-done(((bf16[64,16,128]{2,1,0:T(8,128)(2,1)}), bf16[64,16,128]{2,1,0:T(8,128)(2,1)S(1)}, u32[]{:S(2)}, u32[]{:S(2)}) %all-to-all-start.2) | async-done | bytes 262176 | tf_op jit(solution)/shard_map/all_to_all | solution.py:598
  103.8 7.7 %shard_map.132 = (bf16[64,16,128]{2,1,0:T(8,128)(2,1)}, bf16[64,16,128]{2,1,0:T(8,128)(2,1)}, f32[8,128]{1,0:T(8,128)}, bf16[128,1280]{1,0:T(8,128)(2,1)}, bf16[...) custom-call(s32[2]{0:T(128)} %pad_add_fusion.refs_0_.place_ref, ...), custom_call_target="tpu_custom_call" | custom-call | flops 1200000000 | bytes 8000000 | tf_op jit(solution)/shard_map/pallas_call | solution.py:696
  111.5 18.1 %all_to_all.30.refs_0_ = bf16[64,16,128]{2,1,0:T(8,128)(2,1)} all-to-all(bf16[64,16,128]{2,1,0:T(8,128)(2,1)} %get-tuple-element.75), channel_id=1, replica_groups=mesh['section'=2,'expert'=64,'dp'=2] {'expert'}, dimensions={0} | all-to-all | bytes 524288 | tf_op jit(solution)/shard_map/all_to_all | solution.py:598
  129.6 3.7 %shard_map.133 = (bf16[128,128]{1,0:T(8,128)(2,1)}, bf16[64,32,128]{2,1,0:T(8,128)(2,1)}) custom-call(bf16[64,16,128]{2,1,0:T(8,128)(2,1)} %all_to_all.30.refs_0_, bf16[64,16,128]{2,1,0:T(8,128)(2,1)} %get-tuple-element.76.refs_1_, bf16[128,128]{1,0:T(8,128)(2,1)} %get-tuple-element.67.refs_2_.x_ref.first, bf16[128,128]{1,0:T(8,128)(2,1)} %get-tuple-element.77.refs_3_, ...), custom_call_target="tpu_custom_call" | custom-call | flops 100000000 | bytes 2000000 | tf_op jit(solution)/shard_map/pallas_call | solution.py:78
  133.3 5.9 %all-to-all-start.4 = ((bf16[64,32,128]{2,1,0:T(8,128)(2,1)}), bf16[64,32,128]{2,1,0:T(8,128)(2,1)S(1)}, u32[]{:S(2)}, u32[]{:S(2)}) async-start(bf16[64,32,128]{2,1,0:T(8,128)(2,1)} %get-tuple-element.79), calls=%async_computation.4 | async-start | bytes 1048576 | tf_op jit(solution)/shard_map/all_to_all | solution.py:598
  139.2 1.3 collective-permute-start.26
  140.5 15.8 %all-to-all-done.4.arrived.refs_2_ = bf16[64,32,128]{2,1,0:T(8,128)(2,1)S(1)} async-done(((bf16[64,32,128]{2,1,0:T(8,128)(2,1)}), bf16[64,32,128]{2,1,0:T(8,128)(2,1)S(1)}, u32[]{:S(2)}, u32[]{:S(2)}) %all-to-all-start.4) | async-done | bytes 524320 | tf_op jit(solution)/shard_map/all_to_all | solution.py:598
  157.2 6.3 %shard_map.136 = (bf16[64,32,128]{2,1,0:T(8,128)(2,1)}, bf16[128,2048]{1,0:T(8,128)(2,1)}, bf16[128,2048]{1,0:T(8,128)(2,1)}) custom-call(s32[2]{0:T(128)} %pad_add_fusion.refs_0_.place_ref, f32[8,128]{1,0:T(8,128)} %get-tuple-element.84.refs_1_, bf16[64,32,128]{2,1,0:T(8,128)(2,1)} %copy-done, bf16[64,32,128]{2,1,0:T(8,128)(2,1)} %copy-done.23, ...), custom_call_target="tpu_custom_call" | custom-call | flops 600000000 | bytes 8000000 | tf_op jit(solution)/shard_map/pallas_call | solution.py:721
  163.5 6.1 %all-to-all-start.5 = ((bf16[64,32,128]{2,1,0:T(8,128)(2,1)}), bf16[64,32,128]{2,1,0:T(8,128)(2,1)S(1)}, u32[]{:S(2)}, u32[]{:S(2)}) async-start(bf16[64,32,128]{2,1,0:T(8,128)(2,1)} %get-tuple-element.87), calls=%async_computation.5 | async-start | bytes 1048576 | tf_op jit(solution)/shard_map/all_to_all | solution.py:598
  169.8 3.2 %collective-permute-start.22 = (bf16[128,1280]{1,0:T(8,128)(2,1)}, bf16[128,1280]{1,0:T(8,128)(2,1)S(1)}, u32[]{:S(2)}, u32[]{:S(2)}) collective-permute-start(bf16[128,1280]{1,0:T(8,128)(2,1)} %get-tuple-element.98), channel_id=1, source_target_pairs={{0,129},{1,128},{2,131},{3,130},{4,133},{5,132},{6,135},{7,134},{8... | collective-permute-start | bytes 983048 | tf_op jit(solution)/shard_map/ppermute | solution.py:595
  173.0 1.0 copy-done.1
  178.0 1.9 collective-permute-start.28
  180.0 4.8 %collective-permute-done.21.refs_3_ = bf16[128,1280]{1,0:T(8,128)(2,1)S(1)} collective-permute-done((bf16[128,1280]{1,0:T(8,128)(2,1)S(1)}, bf16[128,1280]{1,0:T(8,128)(2,1)S(1)}, u32[]{:S(2)}, u32[]{:S(2)}) %collective-permute-start.21) | collective-permute-done | bytes 327712 | tf_op jit(solution)/shard_map/ppermute | solution.py:595
  186.2 5.1 %collective-permute-done.22.refs_4_ = bf16[128,1280]{1,0:T(8,128)(2,1)S(1)} collective-permute-done((bf16[128,1280]{1,0:T(8,128)(2,1)}, bf16[128,1280]{1,0:T(8,128)(2,1)S(1)}, u32[]{:S(2)}, u32[]{:S(2)}) %collective-permute-start.22) | collective-permute-done | bytes 327712 | tf_op jit(solution)/shard_map/ppermute | solution.py:595
  192.0 1.3 collective-permute-start.23
  193.3 1.3 collective-permute-start.25
  194.7 3.9 %collective-permute-start.24 = (bf16[128,2048]{1,0:T(8,128)(2,1)}, bf16[128,2048]{1,0:T(8,128)(2,1)}, u32[]{:S(2)}, u32[]{:S(2)}) collective-permute-start(bf16[128,2048]{1,0:T(8,128)(2,1)} %get-tuple-element.100), channel_id=1, source_target_pairs={{0,1},{1,0},{2,3},{3,2},{4,5},{5,4},{6,7},{7,6},{8,9},{9,8},{10,11... | collective-permute-start | bytes 1572872 | tf_op jit(solution)/shard_map/ppermute | solution.py:595
  198.6 1.2 shard_map.135
  201.5 1.0 shard_map.137
  202.6 2.3 %collective-permute-start.19 = (f32[16,128]{1,0:T(8,128)S(1)}, f32[16,128]{1,0:T(8,128)S(1)}, u32[]{:S(2)}, u32[]{:S(2)}) collective-permute-start(f32[16,128]{1,0:T(8,128)S(1)} %get-tuple-element.92.refs_4_), channel_id=1, source_target_pairs={{0,129},{1,128},{2,131},{3,130},{4,133},{5,132},{6,135},{7,134},{8... | collective-permute-start | bytes 24584 | tf_op jit(solution)/shard_map/ppermute | solution.py:595
  204.9 2.0 collective-permute-start.18
  206.8 7.1 %collective-permute-done.25.refs_8_ = bf16[128,2048]{1,0:T(8,128)(2,1)} collective-permute-done((bf16[128,2048]{1,0:T(8,128)(2,1)}, bf16[128,2048]{1,0:T(8,128)(2,1)}, u32[]{:S(2)}, u32[]{:S(2)}) %collective-permute-start.25) | collective-permute-done | bytes 524320 | tf_op jit(solution)/shard_map/ppermute | solution.py:595
  214.3 1.0 copy-done.6
  217.2 4.9 %shard_map.139 = (f32[512,768]{1,0:T(8,128)}, f32[512,768]{1,0:T(8,128)}, f32[768,512]{1,0:T(8,128)}) custom-call(s32[2]{0:T(128)S(1)} %copy-done.18, bf16[128,1280]{1,0:T(8,128)(2,1)S(1)} %copy-done.4, bf16[128,1280]{1,0:T(8,128)(2,1)S(1)} %copy-done.6, bf16[128,1280]{1,0:T(8,128)(2,1)S(1)} %copy-done.8, bf16[128,1280]{1,0:T(8,128)(2,1)S(1)} %copy-done.10, ...), custom_call_target="tpu_custom_call" | custom-call | flops 1200000000 | bytes 8000000 | tf_op jit(solution)/shard_map/pallas_call | solution.py:753
  222.2 1.2 shard_map.138
  (110 shorter events, 18.3 us)
Async XLA Ops:
  0.6 7.5 %collective-permute-start.4 = (bf16[512,768]{1,0:T(8,128)(2,1)}, bf16[512,768]{1,0:T(8,128)(2,1)S(1)}, u32[]{:S(2)}, u32[]{:S(2)}) collective-permute-start(bf16[512,768]{1,0:T(8,128)(2,1)} %bitcast.28), channel_id=1, source_target_pairs={{0,128},{128,0},{1,129},{129,1},{2,130},{130,2},{3,131},{131,3},{4... | collective-permute-start | bytes 2359304 | tf_op jit(solution)/shard_map/ppermute | solution.py:592
  0.7 29.0 %collective-permute-start.6 = (bf16[512,768]{1,0:T(8,128)(2,1)}, bf16[512,768]{1,0:T(8,128)(2,1)}, u32[]{:S(2)}, u32[]{:S(2)}) collective-permute-start(bf16[512,768]{1,0:T(8,128)(2,1)} %bitcast.22), channel_id=1, source_target_pairs={{0,1},{1,0},{2,3},{3,2},{4,5},{5,4},{6,7},{7,6},{8,9},{9,8},{10,11... | collective-permute-start | bytes 2359304 | tf_op jit(solution)/shard_map/ppermute | solution.py:595
  4.9 29.2 %collective-permute-start.10 = (bf16[768,512]{1,0:T(8,128)(2,1)}, bf16[768,512]{1,0:T(8,128)(2,1)}, u32[]{:S(2)}, u32[]{:S(2)}) collective-permute-start(bf16[768,512]{1,0:T(8,128)(2,1)} %bitcast.33), channel_id=1, source_target_pairs={{0,1},{1,0},{2,3},{3,2},{4,5},{5,4},{6,7},{7,6},{8,9},{9,8},{10,11... | collective-permute-start | bytes 2359304 | tf_op jit(solution)/shard_map/ppermute | solution.py:595
  8.1 29.5 %copy-start.20 = (bf16[512,768]{1,0:T(8,128)(2,1)}, bf16[512,768]{1,0:T(8,128)(2,1)S(1)}, u32[]{:S(2)}) copy-start(bf16[512,768]{1,0:T(8,128)(2,1)S(1)} %collective-permute-done.4.refs_6_.refs_5_.refs_9_.refs_10_) | copy-start | bytes 2359300
  8.1 28.1 %collective-permute-start.8 = (bf16[512,768]{1,0:T(8,128)(2,1)S(1)}, bf16[512,768]{1,0:T(8,128)(2,1)}, u32[]{:S(2)}, u32[]{:S(2)}) collective-permute-start(bf16[512,768]{1,0:T(8,128)(2,1)S(1)} %collective-permute-done.4.refs_6_.refs_5_.refs_9_.refs_10_), channel_id=1, source_target_pairs={{128,129},{129,128},{130,131},{131,130},{132,133},{133,132},{134,1... | collective-permute-start | bytes 2359304 | tf_op jit(solution)/shard_map/ppermute | solution.py:595
  9.7 3.3 %collective-permute-start.2 = (f32[8,128]{1,0:T(8,128)}, f32[8,128]{1,0:T(8,128)S(1)}, u32[]{:S(2)}, u32[]{:S(2)}) collective-permute-start(f32[8,128]{1,0:T(8,128)} %bitcast.18), channel_id=1, source_target_pairs={{0,128},{128,0},{1,129},{129,1},{2,130},{130,2},{3,131},{131,3},{4... | collective-permute-start | bytes 12296 | tf_op jit(solution)/shard_map/ppermute | solution.py:592
  9.7 1.5 collective-permute-start
  11.2 1.4 collective-permute-start.1
  12.6 24.9 %collective-permute-start.3 = (bf16[512,768]{1,0:T(8,128)(2,1)}, bf16[512,768]{1,0:T(8,128)(2,1)S(1)}, u32[]{:S(2)}, u32[]{:S(2)}) collective-permute-start(bf16[512,768]{1,0:T(8,128)(2,1)} %bitcast.23), channel_id=1, source_target_pairs={{0,128},{128,0},{1,129},{129,1},{2,130},{130,2},{3,131},{131,3},{4... | collective-permute-start | bytes 2359304 | tf_op jit(solution)/shard_map/ppermute | solution.py:592
  13.0 24.6 %collective-permute-start.5 = (bf16[768,512]{1,0:T(8,128)(2,1)}, bf16[768,512]{1,0:T(8,128)(2,1)S(1)}, u32[]{:S(2)}, u32[]{:S(2)}) collective-permute-start(bf16[768,512]{1,0:T(8,128)(2,1)} %bitcast.34), channel_id=1, source_target_pairs={{0,128},{128,0},{1,129},{129,1},{2,130},{130,2},{3,131},{131,3},{4... | collective-permute-start | bytes 2359304 | tf_op jit(solution)/shard_map/ppermute | solution.py:592
  17.0 31.0 %all-to-all-start = ((bf16[64,32,128]{2,1,0:T(8,128)(2,1)}), bf16[64,32,128]{2,1,0:T(8,128)(2,1)S(1)}, u32[]{:S(2)}, u32[]{:S(2)}) async-start(bf16[64,32,128]{2,1,0:T(8,128)(2,1)} %get-tuple-element.56), calls=%async_computation | async-start | bytes 1048576 | tf_op jit(solution)/shard_map/all_to_all | solution.py:598
  29.7 18.3 %collective-permute-start.7 = (bf16[512,768]{1,0:T(8,128)(2,1)}, bf16[512,768]{1,0:T(8,128)(2,1)}, u32[]{:S(2)}, u32[]{:S(2)}) collective-permute-start(bf16[512,768]{1,0:T(8,128)(2,1)} %collective-permute-done.6.refs_8_.refs_12_), channel_id=1, source_target_pairs={{0,128},{1,129},{2,130},{3,131},{4,132},{5,133},{6,134},{7,135},{8... | collective-permute-start | bytes 2359304 | tf_op jit(solution)/shard_map/ppermute | solution.py:592
  34.0 14.0 %collective-permute-start.11 = (bf16[768,512]{1,0:T(8,128)(2,1)}, bf16[768,512]{1,0:T(8,128)(2,1)}, u32[]{:S(2)}, u32[]{:S(2)}) collective-permute-start(bf16[768,512]{1,0:T(8,128)(2,1)} %collective-permute-done.10.refs_12_.refs_16_), channel_id=1, source_target_pairs={{0,128},{1,129},{2,130},{3,131},{4,132},{5,133},{6,134},{7,135},{8... | collective-permute-start | bytes 2359304 | tf_op jit(solution)/shard_map/ppermute | solution.py:592
  36.3 11.8 %collective-permute-start.9 = (bf16[512,768]{1,0:T(8,128)(2,1)}, bf16[512,768]{1,0:T(8,128)(2,1)}, u32[]{:S(2)}, u32[]{:S(2)}) collective-permute-start(bf16[512,768]{1,0:T(8,128)(2,1)} %collective-permute-done.8.refs_10_.refs_14_), channel_id=1, source_target_pairs={{128,0},{129,1},{130,2},{131,3},{132,4},{133,5},{134,6},{135,7},{1... | collective-permute-start | bytes 2359304 | tf_op jit(solution)/shard_map/ppermute | solution.py:592
  42.3 21.3 %copy-start.32 = (bf16[384,512]{1,0:T(8,128)(2,1)S(1)}, bf16[384,512]{1,0:T(8,128)(2,1)}, u32[]{:S(2)}) copy-start(bf16[384,512]{1,0:T(8,128)(2,1)} %get-tuple-element.74) | copy-start | bytes 1179652
  42.3 24.0 %collective-permute-start.12 = (bf16[512,768]{1,0:T(8,128)(2,1)}, bf16[512,768]{1,0:T(8,128)(2,1)S(1)}, u32[]{:S(2)}, u32[]{:S(2)}) collective-permute-start(bf16[512,768]{1,0:T(8,128)(2,1)} %get-tuple-element.72), channel_id=1, source_target_pairs={{0,1},{1,0},{2,3},{3,2},{4,5},{5,4},{6,7},{7,6},{8,9},{9,8},{10,11... | collective-permute-start | bytes 2359304 | tf_op jit(solution)/shard_map/ppermute | solution.py:595
  53.1 17.0 %copy-start.19 = (f32[1,1024]{1,0:T(1,128)S(1)}, f32[1,1024]{1,0:T(1,128)}, u32[]{:S(2)}) copy-start(f32[1,1024]{1,0:T(1,128)} %param.10) | copy-start | bytes 12292
  53.1 17.0 %copy-start.31 = (f32[8,128]{1,0:T(8,128)S(1)}, f32[8,128]{1,0:T(8,128)}, u32[]{:S(2)}) copy-start(f32[8,128]{1,0:T(8,128)} %copy-done.30) | copy-start | bytes 12292
  53.1 23.1 %all-to-all-start.1 = ((bf16[64,16,128]{2,1,0:T(8,128)(2,1)}), bf16[64,16,128]{2,1,0:T(8,128)(2,1)S(1)}, u32[]{:S(2)}, u32[]{:S(2)}) async-start(bf16[64,16,128]{2,1,0:T(8,128)(2,1)} %get-tuple-element.57), calls=%async_computation.1 | async-start | bytes 524288 | tf_op jit(solution)/shard_map/all_to_all | solution.py:598
  63.6 27.0 %collective-permute-start.14 = (bf16[384,512]{1,0:T(8,128)(2,1)S(1)}, bf16[384,512]{1,0:T(8,128)(2,1)S(1)}, u32[]{:S(2)}, u32[]{:S(2)}) collective-permute-start(bf16[384,512]{1,0:T(8,128)(2,1)S(1)} %copy-done.32), channel_id=1, source_target_pairs={{0,1},{1,0},{2,3},{3,2},{4,5},{5,4},{6,7},{7,6},{8,9},{9,8},{10,11... | collective-permute-start | bytes 1179656 | tf_op jit(solution)/shard_map/ppermute | solution.py:595
  66.3 14.1 %copy-start.26 = (bf16[512,768]{1,0:T(8,128)(2,1)}, bf16[512,768]{1,0:T(8,128)(2,1)S(1)}, u32[]{:S(2)}) copy-start(bf16[512,768]{1,0:T(8,128)(2,1)S(1)} %collective-permute-done.12.refs_11_) | copy-start | bytes 2359300
  66.3 26.3 %collective-permute-start.13 = (bf16[512,768]{1,0:T(8,128)(2,1)S(1)}, bf16[512,768]{1,0:T(8,128)(2,1)S(1)}, u32[]{:S(2)}, u32[]{:S(2)}) collective-permute-start(bf16[512,768]{1,0:T(8,128)(2,1)S(1)} %collective-permute-done.12.refs_11_), channel_id=1, source_target_pairs={{0,128},{128,0},{1,129},{129,1},{2,130},{130,2},{3,131},{131,3},{4... | collective-permute-start | bytes 2359304 | tf_op jit(solution)/shard_map/ppermute | solution.py:592
  80.4 22.7 %all-to-all-start.2 = ((bf16[64,16,128]{2,1,0:T(8,128)(2,1)}), bf16[64,16,128]{2,1,0:T(8,128)(2,1)S(1)}, u32[]{:S(2)}, u32[]{:S(2)}) async-start(bf16[64,16,128]{2,1,0:T(8,128)(2,1)} %get-tuple-element.68), calls=%async_computation.2 | async-start | bytes 524288 | tf_op jit(solution)/shard_map/all_to_all | solution.py:598
  90.6 12.5 %copy-start.28 = (bf16[384,512]{1,0:T(8,128)(2,1)}, bf16[384,512]{1,0:T(8,128)(2,1)S(1)}, u32[]{:S(2)}) copy-start(bf16[384,512]{1,0:T(8,128)(2,1)S(1)} %collective-permute-done.14.refs_13_) | copy-start | bytes 1179652
  90.6 2.0 collective-permute-start.15
  111.5 27.7 %copy-start.2 = (bf16[128,2048]{1,0:T(8,128)(2,1)S(1)}, bf16[128,2048]{1,0:T(8,128)(2,1)}, u32[]{:S(2)}) copy-start(bf16[128,2048]{1,0:T(8,128)(2,1)} %get-tuple-element.101.refs_9_) | copy-start | bytes 1572868
  133.3 23.1 %all-to-all-start.4 = ((bf16[64,32,128]{2,1,0:T(8,128)(2,1)}), bf16[64,32,128]{2,1,0:T(8,128)(2,1)S(1)}, u32[]{:S(2)}, u32[]{:S(2)}) async-start(bf16[64,32,128]{2,1,0:T(8,128)(2,1)} %get-tuple-element.79), calls=%async_computation.4 | async-start | bytes 1048576 | tf_op jit(solution)/shard_map/all_to_all | solution.py:598
  139.2 54.1 %collective-permute-start.26 = (bf16[128,2048]{1,0:T(8,128)(2,1)S(1)}, bf16[128,2048]{1,0:T(8,128)(2,1)S(1)}, u32[]{:S(2)}, u32[]{:S(2)}) collective-permute-start(bf16[128,2048]{1,0:T(8,128)(2,1)S(1)} %copy-done.2), channel_id=1, source_target_pairs={{0,128},{1,129},{2,130},{3,131},{4,132},{5,133},{6,134},{7,135},{8... | collective-permute-start | bytes 1572872 | tf_op jit(solution)/shard_map/ppermute | solution.py:592
  157.2 12.4 %copy-start.34 = (bf16[128,1280]{1,0:T(8,128)(2,1)S(1)}, bf16[128,1280]{1,0:T(8,128)(2,1)}, u32[]{:S(2)}) copy-start(bf16[128,1280]{1,0:T(8,128)(2,1)} %get-tuple-element.96) | copy-start | bytes 983044
  157.2 12.5 %copy-start.33 = (bf16[128,1280]{1,0:T(8,128)(2,1)S(1)}, bf16[128,1280]{1,0:T(8,128)(2,1)}, u32[]{:S(2)}) copy-start(bf16[128,1280]{1,0:T(8,128)(2,1)} %get-tuple-element.97) | copy-start | bytes 983044
  157.2 15.9 %copy-start.11 = (bf16[128,128]{1,0:T(8,128)(2,1)S(1)}, bf16[128,128]{1,0:T(8,128)(2,1)}, u32[]{:S(2)}) copy-start(bf16[128,128]{1,0:T(8,128)(2,1)} %get-tuple-element.67.refs_2_.x_ref.first) | copy-start | bytes 98308
  157.2 15.9 %copy-start.18 = (s32[2]{0:T(128)S(1)}, s32[2]{0:T(128)}, u32[]{:S(2)}) copy-start(s32[2]{0:T(128)} %pad_add_fusion.refs_0_.place_ref) | copy-start | bytes 28
  163.5 28.6 %copy-start.3 = (bf16[128,2048]{1,0:T(8,128)(2,1)S(1)}, bf16[128,2048]{1,0:T(8,128)(2,1)}, u32[]{:S(2)}) copy-start(bf16[128,2048]{1,0:T(8,128)(2,1)} %get-tuple-element.99.refs_5_) | copy-start | bytes 1572868
  163.5 36.4 %copy-start.15 = (bf16[128,128]{1,0:T(8,128)(2,1)S(1)}, bf16[128,128]{1,0:T(8,128)(2,1)}, u32[]{:S(2)}) copy-start(bf16[128,128]{1,0:T(8,128)(2,1)} %get-tuple-element.58.refs_1_.refs_2_) | copy-start | bytes 98308
  163.5 50.8 %copy-start.4 = (bf16[128,1280]{1,0:T(8,128)(2,1)S(1)}, bf16[128,1280]{1,0:T(8,128)(2,1)}, u32[]{:S(2)}) copy-start(bf16[128,1280]{1,0:T(8,128)(2,1)} %get-tuple-element.95.refs_1_) | copy-start | bytes 983044
  163.5 36.3 %all-to-all-start.5 = ((bf16[64,32,128]{2,1,0:T(8,128)(2,1)}), bf16[64,32,128]{2,1,0:T(8,128)(2,1)S(1)}, u32[]{:S(2)}, u32[]{:S(2)}) async-start(bf16[64,32,128]{2,1,0:T(8,128)(2,1)} %get-tuple-element.87), calls=%async_computation.5 | async-start | bytes 1048576 | tf_op jit(solution)/shard_map/all_to_all | solution.py:598
  169.6 7.7 %collective-permute-start.20 = (bf16[128,1280]{1,0:T(8,128)(2,1)S(1)}, bf16[128,1280]{1,0:T(8,128)(2,1)S(1)}, u32[]{:S(2)}, u32[]{:S(2)}) collective-permute-start(bf16[128,1280]{1,0:T(8,128)(2,1)S(1)} %copy-done.34), channel_id=1, source_target_pairs={{0,128},{128,0},{1,129},{129,1},{2,130},{130,2},{3,131},{131,3},{4... | collective-permute-start | bytes 983048 | tf_op jit(solution)/shard_map/ppermute | solution.py:592
  169.7 15.1 %collective-permute-start.21 = (bf16[128,1280]{1,0:T(8,128)(2,1)S(1)}, bf16[128,1280]{1,0:T(8,128)(2,1)S(1)}, u32[]{:S(2)}, u32[]{:S(2)}) collective-permute-start(bf16[128,1280]{1,0:T(8,128)(2,1)S(1)} %copy-done.33), channel_id=1, source_target_pairs={{0,1},{1,0},{2,3},{3,2},{4,5},{5,4},{6,7},{7,6},{8,9},{9,8},{10,11... | collective-permute-start | bytes 983048 | tf_op jit(solution)/shard_map/ppermute | solution.py:595
  169.8 21.5 %collective-permute-start.22 = (bf16[128,1280]{1,0:T(8,128)(2,1)}, bf16[128,1280]{1,0:T(8,128)(2,1)S(1)}, u32[]{:S(2)}, u32[]{:S(2)}) collective-permute-start(bf16[128,1280]{1,0:T(8,128)(2,1)} %get-tuple-element.98), channel_id=1, source_target_pairs={{0,129},{1,128},{2,131},{3,130},{4,133},{5,132},{6,135},{7,134},{8... | collective-permute-start | bytes 983048 | tf_op jit(solution)/shard_map/ppermute | solution.py:595
  176.8 17.8 %collective-permute-start.16 = (bf16[128,128]{1,0:T(8,128)(2,1)S(1)}, bf16[128,128]{1,0:T(8,128)(2,1)S(1)}, u32[]{:S(2)}, u32[]{:S(2)}) collective-permute-start(bf16[128,128]{1,0:T(8,128)(2,1)S(1)} %get-tuple-element.83), channel_id=1, source_target_pairs={{0,128},{128,0},{1,129},{129,1},{2,130},{130,2},{3,131},{131,3},{4... | collective-permute-start | bytes 98312 | tf_op jit(solution)/shard_map/ppermute | solution.py:592
  178.0 24.5 %collective-permute-start.28 = (bf16[128,2048]{1,0:T(8,128)(2,1)}, bf16[128,2048]{1,0:T(8,128)(2,1)S(1)}, u32[]{:S(2)}, u32[]{:S(2)}) collective-permute-start(bf16[128,2048]{1,0:T(8,128)(2,1)} %get-tuple-element.102), channel_id=1, source_target_pairs={{0,129},{1,128},{2,131},{3,130},{4,133},{5,132},{6,135},{7,134},{8... | collective-permute-start | bytes 1572872 | tf_op jit(solution)/shard_map/ppermute | solution.py:595
  185.5 19.3 %collective-permute-start.27 = (bf16[128,2048]{1,0:T(8,128)(2,1)}, bf16[128,2048]{1,0:T(8,128)(2,1)S(1)}, u32[]{:S(2)}, u32[]{:S(2)}) collective-permute-start(bf16[128,2048]{1,0:T(8,128)(2,1)} %get-tuple-element.102), channel_id=1, source_target_pairs={{128,129},{129,128},{130,131},{131,130},{132,133},{133,132},{134,1... | collective-permute-start | bytes 1572872 | tf_op jit(solution)/shard_map/ppermute | solution.py:595
  192.0 14.8 %collective-permute-start.23 = (bf16[128,2048]{1,0:T(8,128)(2,1)S(1)}, bf16[128,2048]{1,0:T(8,128)(2,1)}, u32[]{:S(2)}, u32[]{:S(2)}) collective-permute-start(bf16[128,2048]{1,0:T(8,128)(2,1)S(1)} %copy-done.3), channel_id=1, source_target_pairs={{128,0},{129,1},{130,2},{131,3},{132,4},{133,5},{134,6},{135,7},{1... | collective-permute-start | bytes 1572872 | tf_op jit(solution)/shard_map/ppermute | solution.py:592
  193.3 20.5 %collective-permute-start.25 = (bf16[128,2048]{1,0:T(8,128)(2,1)}, bf16[128,2048]{1,0:T(8,128)(2,1)}, u32[]{:S(2)}, u32[]{:S(2)}) collective-permute-start(bf16[128,2048]{1,0:T(8,128)(2,1)} %get-tuple-element.100), channel_id=1, source_target_pairs={{128,1},{129,0},{130,3},{131,2},{132,5},{133,4},{134,7},{135,6},{1... | collective-permute-start | bytes 1572872 | tf_op jit(solution)/shard_map/ppermute | solution.py:595
  194.7 19.7 %collective-permute-start.24 = (bf16[128,2048]{1,0:T(8,128)(2,1)}, bf16[128,2048]{1,0:T(8,128)(2,1)}, u32[]{:S(2)}, u32[]{:S(2)}) collective-permute-start(bf16[128,2048]{1,0:T(8,128)(2,1)} %get-tuple-element.100), channel_id=1, source_target_pairs={{0,1},{1,0},{2,3},{3,2},{4,5},{5,4},{6,7},{7,6},{8,9},{9,8},{10,11... | collective-permute-start | bytes 1572872 | tf_op jit(solution)/shard_map/ppermute | solution.py:595
  202.6 19.6 %collective-permute-start.19 = (f32[16,128]{1,0:T(8,128)S(1)}, f32[16,128]{1,0:T(8,128)S(1)}, u32[]{:S(2)}, u32[]{:S(2)}) collective-permute-start(f32[16,128]{1,0:T(8,128)S(1)} %get-tuple-element.92.refs_4_), channel_id=1, source_target_pairs={{0,129},{1,128},{2,131},{3,130},{4,133},{5,132},{6,135},{7,134},{8... | collective-permute-start | bytes 24584 | tf_op jit(solution)/shard_map/ppermute | solution.py:595
  204.9 17.3 %collective-permute-start.18 = (f32[16,128]{1,0:T(8,128)S(1)}, f32[16,128]{1,0:T(8,128)S(1)}, u32[]{:S(2)}, u32[]{:S(2)}) collective-permute-start(f32[16,128]{1,0:T(8,128)S(1)} %get-tuple-element.92.refs_4_), channel_id=1, source_target_pairs={{0,1},{1,0},{2,3},{3,2},{4,5},{5,4},{6,7},{7,6},{8,9},{9,8},{10,11... | collective-permute-start | bytes 24584 | tf_op jit(solution)/shard_map/ppermute | solution.py:595
  206.8 15.4 %collective-permute-start.17 = (f32[144,128]{1,0:T(8,128)S(1)}, f32[144,128]{1,0:T(8,128)S(1)}, u32[]{:S(2)}, u32[]{:S(2)}) collective-permute-start(f32[144,128]{1,0:T(8,128)S(1)} %get-tuple-element.91), channel_id=1, source_target_pairs={{0,128},{128,0},{1,129},{129,1},{2,130},{130,2},{3,131},{131,3},{4... | collective-permute-start | bytes 221192 | tf_op jit(solution)/shard_map/ppermute | solution.py:592
  (23 other events, 45.2 us)

commit v4 on v3

--- a/solution.py
+++ b/solution.py
@@ -51,39 +51,9 @@
         copy.wait()
 
 
-def staged_body(body, loaded, inputs, outputs, *refs):
-    ins = list(refs[:inputs])
-    outs = refs[inputs : inputs + outputs]
-    rooms = refs[inputs + outputs : 2 * inputs + 2 * outputs - loaded]
-    rest, sems = refs[2 * inputs + 2 * outputs - loaded : -1], refs[-1]
-    copies = []
-    for n in range(loaded, inputs):
-        copies.append(begin(ins[n], rooms[n - loaded], sems.at[n - loaded]))
-        ins[n] = rooms[n - loaded]
-    results = rooms[inputs - loaded :]
-    finish(copies)
-    body(*ins, *results, *rest)
-    finish(
-        [
-            begin(source, target, sems.at[inputs - loaded + n])
-            for n, (source, target) in enumerate(zip(results, outs))
-        ]
-    )
-
-
-def staged(body, in_specs, outs, arrays, scratch=()):
-    loaded = len(in_specs)
-    rooms = [pltpu.VMEM(array.shape, array.dtype) for array in arrays[loaded:]]
-    rooms += [pltpu.VMEM(shape, dtype) for shape, dtype in outs]
-    return call(
-        functools.partial(staged_body, body, loaded, len(arrays), len(outs)),
-        list(in_specs) + [hbm] * (len(arrays) - loaded),
-        outs,
-        rooms + list(scratch) + [pltpu.SemaphoreType.DMA((len(rooms),))],
-        flops=10**8,
-        moved=2 * 10**6,
-        out_spec=hbm,
-    )(*arrays)
+def plain(body, in_specs, outs, arrays, scratch=()):
+    specs = list(in_specs) + [vmem] * (len(arrays) - len(in_specs))
+    return call(body, specs, outs, scratch, flops=10**8, moved=2 * 10**6)(*arrays)
 
 
 def token_rows(block, wide):
@@ -179,10 +149,8 @@
     x_block = token_rows(x_ref[section], wide)
     x_rows[...] = x_block
     gain = jnp.where(lower, own_gain[...], got_gain[...])
-    out[:, :16, :] = chunked(dot(pick0[...], normalized(x_block, gain)))
-    grad = token_rows(grad_ref[section], wide)
-    grad_rows[...] = grad
-    out[:, 16:, :] = chunked(dot(high1[...], grad) + dot(low1[...], grad))
+    out[...] = chunked(dot(pick0[...], normalized(x_block, gain)))
+    grad_rows[...] = token_rows(grad_ref[section], wide)
 
 
 def flip_body(*refs):
@@ -279,21 +247,18 @@
         lower, upper = (), ()
         others = [far(0), far(1), far(2)]
 
-    @pl.when(section == 0)
-    def _():
-        groups = near(own if layer == 0 else swapped, lower)
-        for n in order:
-            for copy in groups[n]:
+    for n in order:
+
+        @pl.when(section == 0)
+        def _(n=n):
+            for copy in near(own if layer == 0 else swapped, lower)[n]:
                 copy.start()
 
-    @pl.when(section != 0)
-    def _():
-        groups = near(swapped if layer == 0 else own, upper)
-        for n in order:
-            for copy in groups[n]:
+        @pl.when(section != 0)
+        def _(n=n):
+            for copy in near(swapped if layer == 0 else own, upper)[n]:
                 copy.start()
 
-    for n in order:
         for copy in others[n]:
             copy.start()
     return [first + second for first, second in zip(near(own, lower), others)]
@@ -316,7 +281,7 @@
     outs = refs[14:19]
     w_gate, w_up, w_down, wide, rows = refs[19:24]
     early, early_far, gate_out, up_out, arrived, result, sems, more = refs[24:]
-    load = begin(arrived_ref.at[:, 0:16, :], arrived, more.at[4])
+    load = begin(arrived_ref, arrived, more.at[4])
     waits = fetch(place_ref, 0, sources, (w_gate, w_up, w_down), sems)
     load.wait()
     to_matrix(arrived[...].reshape(1024, 128).astype(f32), wide, rows)
@@ -353,23 +318,23 @@
 
 
 def second_body(*refs):
-    place_ref, arrived, cot_ref, early0_ref, early0_far_ref = refs[0:5]
-    sources = refs[5:15]
-    ends = refs[15:18]
-    outs = refs[18:24]
-    w_gate, w_up, w_down, wide, rows, grads, early, early_far = refs[24:32]
-    cot, early0, early0_far, late, late_far, picked, result, gain_out, sems, more = refs[32:]
+    place_ref, arrived_ref, early0_ref, early0_far_ref = refs[0:4]
+    sources = refs[4:14]
+    ends = refs[14:17]
+    outs = refs[17:23]
+    w_gate, w_up, w_down, wide, rows, grads, early, early_far = refs[23:31]
+    arrived, early0, early0_far, late, late_far, picked, result, gain_out, sems, more = refs[31:]
+    load = begin(arrived_ref, arrived, more.at[0])
     waits = fetch(place_ref, 1, sources, (w_gate, w_up, w_down), sems)
     loads = [
-        begin(cot_ref.at[:, 16:32, :], cot, more.at[0]),
         begin(early0_ref, early0, more.at[1]),
         begin(early0_far_ref, early0_far, more.at[2]),
     ]
-    normed_rows = arrived[...].reshape(1024, 128)
+    load.wait()
+    normed_rows = arrived[:, :16, :].reshape(1024, 128)
     to_matrix(normed_rows.astype(f32), wide, rows)
     halves(place_ref, rows, early, early_far)
-    finish(loads)
-    to_matrix(cot[...].reshape(1024, 128).astype(f32), wide, grads)
+    to_matrix(arrived[:, 16:, :].reshape(1024, 128).astype(f32), wide, grads)
     halves(place_ref, grads, late, late_far)
     finish(waits[0])
     pre_gate = dot(rows[...], w_gate[...])
@@ -378,6 +343,8 @@
     acts = gated(pre_gate, pre_up).astype(bf16)
     early[:, 512:] = acts
     early_far[:, 512:] = acts
+
+    finish(loads)
 
     def moves(order):
         return [
@@ -421,12 +388,9 @@
     w_gate, w_up, w_down, wide, grads = refs[21:26]
     arrived, normed, pre_gate, pre_up, late, late_far, picked, sems, more = refs[26:]
     load = begin(arrived_ref.at[:, 0:16, :], arrived, more.at[0])
+    loads = [begin(gate_ref, pre_gate, more.at[1]), begin(up_ref, pre_up, more.at[2])]
     waits = fetch(place_ref, 0, sources, (w_gate, w_up, w_down), sems, (2, 0, 1))
-    loads = [
-        begin(gate_ref, pre_gate, more.at[1]),
-        begin(up_ref, pre_up, more.at[2]),
-        begin(normed_ref.at[:, 0:16, :], normed, more.at[3]),
-    ]
+    loads.append(begin(normed_ref, normed, more.at[3]))
     load.wait()
     to_matrix(arrived[...].reshape(1024, 128).astype(f32), wide, grads)
     halves(place_ref, grads, late, late_far)
@@ -453,11 +417,17 @@
     return dot(high_t[...], rows) + dot(low_t[...], rows)
 
 
-def between_body(returned, x_ref, gain_ref, high_t, low_t, pick, hidden, out):
+def cotangent_body(grad_ref, high, low, out):
+    grad = grad_ref[...]
+    out[...] = chunked(dot(high[...], grad) + dot(low[...], grad))
+
+
+def between_body(returned, x_ref, gain_ref, high_t, low_t, pick, cot, hidden, out):
     rows = returned[...].reshape(1024, 128)
     result = (x_ref[...].astype(f32) + combined(high_t, low_t, rows)).astype(bf16)
     hidden[...] = result
-    out[...] = chunked(dot(pick[...], normalized(result, gain_ref[...])))
+    out[:, :16, :] = chunked(dot(pick[...], normalized(result, gain_ref[...])))
+    out[:, 16:, :] = cot[...]
 
 
 def input_gradient(rows, upstream, x_block, gain, pick_t):
@@ -627,15 +597,15 @@
     plain_room = pltpu.VMEM((128, 768), f32)
     arrival = pltpu.VMEM((64, 16, 128), bf16)
 
-    out_first, x_first, grad_last, *maps = staged(
+    out_first, x_first, grad_last, *maps = plain(
         start_body,
         [smem] + [vmem] * 8,
-        [big, block, block] + [down] * 6,
+        [small, block, block] + [down] * 6,
         [place, own_routes, got_routes, own_gates, got_gates]
         + [activations, cotangent, own_gain, got_gain],
         [narrow],
     )
-    _, high0, low0, pick1, _, _ = maps
+    _, high0, low0, pick1, high1, low1 = maps
     first_gain = jnp.where(section == 0, own_gain, got_gain)
     second_gain = jnp.where(section == 0, got_gain, own_gain)
 
@@ -665,6 +635,7 @@
 
     flipped = call(flip_body, [vmem] * 6, [across] * 6, flops=10**6, moved=3 * 10**6)(*maps)
     pick0_t, high0_t, low0_t, pick1_t, high1_t, low1_t = flipped
+    cot = plain(cotangent_body, [], [small], [grad_last, high1, low1])[0]
 
     portions1 = [
         away(after(w, other))
@@ -685,32 +656,33 @@
     )(place, arrived_first, *own, *swapped, *portions0)
     returned = exchange(result)
 
-    hidden_first, out_second = staged(
+    hidden_first, out_second = plain(
         between_body,
         [vmem],
-        [block, small],
-        [returned, x_first, second_gain, high0_t, low0_t, pick1],
+        [block, big],
+        [returned, x_first, second_gain, high0_t, low0_t, pick1, cot],
     )
     arrived_second = exchange(out_second)
 
     picked, result_second, gain_second, kept, sent, straight, cross, late1, late1_far = call(
         second_body,
-        [smem, vmem] + [hbm] * 13,
+        [smem] + [hbm] * 13,
         [small, small, ((8, 128), f32)] + [early_shape] * 4 + [late_shape] * 2,
         weight_scratch
         + [wide, matrix, matrix, early_room, early_room]
-        + [arrival, early_room, early_room, late_room, late_room, arrival, arrival]
+        + [pltpu.VMEM((64, 32, 128), bf16), early_room, early_room]
+        + [late_room, late_room, arrival, arrival]
         + [pltpu.VMEM((8, 128), f32), sems, pltpu.SemaphoreType.DMA((12,))],
         flops=12 * 10**8,
         moved=8 * 10**6,
         out_spec=hbm,
-    )(place, arrived_second, arrived_first, early0, early0_far, *own, *swapped, *portions1)
+    )(place, arrived_second, early0, early0_far, *own, *swapped, *portions1)
     returned = exchange(picked)
 
     early_parts = (kept, beside(sent), away(straight), away(cross, cross=True))
     late1_parts = (late1, beside(late1, [(0, 1)]), away(late1_far, 1), away(late1_far, 1, True))
 
-    grad_middle, out_third = staged(
+    grad_middle, out_third = plain(
         turn_body,
         [vmem],
         [block, big],

time: 226 us -> 245 us (1.084)
  waiting for transfers between devices: 58.1 us -> 83.7 us
  starting transfers between devices: 86.8 us -> 75.5 us
  blocking collectives: 18.1 us -> 23 us
    ppermute x13, waiting for transfers between devices: 18.9 us -> 50.5 us  [away(): return lax.ppermute(block, every, pairs(layer, cross))]
    all_to_all x5, starting transfers between devices: 45.3 us -> 38 us  [exchange(): lax.all_to_all(block, 'expert', split_axis=0, concat_axis=0, tiled=True)]
    all_to_all x5, waiting for transfers between devices: 35.4 us -> 29.3 us  [exchange(): lax.all_to_all(block, 'expert', split_axis=0, concat_axis=0, tiled=True)]
    all_to_all x1, blocking collectives: 18.1 us -> 23 us  [exchange(): lax.all_to_all(block, 'expert', split_axis=0, concat_axis=0, tiled=True)]
    pallas_call x4 -> x5, Pallas kernels: 17.9 us -> 17.3 us  [the longest x4 10.1 us: plain(): call(body, specs, outs, scratch, flops=10 ** 8, moved=2 * 10 ** 6)(*arrays)]
  transfers between devices with their start and end apart: 34 -> 34, of which waited for: 12 -> 13; matrix products, arithmetic and copies ran while one was open for 1% -> 1% of each run, Pallas kernels for 14% -> 13%
where the time goes in v4:
time: 245 us; the launch traced here: 242 us
  waiting for transfers between devices  83.7 us (34%)
  starting transfers between devices  75.5 us (31%)
  Pallas kernels  42.8 us (17%)
  blocking collectives  23 us (9%)
  local copies, waits for them, and re-layouts  15 us (6%)
    ppermute x13, waiting for transfers between devices, away(): return lax.ppermute(block, every, pairs(layer, cross))  50.5 us
    all_to_all x5, starting transfers between devices, exchange(): lax.all_to_all(block, 'expert', split_axis=0, concat_axis=0, tiled=True)  38 us
    all_to_all x5, waiting for transfers between devices, exchange(): lax.all_to_all(block, 'expert', split_axis=0, concat_axis=0, tiled=True)  29.3 us
    ppermute x13, starting transfers between devices, away(): return lax.ppermute(block, every, pairs(layer, cross))  27.2 us
    all_to_all x1, blocking collectives, exchange(): lax.all_to_all(block, 'expert', split_axis=0, concat_axis=0, tiled=True)  23 us
    unnamed x74, local copies, waits for them, and re-layouts  15 us
    ppermute x16, starting transfers between devices, beside(): return lax.ppermute(block, 'section', route)  10.3 us
    pallas_call x4, Pallas kernels, plain(): call(body, specs, outs, scratch, flops=10 ** 8, moved=2 * 10 ** 6)(*arrays)  10.1 us
  transfers between devices with their start and end apart: 34, of which 13 were waited for; matrix products, arithmetic and copies ran while one was open for 1% of the time, Pallas kernels for 13%

profile of v4, /device:TPU:4, one launch (start us, length us, event | category | flops | bytes accessed | tf_op | source)
XLA Modules:
  0.0 242.3 jit_solution(6991961802205165706)
XLA Ops:
  0.7 4.1 %collective-permute-start.6 = (bf16[512,768]{1,0:T(8,128)(2,1)}, bf16[512,768]{1,0:T(8,128)(2,1)S(1)}, u32[]{:S(2)}, u32[]{:S(2)}) collective-permute-start(bf16[512,768]{1,0:T(8,128)(2,1)} %bitcast.22), channel_id=1, source_target_pairs={{0,1},{1,0},{2,3},{3,2},{4,5},{5,4},{6,7},{7,6},{8,9},{9,8},{10,11... | collective-permute-start | bytes 2359304 | tf_op jit(solution)/shard_map/ppermute | solution.py:565
  4.9 3.2 %collective-permute-start.10 = (bf16[768,512]{1,0:T(8,128)(2,1)}, bf16[768,512]{1,0:T(8,128)(2,1)}, u32[]{:S(2)}, u32[]{:S(2)}) collective-permute-start(bf16[768,512]{1,0:T(8,128)(2,1)} %bitcast.33), channel_id=1, source_target_pairs={{0,1},{1,0},{2,3},{3,2},{4,5},{5,4},{6,7},{7,6},{8,9},{9,8},{10,11... | collective-permute-start | bytes 2359304 | tf_op jit(solution)/shard_map/ppermute | solution.py:565
  8.1 1.6 collective-permute-start.8
  10.2 1.0 collective-permute-done.refs_2_
  11.6 1.0 collective-permute-done.1.refs_4_
  13.1 10.1 %collective-permute-done.6.refs_8_.refs_12_ = bf16[512,768]{1,0:T(8,128)(2,1)S(1)} collective-permute-done((bf16[512,768]{1,0:T(8,128)(2,1)}, bf16[512,768]{1,0:T(8,128)(2,1)S(1)}, u32[]{:S(2)}, u32[]{:S(2)}) %collective-permute-start.6) | collective-permute-done | bytes 786464 | tf_op jit(solution)/shard_map/ppermute | solution.py:565
  23.2 2.2 collective-permute-start.7
  25.4 7.9 %collective-permute-done.10.refs_12_.refs_16_ = bf16[768,512]{1,0:T(8,128)(2,1)} collective-permute-done((bf16[768,512]{1,0:T(8,128)(2,1)}, bf16[768,512]{1,0:T(8,128)(2,1)}, u32[]{:S(2)}, u32[]{:S(2)}) %collective-permute-start.10) | collective-permute-done | bytes 786464 | tf_op jit(solution)/shard_map/ppermute | solution.py:565
  33.3 2.2 collective-permute-start.11
  35.5 1.3 collective-permute-start.9
  37.4 2.6 %shard_map.127 = (bf16[64,16,128]{2,1,0:T(8,128)(2,1)}, bf16[128,128]{1,0:T(8,128)(2,1)}, bf16[128,128]{1,0:T(8,128)(2,1)}, bf16[1024,128]{1,0:T(8,128)(2,1)}, b...) custom-call(s32[2]{0:T(128)} %pad_add_fusion.refs_0_.place_ref, ...), custom_call_target="tpu_custom_call" | custom-call | flops 100000000 | bytes 2000000 | tf_op jit(solution)/shard_map/pallas_call | solution.py:56
  40.1 12.8 %all-to-all-start = ((bf16[64,16,128]{2,1,0:T(8,128)(2,1)}), bf16[64,16,128]{2,1,0:T(8,128)(2,1)S(1)}, u32[]{:S(2)}, u32[]{:S(2)}) async-start(bf16[64,16,128]{2,1,0:T(8,128)(2,1)} %get-tuple-element.56), calls=%async_computation | async-start | bytes 524288 | tf_op jit(solution)/shard_map/all_to_all | solution.py:568
  54.6 3.0 %shard_map.132 = (bf16[512,768]{1,0:T(8,128)(2,1)}, bf16[384,512]{1,0:T(8,128)(2,1)}) custom-call(s32[2]{0:T(128)} %pad_add_fusion.refs_0_.place_ref, bf16[512,768]{1,0:T(8,128)(2,1)} %bitcast.24, bf16[512,768]{1,0:T(8,128)(2,1)} %bitcast.29, bf16[768,512]{1,0:T(8,128)(2,1)} %bitcast.35, bf16[512,768]{1,0:T(8,128)(2,1)} %copy-done.20, ...), custom_call_target="tpu_custom_call" | custom-call | flops 1 | bytes 2500000 | tf_op jit(solution)/shard_map/pallas_call | solution.py:614
  58.5 6.4 %all-to-all-done.refs_1_.refs_3_ = bf16[64,16,128]{2,1,0:T(8,128)(2,1)S(1)} async-done(((bf16[64,16,128]{2,1,0:T(8,128)(2,1)}), bf16[64,16,128]{2,1,0:T(8,128)(2,1)S(1)}, u32[]{:S(2)}, u32[]{:S(2)}) %all-to-all-start) | async-done | bytes 262176 | tf_op jit(solution)/shard_map/all_to_all | solution.py:568
  65.7 4.3 %shard_map.128 = (bf16[64,16,128]{2,1,0:T(8,128)(2,1)}, bf16[128,1280]{1,0:T(8,128)(2,1)}, bf16[128,1280]{1,0:T(8,128)(2,1)}, f32[128,768]{1,0:T(8,128)}, f32[128,768]{1,0:T(8,128)}) custom-call(s32[2]{0:T(128)} %pad_add_fusion.refs_0_.place_ref, bf16[64,16,128]{2,1,0:T(8,128)(2,1)} %copy-done.23, bf16[512,768]{1,0:T(8,128)(2,1)} %bitcast.25, ...), custom_call_target="tpu_custom_call" | custom-call | flops 600000000 | bytes 6000000 | tf_op jit(solution)/shard_map/pallas_call | solution.py:646
  70.0 7.1 %all-to-all-start.1 = ((bf16[64,16,128]{2,1,0:T(8,128)(2,1)}), bf16[64,16,128]{2,1,0:T(8,128)(2,1)S(1)}, u32[]{:S(2)}, u32[]{:S(2)}) async-start(bf16[64,16,128]{2,1,0:T(8,128)(2,1)} %get-tuple-element.57), calls=%async_computation.1 | async-start | bytes 524288 | tf_op jit(solution)/shard_map/all_to_all | solution.py:568
  77.2 2.7 %shard_map.129 = (bf16[128,1024]{1,0:T(8,128)(2,1)}, bf16[128,1024]{1,0:T(8,128)(2,1)}, bf16[128,1024]{1,0:T(8,128)(2,1)}, bf16[128,1024]{1,0:T(8,128)(2,1)}, bf...) custom-call(bf16[1024,128]{1,0:T(8,128)(2,1)} %get-tuple-element.59.refs_0_, ...), custom_call_target="tpu_custom_call" | custom-call | flops 1000000 | bytes 3000000 | tf_op jit(solution)/shard_map/pallas_call | solution.py:636
  79.8 2.1 shard_map.130.cot
  82.5 7.0 %all-to-all-done.1.returned = bf16[64,16,128]{2,1,0:T(8,128)(2,1)S(1)} async-done(((bf16[64,16,128]{2,1,0:T(8,128)(2,1)}), bf16[64,16,128]{2,1,0:T(8,128)(2,1)S(1)}, u32[]{:S(2)}, u32[]{:S(2)}) %all-to-all-start.1) | async-done | bytes 262176 | tf_op jit(solution)/shard_map/all_to_all | solution.py:568
  90.2 2.7 %shard_map.131 = (bf16[128,128]{1,0:T(8,128)(2,1)}, bf16[64,32,128]{2,1,0:T(8,128)(2,1)}) custom-call(bf16[64,16,128]{2,1,0:T(8,128)(2,1)} %copy-done.25, bf16[128,128]{1,0:T(8,128)(2,1)} %get-tuple-element.58.x_ref.refs_2_, f32[8,128]{1,0:T(8,128)} %get-tuple-element.107.gain_ref, bf16[128,1024]{1,0:T(8,128)(2,1)} %get-tuple-element.65.high_t, ...), custom_call_target="tpu_custom_call" | custom-call | flops 100000000 | bytes 2000000 | tf_op jit(solution)/shard_map/pallas_call | solution.py:56
  92.9 6.0 %all-to-all-start.2 = ((bf16[64,32,128]{2,1,0:T(8,128)(2,1)}), bf16[64,32,128]{2,1,0:T(8,128)(2,1)S(1)}, u32[]{:S(2)}, u32[]{:S(2)}) async-start(bf16[64,32,128]{2,1,0:T(8,128)(2,1)} %get-tuple-element.69), calls=%async_computation.2 | async-start | bytes 1048576 | tf_op jit(solution)/shard_map/all_to_all | solution.py:568
  99.8 15.3 %collective-permute-done.14.refs_12_ = bf16[384,512]{1,0:T(8,128)(2,1)S(1)} collective-permute-done((bf16[384,512]{1,0:T(8,128)(2,1)S(1)}, bf16[384,512]{1,0:T(8,128)(2,1)S(1)}, u32[]{:S(2)}, u32[]{:S(2)}) %collective-permute-start.14) | collective-permute-done | bytes 393248 | tf_op jit(solution)/shard_map/ppermute | solution.py:565
  115.2 1.7 collective-permute-done.15.refs_13_
  118.1 7.2 %shard_map.133 = (bf16[64,16,128]{2,1,0:T(8,128)(2,1)}, bf16[64,16,128]{2,1,0:T(8,128)(2,1)}, f32[8,128]{1,0:T(8,128)}, bf16[128,1280]{1,0:T(8,128)(2,1)}, bf16[...) custom-call(s32[2]{0:T(128)} %pad_add_fusion.refs_0_.place_ref, ...), custom_call_target="tpu_custom_call" | custom-call | flops 1200000000 | bytes 8000000 | tf_op jit(solution)/shard_map/pallas_call | solution.py:667
  125.4 23.0 %all_to_all.30.returned = bf16[64,16,128]{2,1,0:T(8,128)(2,1)} all-to-all(bf16[64,16,128]{2,1,0:T(8,128)(2,1)} %get-tuple-element.76), channel_id=1, replica_groups=mesh['section'=2,'expert'=64,'dp'=2] {'expert'}, dimensions={0} | all-to-all | bytes 524288 | tf_op jit(solution)/shard_map/all_to_all | solution.py:568
  148.4 2.7 %shard_map.134 = (bf16[128,128]{1,0:T(8,128)(2,1)}, bf16[64,32,128]{2,1,0:T(8,128)(2,1)}) custom-call(bf16[64,16,128]{2,1,0:T(8,128)(2,1)} %all_to_all.30.returned, bf16[64,16,128]{2,1,0:T(8,128)(2,1)} %get-tuple-element.77.result, bf16[128,128]{1,0:T(8,128)(2,1)} %get-tuple-element.68.x_ref.first, bf16[128,128]{1,0:T(8,128)(2,1)} %get-tuple-element.67.grad_ref, ...), custom_call_target="tpu_custom_call" | custom-call | flops 100000000 | bytes 2000000 | tf_op jit(solution)/shard_map/pallas_call | solution.py:56
  151.1 6.0 %all-to-all-start.4 = ((bf16[64,32,128]{2,1,0:T(8,128)(2,1)}), bf16[64,32,128]{2,1,0:T(8,128)(2,1)S(1)}, u32[]{:S(2)}, u32[]{:S(2)}) async-start(bf16[64,32,128]{2,1,0:T(8,128)(2,1)} %get-tuple-element.79), calls=%async_computation.4 | async-start | bytes 1048576 | tf_op jit(solution)/shard_map/all_to_all | solution.py:568
  157.1 1.3 collective-permute-start.26
  158.4 15.9 %all-to-all-done.4.arrived.refs_2_ = bf16[64,32,128]{2,1,0:T(8,128)(2,1)S(1)} async-done(((bf16[64,32,128]{2,1,0:T(8,128)(2,1)}), bf16[64,32,128]{2,1,0:T(8,128)(2,1)S(1)}, u32[]{:S(2)}, u32[]{:S(2)}) %all-to-all-start.4) | async-done | bytes 524320 | tf_op jit(solution)/shard_map/all_to_all | solution.py:568
  175.2 6.3 %shard_map.137 = (bf16[64,32,128]{2,1,0:T(8,128)(2,1)}, bf16[128,2048]{1,0:T(8,128)(2,1)}, bf16[128,2048]{1,0:T(8,128)(2,1)}) custom-call(s32[2]{0:T(128)} %pad_add_fusion.refs_0_.place_ref, f32[8,128]{1,0:T(8,128)} %get-tuple-element.84.refs_1_, bf16[64,32,128]{2,1,0:T(8,128)(2,1)} %copy-done, bf16[64,16,128]{2,1,0:T(8,128)(2,1)} %copy-done.23, ...), custom_call_target="tpu_custom_call" | custom-call | flops 600000000 | bytes 8000000 | tf_op jit(solution)/shard_map/pallas_call | solution.py:693
  181.5 6.1 %all-to-all-start.5 = ((bf16[64,32,128]{2,1,0:T(8,128)(2,1)}), bf16[64,32,128]{2,1,0:T(8,128)(2,1)S(1)}, u32[]{:S(2)}, u32[]{:S(2)}) async-start(bf16[64,32,128]{2,1,0:T(8,128)(2,1)} %get-tuple-element.87), calls=%async_computation.5 | async-start | bytes 1048576 | tf_op jit(solution)/shard_map/all_to_all | solution.py:568
  187.7 1.5 collective-permute-start.21
  189.2 1.8 collective-permute-start.22
  191.1 1.0 copy-done.1
  196.0 3.1 %collective-permute-start.28 = (bf16[128,2048]{1,0:T(8,128)(2,1)}, bf16[128,2048]{1,0:T(8,128)(2,1)S(1)}, u32[]{:S(2)}, u32[]{:S(2)}) collective-permute-start(bf16[128,2048]{1,0:T(8,128)(2,1)} %get-tuple-element.102), channel_id=1, source_target_pairs={{0,129},{1,128},{2,131},{3,130},{4,133},{5,132},{6,135},{7,134},{8... | collective-permute-start | bytes 1572872 | tf_op jit(solution)/shard_map/ppermute | solution.py:565
  199.1 4.4 %collective-permute-done.21.refs_3_ = bf16[128,1280]{1,0:T(8,128)(2,1)S(1)} collective-permute-done((bf16[128,1280]{1,0:T(8,128)(2,1)S(1)}, bf16[128,1280]{1,0:T(8,128)(2,1)S(1)}, u32[]{:S(2)}, u32[]{:S(2)}) %collective-permute-start.21) | collective-permute-done | bytes 327712 | tf_op jit(solution)/shard_map/ppermute | solution.py:565
  205.0 5.1 %collective-permute-done.22.refs_4_ = bf16[128,1280]{1,0:T(8,128)(2,1)S(1)} collective-permute-done((bf16[128,1280]{1,0:T(8,128)(2,1)}, bf16[128,1280]{1,0:T(8,128)(2,1)S(1)}, u32[]{:S(2)}, u32[]{:S(2)}) %collective-permute-start.22) | collective-permute-done | bytes 327712 | tf_op jit(solution)/shard_map/ppermute | solution.py:565
  210.8 1.3 collective-permute-start.23
  212.1 1.3 collective-permute-start.25
  213.4 3.8 %collective-permute-start.24 = (bf16[128,2048]{1,0:T(8,128)(2,1)}, bf16[128,2048]{1,0:T(8,128)(2,1)}, u32[]{:S(2)}, u32[]{:S(2)}) collective-permute-start(bf16[128,2048]{1,0:T(8,128)(2,1)} %get-tuple-element.100), channel_id=1, source_target_pairs={{0,1},{1,0},{2,3},{3,2},{4,5},{5,4},{6,7},{7,6},{8,9},{9,8},{10,11... | collective-permute-start | bytes 1572872 | tf_op jit(solution)/shard_map/ppermute | solution.py:565
  217.3 1.2 shard_map.136
  220.2 1.0 shard_map.138
  221.2 2.4 collective-permute-start.19
  223.6 1.9 collective-permute-start.18
  225.5 7.2 %collective-permute-done.25.refs_8_ = bf16[128,2048]{1,0:T(8,128)(2,1)} collective-permute-done((bf16[128,2048]{1,0:T(8,128)(2,1)}, bf16[128,2048]{1,0:T(8,128)(2,1)}, u32[]{:S(2)}, u32[]{:S(2)}) %collective-permute-start.25) | collective-permute-done | bytes 524320 | tf_op jit(solution)/shard_map/ppermute | solution.py:565
  233.1 1.0 copy-done.6
  236.1 4.9 %shard_map.140 = (f32[512,768]{1,0:T(8,128)}, f32[512,768]{1,0:T(8,128)}, f32[768,512]{1,0:T(8,128)}) custom-call(s32[2]{0:T(128)S(1)} %copy-done.17, bf16[128,1280]{1,0:T(8,128)(2,1)S(1)} %copy-done.4, bf16[128,1280]{1,0:T(8,128)(2,1)S(1)} %copy-done.6, bf16[128,1280]{1,0:T(8,128)(2,1)S(1)} %copy-done.8, bf16[128,1280]{1,0:T(8,128)(2,1)S(1)} %copy-done.10, ...), custom_call_target="tpu_custom_call" | custom-call | flops 1200000000 | bytes 8000000 | tf_op jit(solution)/shard_map/pallas_call | solution.py:725
  241.0 1.2 shard_map.139
  (111 shorter events, 20.1 us)
Async XLA Ops:
  0.6 7.5 %collective-permute-start.4 = (bf16[512,768]{1,0:T(8,128)(2,1)}, bf16[512,768]{1,0:T(8,128)(2,1)S(1)}, u32[]{:S(2)}, u32[]{:S(2)}) collective-permute-start(bf16[512,768]{1,0:T(8,128)(2,1)} %bitcast.28), channel_id=1, source_target_pairs={{0,128},{128,0},{1,129},{129,1},{2,130},{130,2},{3,131},{131,3},{4... | collective-permute-start | bytes 2359304 | tf_op jit(solution)/shard_map/ppermute | solution.py:562
  0.7 22.5 %collective-permute-start.6 = (bf16[512,768]{1,0:T(8,128)(2,1)}, bf16[512,768]{1,0:T(8,128)(2,1)S(1)}, u32[]{:S(2)}, u32[]{:S(2)}) collective-permute-start(bf16[512,768]{1,0:T(8,128)(2,1)} %bitcast.22), channel_id=1, source_target_pairs={{0,1},{1,0},{2,3},{3,2},{4,5},{5,4},{6,7},{7,6},{8,9},{9,8},{10,11... | collective-permute-start | bytes 2359304 | tf_op jit(solution)/shard_map/ppermute | solution.py:565
  4.9 28.4 %collective-permute-start.10 = (bf16[768,512]{1,0:T(8,128)(2,1)}, bf16[768,512]{1,0:T(8,128)(2,1)}, u32[]{:S(2)}, u32[]{:S(2)}) collective-permute-start(bf16[768,512]{1,0:T(8,128)(2,1)} %bitcast.33), channel_id=1, source_target_pairs={{0,1},{1,0},{2,3},{3,2},{4,5},{5,4},{6,7},{7,6},{8,9},{9,8},{10,11... | collective-permute-start | bytes 2359304 | tf_op jit(solution)/shard_map/ppermute | solution.py:565
  8.1 44.8 %copy-start.19 = (bf16[512,768]{1,0:T(8,128)(2,1)}, bf16[512,768]{1,0:T(8,128)(2,1)S(1)}, u32[]{:S(2)}) copy-start(bf16[512,768]{1,0:T(8,128)(2,1)S(1)} %collective-permute-done.4.refs_6_.refs_5_.refs_8_.refs_10_) | copy-start | bytes 2359300
  8.1 27.4 %collective-permute-start.8 = (bf16[512,768]{1,0:T(8,128)(2,1)S(1)}, bf16[512,768]{1,0:T(8,128)(2,1)}, u32[]{:S(2)}, u32[]{:S(2)}) collective-permute-start(bf16[512,768]{1,0:T(8,128)(2,1)S(1)} %collective-permute-done.4.refs_6_.refs_5_.refs_8_.refs_10_), channel_id=1, source_target_pairs={{128,129},{129,128},{130,131},{131,130},{132,133},{133,132},{134,1... | collective-permute-start | bytes 2359304 | tf_op jit(solution)/shard_map/ppermute | solution.py:565
  9.7 3.3 %collective-permute-start.2 = (f32[8,128]{1,0:T(8,128)}, f32[8,128]{1,0:T(8,128)S(1)}, u32[]{:S(2)}, u32[]{:S(2)}) collective-permute-start(f32[8,128]{1,0:T(8,128)} %bitcast.18), channel_id=1, source_target_pairs={{0,128},{128,0},{1,129},{129,1},{2,130},{130,2},{3,131},{131,3},{4... | collective-permute-start | bytes 12296 | tf_op jit(solution)/shard_map/ppermute | solution.py:562
  9.7 1.5 collective-permute-start
  11.2 26.2 %copy-start.35 = (s32[6,2,16]{2,1,0:T(2,128)}, s32[6,2,16]{2,1,0:T(2,128)S(1)}, u32[]{:S(2)}) copy-start(s32[6,2,16]{2,1,0:T(2,128)S(1)} %collective-permute-done.refs_2_) | copy-start | bytes 2308
  11.2 1.4 collective-permute-start.1
  12.6 24.8 %copy-start.36 = (f32[6,2,16]{2,1,0:T(2,128)}, f32[6,2,16]{2,1,0:T(2,128)S(1)}, u32[]{:S(2)}) copy-start(f32[6,2,16]{2,1,0:T(2,128)S(1)} %collective-permute-done.1.refs_4_) | copy-start | bytes 2308
  12.6 40.2 %collective-permute-start.3 = (bf16[512,768]{1,0:T(8,128)(2,1)}, bf16[512,768]{1,0:T(8,128)(2,1)S(1)}, u32[]{:S(2)}, u32[]{:S(2)}) collective-permute-start(bf16[512,768]{1,0:T(8,128)(2,1)} %bitcast.23), channel_id=1, source_target_pairs={{0,128},{128,0},{1,129},{129,1},{2,130},{130,2},{3,131},{131,3},{4... | collective-permute-start | bytes 2359304 | tf_op jit(solution)/shard_map/ppermute | solution.py:562
  13.0 24.5 %copy-start.30 = (f32[8,128]{1,0:T(8,128)}, f32[8,128]{1,0:T(8,128)S(1)}, u32[]{:S(2)}) copy-start(f32[8,128]{1,0:T(8,128)S(1)} %collective-permute-done.2.refs_8_) | copy-start | bytes 12292
  13.0 39.9 %collective-permute-start.5 = (bf16[768,512]{1,0:T(8,128)(2,1)}, bf16[768,512]{1,0:T(8,128)(2,1)S(1)}, u32[]{:S(2)}, u32[]{:S(2)}) collective-permute-start(bf16[768,512]{1,0:T(8,128)(2,1)} %bitcast.34), channel_id=1, source_target_pairs={{0,128},{128,0},{1,129},{129,1},{2,130},{130,2},{3,131},{131,3},{4... | collective-permute-start | bytes 2359304 | tf_op jit(solution)/shard_map/ppermute | solution.py:562
  23.2 41.8 %copy-start.22 = (bf16[512,768]{1,0:T(8,128)(2,1)}, bf16[512,768]{1,0:T(8,128)(2,1)S(1)}, u32[]{:S(2)}) copy-start(bf16[512,768]{1,0:T(8,128)(2,1)S(1)} %collective-permute-done.6.refs_8_.refs_12_) | copy-start | bytes 2359300
  23.2 41.7 %collective-permute-start.7 = (bf16[512,768]{1,0:T(8,128)(2,1)S(1)}, bf16[512,768]{1,0:T(8,128)(2,1)}, u32[]{:S(2)}, u32[]{:S(2)}) collective-permute-start(bf16[512,768]{1,0:T(8,128)(2,1)S(1)} %collective-permute-done.6.refs_8_.refs_12_), channel_id=1, source_target_pairs={{0,128},{1,129},{2,130},{3,131},{4,132},{5,133},{6,134},{7,135},{8... | collective-permute-start | bytes 2359304 | tf_op jit(solution)/shard_map/ppermute | solution.py:562
  33.3 31.7 %collective-permute-start.11 = (bf16[768,512]{1,0:T(8,128)(2,1)}, bf16[768,512]{1,0:T(8,128)(2,1)}, u32[]{:S(2)}, u32[]{:S(2)}) collective-permute-start(bf16[768,512]{1,0:T(8,128)(2,1)} %collective-permute-done.10.refs_12_.refs_16_), channel_id=1, source_target_pairs={{0,128},{1,129},{2,130},{3,131},{4,132},{5,133},{6,134},{7,135},{8... | collective-permute-start | bytes 2359304 | tf_op jit(solution)/shard_map/ppermute | solution.py:562
  35.5 29.4 %collective-permute-start.9 = (bf16[512,768]{1,0:T(8,128)(2,1)}, bf16[512,768]{1,0:T(8,128)(2,1)}, u32[]{:S(2)}, u32[]{:S(2)}) collective-permute-start(bf16[512,768]{1,0:T(8,128)(2,1)} %collective-permute-done.8.refs_10_.refs_14_), channel_id=1, source_target_pairs={{128,0},{129,1},{130,2},{131,3},{132,4},{133,5},{134,6},{135,7},{1... | collective-permute-start | bytes 2359304 | tf_op jit(solution)/shard_map/ppermute | solution.py:562
  40.1 24.8 %all-to-all-start = ((bf16[64,16,128]{2,1,0:T(8,128)(2,1)}), bf16[64,16,128]{2,1,0:T(8,128)(2,1)S(1)}, u32[]{:S(2)}, u32[]{:S(2)}) async-start(bf16[64,16,128]{2,1,0:T(8,128)(2,1)} %get-tuple-element.56), calls=%async_computation | async-start | bytes 524288 | tf_op jit(solution)/shard_map/all_to_all | solution.py:568
  57.6 42.2 %collective-permute-start.12 = (bf16[512,768]{1,0:T(8,128)(2,1)}, bf16[512,768]{1,0:T(8,128)(2,1)S(1)}, u32[]{:S(2)}, u32[]{:S(2)}) collective-permute-start(bf16[512,768]{1,0:T(8,128)(2,1)} %get-tuple-element.73), channel_id=1, source_target_pairs={{0,1},{1,0},{2,3},{3,2},{4,5},{5,4},{6,7},{7,6},{8,9},{9,8},{10,11... | collective-permute-start | bytes 2359304 | tf_op jit(solution)/shard_map/ppermute | solution.py:565
  70.0 19.5 %all-to-all-start.1 = ((bf16[64,16,128]{2,1,0:T(8,128)(2,1)}), bf16[64,16,128]{2,1,0:T(8,128)(2,1)S(1)}, u32[]{:S(2)}, u32[]{:S(2)}) async-start(bf16[64,16,128]{2,1,0:T(8,128)(2,1)} %get-tuple-element.57), calls=%async_computation.1 | async-start | bytes 524288 | tf_op jit(solution)/shard_map/all_to_all | solution.py:568
  79.8 19.1 %copy-start.32 = (bf16[384,512]{1,0:T(8,128)(2,1)S(1)}, bf16[384,512]{1,0:T(8,128)(2,1)}, u32[]{:S(2)}) copy-start(bf16[384,512]{1,0:T(8,128)(2,1)} %get-tuple-element.75) | copy-start | bytes 1179652
  92.9 24.0 %all-to-all-start.2 = ((bf16[64,32,128]{2,1,0:T(8,128)(2,1)}), bf16[64,32,128]{2,1,0:T(8,128)(2,1)S(1)}, u32[]{:S(2)}, u32[]{:S(2)}) async-start(bf16[64,32,128]{2,1,0:T(8,128)(2,1)} %get-tuple-element.69), calls=%async_computation.2 | async-start | bytes 1048576 | tf_op jit(solution)/shard_map/all_to_all | solution.py:568
  98.9 16.3 %collective-permute-start.14 = (bf16[384,512]{1,0:T(8,128)(2,1)S(1)}, bf16[384,512]{1,0:T(8,128)(2,1)S(1)}, u32[]{:S(2)}, u32[]{:S(2)}) collective-permute-start(bf16[384,512]{1,0:T(8,128)(2,1)S(1)} %copy-done.32), channel_id=1, source_target_pairs={{0,1},{1,0},{2,3},{3,2},{4,5},{5,4},{6,7},{7,6},{8,9},{9,8},{10,11... | collective-permute-start | bytes 1179656 | tf_op jit(solution)/shard_map/ppermute | solution.py:565
  99.8 17.1 %copy-start.26 = (bf16[512,768]{1,0:T(8,128)(2,1)}, bf16[512,768]{1,0:T(8,128)(2,1)S(1)}, u32[]{:S(2)}) copy-start(bf16[512,768]{1,0:T(8,128)(2,1)S(1)} %collective-permute-done.12.refs_10_) | copy-start | bytes 2359300
  99.8 17.1 %collective-permute-start.13 = (bf16[512,768]{1,0:T(8,128)(2,1)S(1)}, bf16[512,768]{1,0:T(8,128)(2,1)S(1)}, u32[]{:S(2)}, u32[]{:S(2)}) collective-permute-start(bf16[512,768]{1,0:T(8,128)(2,1)S(1)} %collective-permute-done.12.refs_10_), channel_id=1, source_target_pairs={{0,128},{128,0},{1,129},{129,1},{2,130},{130,2},{3,131},{131,3},{4... | collective-permute-start | bytes 2359304 | tf_op jit(solution)/shard_map/ppermute | solution.py:562
  115.2 1.7 collective-permute-start.15
  125.4 31.7 %copy-start.2 = (bf16[128,2048]{1,0:T(8,128)(2,1)S(1)}, bf16[128,2048]{1,0:T(8,128)(2,1)}, u32[]{:S(2)}) copy-start(bf16[128,2048]{1,0:T(8,128)(2,1)} %get-tuple-element.101.refs_9_) | copy-start | bytes 1572868
  151.1 23.2 %all-to-all-start.4 = ((bf16[64,32,128]{2,1,0:T(8,128)(2,1)}), bf16[64,32,128]{2,1,0:T(8,128)(2,1)S(1)}, u32[]{:S(2)}, u32[]{:S(2)}) async-start(bf16[64,32,128]{2,1,0:T(8,128)(2,1)} %get-tuple-element.79), calls=%async_computation.4 | async-start | bytes 1048576 | tf_op jit(solution)/shard_map/all_to_all | solution.py:568
  157.1 55.0 %collective-permute-start.26 = (bf16[128,2048]{1,0:T(8,128)(2,1)S(1)}, bf16[128,2048]{1,0:T(8,128)(2,1)S(1)}, u32[]{:S(2)}, u32[]{:S(2)}) collective-permute-start(bf16[128,2048]{1,0:T(8,128)(2,1)S(1)} %copy-done.2), channel_id=1, source_target_pairs={{0,128},{1,129},{2,130},{3,131},{4,132},{5,133},{6,134},{7,135},{8... | collective-permute-start | bytes 1572872 | tf_op jit(solution)/shard_map/ppermute | solution.py:562
  175.2 12.5 %copy-start.33 = (bf16[128,1280]{1,0:T(8,128)(2,1)S(1)}, bf16[128,1280]{1,0:T(8,128)(2,1)}, u32[]{:S(2)}) copy-start(bf16[128,1280]{1,0:T(8,128)(2,1)} %get-tuple-element.97) | copy-start | bytes 983044
  175.2 15.9 %copy-start.11 = (bf16[128,128]{1,0:T(8,128)(2,1)S(1)}, bf16[128,128]{1,0:T(8,128)(2,1)}, u32[]{:S(2)}) copy-start(bf16[128,128]{1,0:T(8,128)(2,1)} %get-tuple-element.68.x_ref.first) | copy-start | bytes 98308
  175.2 15.9 %copy-start.17 = (s32[2]{0:T(128)S(1)}, s32[2]{0:T(128)}, u32[]{:S(2)}) copy-start(s32[2]{0:T(128)} %pad_add_fusion.refs_0_.place_ref) | copy-start | bytes 28
  181.4 29.4 %copy-start.3 = (bf16[128,2048]{1,0:T(8,128)(2,1)S(1)}, bf16[128,2048]{1,0:T(8,128)(2,1)}, u32[]{:S(2)}) copy-start(bf16[128,2048]{1,0:T(8,128)(2,1)} %get-tuple-element.99.refs_5_) | copy-start | bytes 1572868
  181.4 37.0 %copy-start.15 = (bf16[128,128]{1,0:T(8,128)(2,1)S(1)}, bf16[128,128]{1,0:T(8,128)(2,1)}, u32[]{:S(2)}) copy-start(bf16[128,128]{1,0:T(8,128)(2,1)} %get-tuple-element.88.refs_3_.refs_2_) | copy-start | bytes 98308
  181.5 51.7 %copy-start.4 = (bf16[128,1280]{1,0:T(8,128)(2,1)S(1)}, bf16[128,1280]{1,0:T(8,128)(2,1)}, u32[]{:S(2)}) copy-start(bf16[128,1280]{1,0:T(8,128)(2,1)} %get-tuple-element.95.refs_1_) | copy-start | bytes 983044
  181.5 37.0 %all-to-all-start.5 = ((bf16[64,32,128]{2,1,0:T(8,128)(2,1)}), bf16[64,32,128]{2,1,0:T(8,128)(2,1)S(1)}, u32[]{:S(2)}, u32[]{:S(2)}) async-start(bf16[64,32,128]{2,1,0:T(8,128)(2,1)} %get-tuple-element.87), calls=%async_computation.5 | async-start | bytes 1048576 | tf_op jit(solution)/shard_map/all_to_all | solution.py:568
  187.6 7.7 %collective-permute-start.20 = (bf16[128,1280]{1,0:T(8,128)(2,1)S(1)}, bf16[128,1280]{1,0:T(8,128)(2,1)S(1)}, u32[]{:S(2)}, u32[]{:S(2)}) collective-permute-start(bf16[128,1280]{1,0:T(8,128)(2,1)S(1)} %copy-done.34), channel_id=1, source_target_pairs={{0,128},{128,0},{1,129},{129,1},{2,130},{130,2},{3,131},{131,3},{4... | collective-permute-start | bytes 983048 | tf_op jit(solution)/shard_map/ppermute | solution.py:562
  187.7 15.8 %collective-permute-start.21 = (bf16[128,1280]{1,0:T(8,128)(2,1)S(1)}, bf16[128,1280]{1,0:T(8,128)(2,1)S(1)}, u32[]{:S(2)}, u32[]{:S(2)}) collective-permute-start(bf16[128,1280]{1,0:T(8,128)(2,1)S(1)} %copy-done.33), channel_id=1, source_target_pairs={{0,1},{1,0},{2,3},{3,2},{4,5},{5,4},{6,7},{7,6},{8,9},{9,8},{10,11... | collective-permute-start | bytes 983048 | tf_op jit(solution)/shard_map/ppermute | solution.py:565
  189.2 20.9 %collective-permute-start.22 = (bf16[128,1280]{1,0:T(8,128)(2,1)}, bf16[128,1280]{1,0:T(8,128)(2,1)S(1)}, u32[]{:S(2)}, u32[]{:S(2)}) collective-permute-start(bf16[128,1280]{1,0:T(8,128)(2,1)} %get-tuple-element.98), channel_id=1, source_target_pairs={{0,129},{1,128},{2,131},{3,130},{4,133},{5,132},{6,135},{7,134},{8... | collective-permute-start | bytes 983048 | tf_op jit(solution)/shard_map/ppermute | solution.py:565
  194.8 18.6 %collective-permute-start.16 = (bf16[128,128]{1,0:T(8,128)(2,1)S(1)}, bf16[128,128]{1,0:T(8,128)(2,1)S(1)}, u32[]{:S(2)}, u32[]{:S(2)}) collective-permute-start(bf16[128,128]{1,0:T(8,128)(2,1)S(1)} %get-tuple-element.83), channel_id=1, source_target_pairs={{0,128},{128,0},{1,129},{129,1},{2,130},{130,2},{3,131},{131,3},{4... | collective-permute-start | bytes 98312 | tf_op jit(solution)/shard_map/ppermute | solution.py:562
  196.0 25.2 %collective-permute-start.28 = (bf16[128,2048]{1,0:T(8,128)(2,1)}, bf16[128,2048]{1,0:T(8,128)(2,1)S(1)}, u32[]{:S(2)}, u32[]{:S(2)}) collective-permute-start(bf16[128,2048]{1,0:T(8,128)(2,1)} %get-tuple-element.102), channel_id=1, source_target_pairs={{0,129},{1,128},{2,131},{3,130},{4,133},{5,132},{6,135},{7,134},{8... | collective-permute-start | bytes 1572872 | tf_op jit(solution)/shard_map/ppermute | solution.py:565
  204.3 19.3 %collective-permute-start.27 = (bf16[128,2048]{1,0:T(8,128)(2,1)}, bf16[128,2048]{1,0:T(8,128)(2,1)S(1)}, u32[]{:S(2)}, u32[]{:S(2)}) collective-permute-start(bf16[128,2048]{1,0:T(8,128)(2,1)} %get-tuple-element.102), channel_id=1, source_target_pairs={{128,129},{129,128},{130,131},{131,130},{132,133},{133,132},{134,1... | collective-permute-start | bytes 1572872 | tf_op jit(solution)/shard_map/ppermute | solution.py:565
  210.8 14.7 %collective-permute-start.23 = (bf16[128,2048]{1,0:T(8,128)(2,1)S(1)}, bf16[128,2048]{1,0:T(8,128)(2,1)}, u32[]{:S(2)}, u32[]{:S(2)}) collective-permute-start(bf16[128,2048]{1,0:T(8,128)(2,1)S(1)} %copy-done.3), channel_id=1, source_target_pairs={{128,0},{129,1},{130,2},{131,3},{132,4},{133,5},{134,6},{135,7},{1... | collective-permute-start | bytes 1572872 | tf_op jit(solution)/shard_map/ppermute | solution.py:562
  212.1 20.5 %collective-permute-start.25 = (bf16[128,2048]{1,0:T(8,128)(2,1)}, bf16[128,2048]{1,0:T(8,128)(2,1)}, u32[]{:S(2)}, u32[]{:S(2)}) collective-permute-start(bf16[128,2048]{1,0:T(8,128)(2,1)} %get-tuple-element.100), channel_id=1, source_target_pairs={{128,1},{129,0},{130,3},{131,2},{132,5},{133,4},{134,7},{135,6},{1... | collective-permute-start | bytes 1572872 | tf_op jit(solution)/shard_map/ppermute | solution.py:565
  213.4 19.7 %collective-permute-start.24 = (bf16[128,2048]{1,0:T(8,128)(2,1)}, bf16[128,2048]{1,0:T(8,128)(2,1)}, u32[]{:S(2)}, u32[]{:S(2)}) collective-permute-start(bf16[128,2048]{1,0:T(8,128)(2,1)} %get-tuple-element.100), channel_id=1, source_target_pairs={{0,1},{1,0},{2,3},{3,2},{4,5},{5,4},{6,7},{7,6},{8,9},{9,8},{10,11... | collective-permute-start | bytes 1572872 | tf_op jit(solution)/shard_map/ppermute | solution.py:565
  221.2 19.8 %collective-permute-start.19 = (f32[16,128]{1,0:T(8,128)S(1)}, f32[16,128]{1,0:T(8,128)S(1)}, u32[]{:S(2)}, u32[]{:S(2)}) collective-permute-start(f32[16,128]{1,0:T(8,128)S(1)} %get-tuple-element.92.refs_4_), channel_id=1, source_target_pairs={{0,129},{1,128},{2,131},{3,130},{4,133},{5,132},{6,135},{7,134},{8... | collective-permute-start | bytes 24584 | tf_op jit(solution)/shard_map/ppermute | solution.py:565
  223.6 17.4 %collective-permute-start.18 = (f32[16,128]{1,0:T(8,128)S(1)}, f32[16,128]{1,0:T(8,128)S(1)}, u32[]{:S(2)}, u32[]{:S(2)}) collective-permute-start(f32[16,128]{1,0:T(8,128)S(1)} %get-tuple-element.92.refs_4_), channel_id=1, source_target_pairs={{0,1},{1,0},{2,3},{3,2},{4,5},{5,4},{6,7},{7,6},{8,9},{9,8},{10,11... | collective-permute-start | bytes 24584 | tf_op jit(solution)/shard_map/ppermute | solution.py:565
  225.5 15.5 %collective-permute-start.17 = (f32[144,128]{1,0:T(8,128)S(1)}, f32[144,128]{1,0:T(8,128)S(1)}, u32[]{:S(2)}, u32[]{:S(2)}) collective-permute-start(f32[144,128]{1,0:T(8,128)S(1)} %get-tuple-element.91), channel_id=1, source_target_pairs={{0,128},{128,0},{1,129},{129,1},{2,130},{130,2},{3,131},{131,3},{4... | collective-permute-start | bytes 221192 | tf_op jit(solution)/shard_map/ppermute | solution.py:562
  (23 other events, 54.8 us)

commit v5 on v4

--- a/solution.py
+++ b/solution.py
@@ -149,8 +149,10 @@
     x_block = token_rows(x_ref[section], wide)
     x_rows[...] = x_block
     gain = jnp.where(lower, own_gain[...], got_gain[...])
-    out[...] = chunked(dot(pick0[...], normalized(x_block, gain)))
-    grad_rows[...] = token_rows(grad_ref[section], wide)
+    out[:, :16, :] = chunked(dot(pick0[...], normalized(x_block, gain)))
+    grad = token_rows(grad_ref[section], wide)
+    grad_rows[...] = grad
+    out[:, 16:, :] = chunked(dot(high1[...], grad) + dot(low1[...], grad))
 
 
 def flip_body(*refs):
@@ -281,7 +283,7 @@
     outs = refs[14:19]
     w_gate, w_up, w_down, wide, rows = refs[19:24]
     early, early_far, gate_out, up_out, arrived, result, sems, more = refs[24:]
-    load = begin(arrived_ref, arrived, more.at[4])
+    load = begin(arrived_ref.at[:, 0:16, :], arrived, more.at[4])
     waits = fetch(place_ref, 0, sources, (w_gate, w_up, w_down), sems)
     load.wait()
     to_matrix(arrived[...].reshape(1024, 128).astype(f32), wide, rows)
@@ -318,23 +320,26 @@
 
 
 def second_body(*refs):
-    place_ref, arrived_ref, early0_ref, early0_far_ref = refs[0:4]
-    sources = refs[4:14]
-    ends = refs[14:17]
-    outs = refs[17:23]
-    w_gate, w_up, w_down, wide, rows, grads, early, early_far = refs[23:31]
-    arrived, early0, early0_far, late, late_far, picked, result, gain_out, sems, more = refs[31:]
+    place_ref, arrived_ref, cot_ref, early0_ref, early0_far_ref = refs[0:5]
+    sources = refs[5:15]
+    ends = refs[15:18]
+    outs = refs[18:24]
+    w_gate, w_up, w_down, wide, rows, grads, early, early_far = refs[24:32]
+    arrived, cot, early0, early0_far, late, late_far = refs[32:38]
+    picked, result, gain_out, sems, more = refs[38:]
     load = begin(arrived_ref, arrived, more.at[0])
+    load_cot = begin(cot_ref.at[:, 16:32, :], cot, more.at[12])
     waits = fetch(place_ref, 1, sources, (w_gate, w_up, w_down), sems)
     loads = [
         begin(early0_ref, early0, more.at[1]),
         begin(early0_far_ref, early0_far, more.at[2]),
     ]
     load.wait()
-    normed_rows = arrived[:, :16, :].reshape(1024, 128)
+    normed_rows = arrived[...].reshape(1024, 128)
     to_matrix(normed_rows.astype(f32), wide, rows)
     halves(place_ref, rows, early, early_far)
-    to_matrix(arrived[:, 16:, :].reshape(1024, 128).astype(f32), wide, grads)
+    load_cot.wait()
+    to_matrix(cot[...].reshape(1024, 128).astype(f32), wide, grads)
     halves(place_ref, grads, late, late_far)
     finish(waits[0])
     pre_gate = dot(rows[...], w_gate[...])
@@ -390,7 +395,7 @@
     load = begin(arrived_ref.at[:, 0:16, :], arrived, more.at[0])
     loads = [begin(gate_ref, pre_gate, more.at[1]), begin(up_ref, pre_up, more.at[2])]
     waits = fetch(place_ref, 0, sources, (w_gate, w_up, w_down), sems, (2, 0, 1))
-    loads.append(begin(normed_ref, normed, more.at[3]))
+    loads.append(begin(normed_ref.at[:, 0:16, :], normed, more.at[3]))
     load.wait()
     to_matrix(arrived[...].reshape(1024, 128).astype(f32), wide, grads)
     halves(place_ref, grads, late, late_far)
@@ -417,17 +422,11 @@
     return dot(high_t[...], rows) + dot(low_t[...], rows)
 
 
-def cotangent_body(grad_ref, high, low, out):
-    grad = grad_ref[...]
-    out[...] = chunked(dot(high[...], grad) + dot(low[...], grad))
-
-
-def between_body(returned, x_ref, gain_ref, high_t, low_t, pick, cot, hidden, out):
+def between_body(returned, x_ref, gain_ref, high_t, low_t, pick, hidden, out):
     rows = returned[...].reshape(1024, 128)
     result = (x_ref[...].astype(f32) + combined(high_t, low_t, rows)).astype(bf16)
     hidden[...] = result
-    out[:, :16, :] = chunked(dot(pick[...], normalized(result, gain_ref[...])))
-    out[:, 16:, :] = cot[...]
+    out[...] = chunked(dot(pick[...], normalized(result, gain_ref[...])))
 
 
 def input_gradient(rows, upstream, x_block, gain, pick_t):
@@ -600,12 +599,12 @@
     out_first, x_first, grad_last, *maps = plain(
         start_body,
         [smem] + [vmem] * 8,
-        [small, block, block] + [down] * 6,
+        [big, block, block] + [down] * 6,
         [place, own_routes, got_routes, own_gates, got_gates]
         + [activations, cotangent, own_gain, got_gain],
         [narrow],
     )
-    _, high0, low0, pick1, high1, low1 = maps
+    _, high0, low0, pick1, _, _ = maps
     first_gain = jnp.where(section == 0, own_gain, got_gain)
     second_gain = jnp.where(section == 0, got_gain, own_gain)
 
@@ -635,7 +634,6 @@
 
     flipped = call(flip_body, [vmem] * 6, [across] * 6, flops=10**6, moved=3 * 10**6)(*maps)
     pick0_t, high0_t, low0_t, pick1_t, high1_t, low1_t = flipped
-    cot = plain(cotangent_body, [], [small], [grad_last, high1, low1])[0]
 
     portions1 = [
         away(after(w, other))
@@ -659,24 +657,24 @@
     hidden_first, out_second = plain(
         between_body,
         [vmem],
-        [block, big],
-        [returned, x_first, second_gain, high0_t, low0_t, pick1, cot],
+        [block, small],
+        [returned, x_first, second_gain, high0_t, low0_t, pick1],
     )
     arrived_second = exchange(out_second)
 
     picked, result_second, gain_second, kept, sent, straight, cross, late1, late1_far = call(
         second_body,
-        [smem] + [hbm] * 13,
+        [smem] + [hbm] * 14,
         [small, small, ((8, 128), f32)] + [early_shape] * 4 + [late_shape] * 2,
         weight_scratch
         + [wide, matrix, matrix, early_room, early_room]
-        + [pltpu.VMEM((64, 32, 128), bf16), early_room, early_room]
+        + [arrival, arrival, early_room, early_room]
         + [late_room, late_room, arrival, arrival]
-        + [pltpu.VMEM((8, 128), f32), sems, pltpu.SemaphoreType.DMA((12,))],
+        + [pltpu.VMEM((8, 128), f32), sems, pltpu.SemaphoreType.DMA((13,))],
         flops=12 * 10**8,
         moved=8 * 10**6,
         out_spec=hbm,
-    )(place, arrived_second, early0, early0_far, *own, *swapped, *portions1)
+    )(place, arrived_second, arrived_first, early0, early0_far, *own, *swapped, *portions1)
     returned = exchange(picked)
 
     early_parts = (kept, beside(sent), away(straight), away(cross, cross=True))

time: 245 us -> 224 us (0.914)
  waiting for transfers between devices: 83.7 us -> 57.8 us
  starting transfers between devices: 75.5 us -> 87.7 us
  blocking collectives: 23 us -> 18 us
    ppermute x13, waiting for transfers between devices: 50.5 us -> 19.3 us  [away(): return lax.ppermute(block, every, pairs(layer, cross))]
    all_to_all x5, starting transfers between devices: 38 us -> 46.1 us  [exchange(): lax.all_to_all(block, 'expert', split_axis=0, concat_axis=0, tiled=True)]
    all_to_all x5, waiting for transfers between devices: 29.3 us -> 34.6 us  [exchange(): lax.all_to_all(block, 'expert', split_axis=0, concat_axis=0, tiled=True)]
    all_to_all x1, blocking collectives: 23 us -> 18 us  [exchange(): lax.all_to_all(block, 'expert', split_axis=0, concat_axis=0, tiled=True)]
    pallas_call x4 -> x3, Pallas kernels: 10.1 us -> 7.91 us  [plain(): call(body, specs, outs, scratch, flops=10 ** 8, moved=2 * 10 ** 6)(*arrays)]
  transfers between devices with their start and end apart: 34 -> 34, of which waited for: 13 -> 12; matrix products, arithmetic and copies ran while one was open for 1% -> 1% of each run, Pallas kernels for 13% -> 13%
where the time goes in v5:
time: 224 us; the launch traced here: 221 us
  starting transfers between devices  87.7 us (39%)
  waiting for transfers between devices  57.8 us (26%)
  Pallas kernels  40.4 us (18%)
  blocking collectives  18 us (8%)
  local copies, waits for them, and re-layouts  14.6 us (7%)
    all_to_all x5, starting transfers between devices, exchange(): lax.all_to_all(block, 'expert', split_axis=0, concat_axis=0, tiled=True)  46.1 us
    all_to_all x5, waiting for transfers between devices, exchange(): lax.all_to_all(block, 'expert', split_axis=0, concat_axis=0, tiled=True)  34.6 us
    ppermute x13, starting transfers between devices, away(): return lax.ppermute(block, every, pairs(layer, cross))  29.2 us
    ppermute x13, waiting for transfers between devices, away(): return lax.ppermute(block, every, pairs(layer, cross))  19.3 us
    all_to_all x1, blocking collectives, exchange(): lax.all_to_all(block, 'expert', split_axis=0, concat_axis=0, tiled=True)  18 us
    unnamed x74, local copies, waits for them, and re-layouts  14.6 us
    ppermute x16, starting transfers between devices, beside(): return lax.ppermute(block, 'section', route)  12.4 us
    pallas_call x3, Pallas kernels, plain(): call(body, specs, outs, scratch, flops=10 ** 8, moved=2 * 10 ** 6)(*arrays)  7.91 us
  transfers between devices with their start and end apart: 34, of which 12 were waited for; matrix products, arithmetic and copies ran while one was open for 1% of the time, Pallas kernels for 13%

profile of v5, /device:TPU:4, one launch (start us, length us, event | category | flops | bytes accessed | tf_op | source)
XLA Modules:
  0.0 220.9 jit_solution(18001817519284637232)
XLA Ops:
  0.7 4.1 %collective-permute-start.6 = (bf16[512,768]{1,0:T(8,128)(2,1)}, bf16[512,768]{1,0:T(8,128)(2,1)}, u32[]{:S(2)}, u32[]{:S(2)}) collective-permute-start(bf16[512,768]{1,0:T(8,128)(2,1)} %bitcast.22), channel_id=1, source_target_pairs={{0,1},{1,0},{2,3},{3,2},{4,5},{5,4},{6,7},{7,6},{8,9},{9,8},{10,11... | collective-permute-start | bytes 2359304 | tf_op jit(solution)/shard_map/ppermute | solution.py:564
  4.9 3.2 %collective-permute-start.10 = (bf16[768,512]{1,0:T(8,128)(2,1)}, bf16[768,512]{1,0:T(8,128)(2,1)}, u32[]{:S(2)}, u32[]{:S(2)}) collective-permute-start(bf16[768,512]{1,0:T(8,128)(2,1)} %bitcast.33), channel_id=1, source_target_pairs={{0,1},{1,0},{2,3},{3,2},{4,5},{5,4},{6,7},{7,6},{8,9},{9,8},{10,11... | collective-permute-start | bytes 2359304 | tf_op jit(solution)/shard_map/ppermute | solution.py:564
  8.1 1.6 collective-permute-start.8
  10.2 1.0 collective-permute-done.refs_2_
  11.6 1.0 collective-permute-done.1.refs_4_
  13.8 2.7 %shard_map.127 = (bf16[64,32,128]{2,1,0:T(8,128)(2,1)}, bf16[128,128]{1,0:T(8,128)(2,1)}, bf16[128,128]{1,0:T(8,128)(2,1)}, bf16[1024,128]{1,0:T(8,128)(2,1)}, b...) custom-call(s32[2]{0:T(128)} %pad_add_fusion.refs_0_.place_ref, ...), custom_call_target="tpu_custom_call" | custom-call | flops 100000000 | bytes 2000000 | tf_op jit(solution)/shard_map/pallas_call | solution.py:56
  16.5 12.8 %all-to-all-start = ((bf16[64,32,128]{2,1,0:T(8,128)(2,1)}), bf16[64,32,128]{2,1,0:T(8,128)(2,1)S(1)}, u32[]{:S(2)}, u32[]{:S(2)}) async-start(bf16[64,32,128]{2,1,0:T(8,128)(2,1)} %get-tuple-element.56), calls=%async_computation | async-start | bytes 1048576 | tf_op jit(solution)/shard_map/all_to_all | solution.py:567
  29.2 2.9 %collective-permute-start.7 = (bf16[512,768]{1,0:T(8,128)(2,1)}, bf16[512,768]{1,0:T(8,128)(2,1)}, u32[]{:S(2)}, u32[]{:S(2)}) collective-permute-start(bf16[512,768]{1,0:T(8,128)(2,1)} %collective-permute-done.6.refs_8_.refs_12_), channel_id=1, source_target_pairs={{0,128},{1,129},{2,130},{3,131},{4,132},{5,133},{6,134},{7,135},{8... | collective-permute-start | bytes 2359304 | tf_op jit(solution)/shard_map/ppermute | solution.py:561
  32.1 2.2 collective-permute-done.10.refs_12_.refs_16_
  34.3 2.2 collective-permute-start.11
  36.5 1.3 collective-permute-start.9
  39.5 3.0 %shard_map.131 = (bf16[512,768]{1,0:T(8,128)(2,1)}, bf16[384,512]{1,0:T(8,128)(2,1)}) custom-call(s32[2]{0:T(128)} %pad_add_fusion.refs_0_.place_ref, bf16[512,768]{1,0:T(8,128)(2,1)} %bitcast.24, bf16[512,768]{1,0:T(8,128)(2,1)} %bitcast.29, bf16[768,512]{1,0:T(8,128)(2,1)} %bitcast.35, bf16[512,768]{1,0:T(8,128)(2,1)} %copy-done.21, ...), custom_call_target="tpu_custom_call" | custom-call | flops 1 | bytes 2500000 | tf_op jit(solution)/shard_map/pallas_call | solution.py:613
  42.5 2.1 collective-permute-start.12
  44.6 2.9 %all-to-all-done.refs_1_.refs_2_.refs_3_ = bf16[64,32,128]{2,1,0:T(8,128)(2,1)S(1)} async-done(((bf16[64,32,128]{2,1,0:T(8,128)(2,1)}), bf16[64,32,128]{2,1,0:T(8,128)(2,1)S(1)}, u32[]{:S(2)}, u32[]{:S(2)}) %all-to-all-start) | async-done | bytes 524320 | tf_op jit(solution)/shard_map/all_to_all | solution.py:567
  48.3 4.3 %shard_map.128 = (bf16[64,16,128]{2,1,0:T(8,128)(2,1)}, bf16[128,1280]{1,0:T(8,128)(2,1)}, bf16[128,1280]{1,0:T(8,128)(2,1)}, f32[128,768]{1,0:T(8,128)}, f32[128,768]{1,0:T(8,128)}) custom-call(s32[2]{0:T(128)} %pad_add_fusion.refs_0_.place_ref, bf16[64,32,128]{2,1,0:T(8,128)(2,1)} %copy-done.23, bf16[512,768]{1,0:T(8,128)(2,1)} %bitcast.25, ...), custom_call_target="tpu_custom_call" | custom-call | flops 600000000 | bytes 6000000 | tf_op jit(solution)/shard_map/pallas_call | solution.py:644
  52.6 11.4 %all-to-all-start.1 = ((bf16[64,16,128]{2,1,0:T(8,128)(2,1)}), bf16[64,16,128]{2,1,0:T(8,128)(2,1)S(1)}, u32[]{:S(2)}, u32[]{:S(2)}) async-start(bf16[64,16,128]{2,1,0:T(8,128)(2,1)} %get-tuple-element.57), calls=%async_computation.1 | async-start | bytes 524288 | tf_op jit(solution)/shard_map/all_to_all | solution.py:567
  64.0 2.7 %collective-permute-start.14 = (bf16[384,512]{1,0:T(8,128)(2,1)S(1)}, bf16[384,512]{1,0:T(8,128)(2,1)S(1)}, u32[]{:S(2)}, u32[]{:S(2)}) collective-permute-start(bf16[384,512]{1,0:T(8,128)(2,1)S(1)} %copy-done.32), channel_id=1, source_target_pairs={{0,1},{1,0},{2,3},{3,2},{4,5},{5,4},{6,7},{7,6},{8,9},{9,8},{10,11... | collective-permute-start | bytes 1179656 | tf_op jit(solution)/shard_map/ppermute | solution.py:564
  66.8 1.1 collective-permute-start.13
  67.9 2.7 %shard_map.129 = (bf16[128,1024]{1,0:T(8,128)(2,1)}, bf16[128,1024]{1,0:T(8,128)(2,1)}, bf16[128,1024]{1,0:T(8,128)(2,1)}, bf16[128,1024]{1,0:T(8,128)(2,1)}, bf...) custom-call(bf16[1024,128]{1,0:T(8,128)(2,1)} %get-tuple-element.59.refs_0_, ...), custom_call_target="tpu_custom_call" | custom-call | flops 1000000 | bytes 3000000 | tf_op jit(solution)/shard_map/pallas_call | solution.py:635
  71.2 5.5 %all-to-all-done.1.returned = bf16[64,16,128]{2,1,0:T(8,128)(2,1)S(1)} async-done(((bf16[64,16,128]{2,1,0:T(8,128)(2,1)}), bf16[64,16,128]{2,1,0:T(8,128)(2,1)S(1)}, u32[]{:S(2)}, u32[]{:S(2)}) %all-to-all-start.1) | async-done | bytes 262176 | tf_op jit(solution)/shard_map/all_to_all | solution.py:567
  77.4 2.5 %shard_map.130 = (bf16[128,128]{1,0:T(8,128)(2,1)}, bf16[64,16,128]{2,1,0:T(8,128)(2,1)}) custom-call(bf16[64,16,128]{2,1,0:T(8,128)(2,1)} %copy-done.25, bf16[128,128]{1,0:T(8,128)(2,1)} %get-tuple-element.58.x_ref.refs_2_, f32[8,128]{1,0:T(8,128)} %get-tuple-element.107.gain_ref, bf16[128,1024]{1,0:T(8,128)(2,1)} %get-tuple-element.65.high_t, ...), custom_call_target="tpu_custom_call" | custom-call | flops 100000000 | bytes 2000000 | tf_op jit(solution)/shard_map/pallas_call | solution.py:56
  79.9 10.1 %all-to-all-start.2 = ((bf16[64,16,128]{2,1,0:T(8,128)(2,1)}), bf16[64,16,128]{2,1,0:T(8,128)(2,1)S(1)}, u32[]{:S(2)}, u32[]{:S(2)}) async-start(bf16[64,16,128]{2,1,0:T(8,128)(2,1)} %get-tuple-element.68), calls=%async_computation.2 | async-start | bytes 524288 | tf_op jit(solution)/shard_map/all_to_all | solution.py:567
  90.4 1.7 collective-permute-done.15.refs_14_
  92.1 10.5 %all-to-all-done.2.refs_1_ = bf16[64,16,128]{2,1,0:T(8,128)(2,1)S(1)} async-done(((bf16[64,16,128]{2,1,0:T(8,128)(2,1)}), bf16[64,16,128]{2,1,0:T(8,128)(2,1)S(1)}, u32[]{:S(2)}, u32[]{:S(2)}) %all-to-all-start.2) | async-done | bytes 262176 | tf_op jit(solution)/shard_map/all_to_all | solution.py:567
  103.4 7.0 %shard_map.132 = (bf16[64,16,128]{2,1,0:T(8,128)(2,1)}, bf16[64,16,128]{2,1,0:T(8,128)(2,1)}, f32[8,128]{1,0:T(8,128)}, bf16[128,1280]{1,0:T(8,128)(2,1)}, bf16[...) custom-call(s32[2]{0:T(128)} %pad_add_fusion.refs_0_.place_ref, ...), custom_call_target="tpu_custom_call" | custom-call | flops 1200000000 | bytes 8000000 | tf_op jit(solution)/shard_map/pallas_call | solution.py:665
  110.4 18.0 %all_to_all.30.returned = bf16[64,16,128]{2,1,0:T(8,128)(2,1)} all-to-all(bf16[64,16,128]{2,1,0:T(8,128)(2,1)} %get-tuple-element.75), channel_id=1, replica_groups=mesh['section'=2,'expert'=64,'dp'=2] {'expert'}, dimensions={0} | all-to-all | bytes 524288 | tf_op jit(solution)/shard_map/all_to_all | solution.py:567
  128.5 2.7 %shard_map.133 = (bf16[128,128]{1,0:T(8,128)(2,1)}, bf16[64,32,128]{2,1,0:T(8,128)(2,1)}) custom-call(bf16[64,16,128]{2,1,0:T(8,128)(2,1)} %all_to_all.30.returned, bf16[64,16,128]{2,1,0:T(8,128)(2,1)} %get-tuple-element.76.result, bf16[128,128]{1,0:T(8,128)(2,1)} %get-tuple-element.67.x_ref.first, bf16[128,128]{1,0:T(8,128)(2,1)} %get-tuple-element.77.grad_ref, ...), custom_call_target="tpu_custom_call" | custom-call | flops 100000000 | bytes 2000000 | tf_op jit(solution)/shard_map/pallas_call | solution.py:56
  131.2 5.7 %all-to-all-start.4 = ((bf16[64,32,128]{2,1,0:T(8,128)(2,1)}), bf16[64,32,128]{2,1,0:T(8,128)(2,1)S(1)}, u32[]{:S(2)}, u32[]{:S(2)}) async-start(bf16[64,32,128]{2,1,0:T(8,128)(2,1)} %get-tuple-element.79), calls=%async_computation.4 | async-start | bytes 1048576 | tf_op jit(solution)/shard_map/all_to_all | solution.py:567
  136.9 1.3 collective-permute-start.26
  138.2 15.7 %all-to-all-done.4.arrived.refs_2_ = bf16[64,32,128]{2,1,0:T(8,128)(2,1)S(1)} async-done(((bf16[64,32,128]{2,1,0:T(8,128)(2,1)}), bf16[64,32,128]{2,1,0:T(8,128)(2,1)S(1)}, u32[]{:S(2)}, u32[]{:S(2)}) %all-to-all-start.4) | async-done | bytes 524320 | tf_op jit(solution)/shard_map/all_to_all | solution.py:567
  154.8 6.3 %shard_map.136 = (bf16[64,32,128]{2,1,0:T(8,128)(2,1)}, bf16[128,2048]{1,0:T(8,128)(2,1)}, bf16[128,2048]{1,0:T(8,128)(2,1)}) custom-call(s32[2]{0:T(128)} %pad_add_fusion.refs_0_.place_ref, f32[8,128]{1,0:T(8,128)} %get-tuple-element.84.refs_1_, bf16[64,32,128]{2,1,0:T(8,128)(2,1)} %copy-done, bf16[64,32,128]{2,1,0:T(8,128)(2,1)} %copy-done.23, ...), custom_call_target="tpu_custom_call" | custom-call | flops 600000000 | bytes 8000000 | tf_op jit(solution)/shard_map/pallas_call | solution.py:691
  161.1 6.1 %all-to-all-start.5 = ((bf16[64,32,128]{2,1,0:T(8,128)(2,1)}), bf16[64,32,128]{2,1,0:T(8,128)(2,1)S(1)}, u32[]{:S(2)}, u32[]{:S(2)}) async-start(bf16[64,32,128]{2,1,0:T(8,128)(2,1)} %get-tuple-element.87), calls=%async_computation.5 | async-start | bytes 1048576 | tf_op jit(solution)/shard_map/all_to_all | solution.py:567
  167.4 3.2 %collective-permute-start.22 = (bf16[128,1280]{1,0:T(8,128)(2,1)}, bf16[128,1280]{1,0:T(8,128)(2,1)S(1)}, u32[]{:S(2)}, u32[]{:S(2)}) collective-permute-start(bf16[128,1280]{1,0:T(8,128)(2,1)} %get-tuple-element.98), channel_id=1, source_target_pairs={{0,129},{1,128},{2,131},{3,130},{4,133},{5,132},{6,135},{7,134},{8... | collective-permute-start | bytes 983048 | tf_op jit(solution)/shard_map/ppermute | solution.py:564
  170.7 1.0 copy-done.1
  175.6 1.9 collective-permute-start.28
  177.6 4.6 %collective-permute-done.21.refs_3_ = bf16[128,1280]{1,0:T(8,128)(2,1)S(1)} collective-permute-done((bf16[128,1280]{1,0:T(8,128)(2,1)S(1)}, bf16[128,1280]{1,0:T(8,128)(2,1)S(1)}, u32[]{:S(2)}, u32[]{:S(2)}) %collective-permute-start.21) | collective-permute-done | bytes 327712 | tf_op jit(solution)/shard_map/ppermute | solution.py:564
  183.6 5.3 %collective-permute-done.22.refs_4_ = bf16[128,1280]{1,0:T(8,128)(2,1)S(1)} collective-permute-done((bf16[128,1280]{1,0:T(8,128)(2,1)}, bf16[128,1280]{1,0:T(8,128)(2,1)S(1)}, u32[]{:S(2)}, u32[]{:S(2)}) %collective-permute-start.22) | collective-permute-done | bytes 327712 | tf_op jit(solution)/shard_map/ppermute | solution.py:564
  189.6 1.3 collective-permute-start.23
  190.9 1.3 collective-permute-start.25
  192.2 4.0 %collective-permute-start.24 = (bf16[128,2048]{1,0:T(8,128)(2,1)}, bf16[128,2048]{1,0:T(8,128)(2,1)}, u32[]{:S(2)}, u32[]{:S(2)}) collective-permute-start(bf16[128,2048]{1,0:T(8,128)(2,1)} %get-tuple-element.100), channel_id=1, source_target_pairs={{0,1},{1,0},{2,3},{3,2},{4,5},{5,4},{6,7},{7,6},{8,9},{9,8},{10,11... | collective-permute-start | bytes 1572872 | tf_op jit(solution)/shard_map/ppermute | solution.py:564
  196.2 1.2 shard_map.135
  199.1 1.0 shard_map.137
  200.2 2.3 %collective-permute-start.19 = (f32[16,128]{1,0:T(8,128)S(1)}, f32[16,128]{1,0:T(8,128)S(1)}, u32[]{:S(2)}, u32[]{:S(2)}) collective-permute-start(f32[16,128]{1,0:T(8,128)S(1)} %get-tuple-element.92.refs_4_), channel_id=1, source_target_pairs={{0,129},{1,128},{2,131},{3,130},{4,133},{5,132},{6,135},{7,134},{8... | collective-permute-start | bytes 24584 | tf_op jit(solution)/shard_map/ppermute | solution.py:564
  202.5 2.0 collective-permute-start.18
  204.4 7.0 %collective-permute-done.25.refs_8_ = bf16[128,2048]{1,0:T(8,128)(2,1)} collective-permute-done((bf16[128,2048]{1,0:T(8,128)(2,1)}, bf16[128,2048]{1,0:T(8,128)(2,1)}, u32[]{:S(2)}, u32[]{:S(2)}) %collective-permute-start.25) | collective-permute-done | bytes 524320 | tf_op jit(solution)/shard_map/ppermute | solution.py:564
  211.8 1.0 copy-done.6
  214.7 4.9 %shard_map.139 = (f32[512,768]{1,0:T(8,128)}, f32[512,768]{1,0:T(8,128)}, f32[768,512]{1,0:T(8,128)}) custom-call(s32[2]{0:T(128)S(1)} %copy-done.18, bf16[128,1280]{1,0:T(8,128)(2,1)S(1)} %copy-done.4, bf16[128,1280]{1,0:T(8,128)(2,1)S(1)} %copy-done.6, bf16[128,1280]{1,0:T(8,128)(2,1)S(1)} %copy-done.8, bf16[128,1280]{1,0:T(8,128)(2,1)S(1)} %copy-done.10, ...), custom_call_target="tpu_custom_call" | custom-call | flops 1200000000 | bytes 8000000 | tf_op jit(solution)/shard_map/pallas_call | solution.py:723
  219.7 1.2 shard_map.138
  (110 shorter events, 18.2 us)
Async XLA Ops:
  0.6 7.5 %collective-permute-start.4 = (bf16[512,768]{1,0:T(8,128)(2,1)}, bf16[512,768]{1,0:T(8,128)(2,1)S(1)}, u32[]{:S(2)}, u32[]{:S(2)}) collective-permute-start(bf16[512,768]{1,0:T(8,128)(2,1)} %bitcast.28), channel_id=1, source_target_pairs={{0,128},{128,0},{1,129},{129,1},{2,130},{130,2},{3,131},{131,3},{4... | collective-permute-start | bytes 2359304 | tf_op jit(solution)/shard_map/ppermute | solution.py:561
  0.7 28.5 %collective-permute-start.6 = (bf16[512,768]{1,0:T(8,128)(2,1)}, bf16[512,768]{1,0:T(8,128)(2,1)}, u32[]{:S(2)}, u32[]{:S(2)}) collective-permute-start(bf16[512,768]{1,0:T(8,128)(2,1)} %bitcast.22), channel_id=1, source_target_pairs={{0,1},{1,0},{2,3},{3,2},{4,5},{5,4},{6,7},{7,6},{8,9},{9,8},{10,11... | collective-permute-start | bytes 2359304 | tf_op jit(solution)/shard_map/ppermute | solution.py:564
  4.9 29.4 %collective-permute-start.10 = (bf16[768,512]{1,0:T(8,128)(2,1)}, bf16[768,512]{1,0:T(8,128)(2,1)}, u32[]{:S(2)}, u32[]{:S(2)}) collective-permute-start(bf16[768,512]{1,0:T(8,128)(2,1)} %bitcast.33), channel_id=1, source_target_pairs={{0,1},{1,0},{2,3},{3,2},{4,5},{5,4},{6,7},{7,6},{8,9},{9,8},{10,11... | collective-permute-start | bytes 2359304 | tf_op jit(solution)/shard_map/ppermute | solution.py:564
  8.1 29.7 %copy-start.20 = (bf16[512,768]{1,0:T(8,128)(2,1)}, bf16[512,768]{1,0:T(8,128)(2,1)S(1)}, u32[]{:S(2)}) copy-start(bf16[512,768]{1,0:T(8,128)(2,1)S(1)} %collective-permute-done.4.refs_6_.refs_5_.refs_9_.refs_10_) | copy-start | bytes 2359300
  8.1 28.3 %collective-permute-start.8 = (bf16[512,768]{1,0:T(8,128)(2,1)S(1)}, bf16[512,768]{1,0:T(8,128)(2,1)}, u32[]{:S(2)}, u32[]{:S(2)}) collective-permute-start(bf16[512,768]{1,0:T(8,128)(2,1)S(1)} %collective-permute-done.4.refs_6_.refs_5_.refs_9_.refs_10_), channel_id=1, source_target_pairs={{128,129},{129,128},{130,131},{131,130},{132,133},{133,132},{134,1... | collective-permute-start | bytes 2359304 | tf_op jit(solution)/shard_map/ppermute | solution.py:564
  9.7 3.3 %collective-permute-start.2 = (f32[8,128]{1,0:T(8,128)}, f32[8,128]{1,0:T(8,128)S(1)}, u32[]{:S(2)}, u32[]{:S(2)}) collective-permute-start(f32[8,128]{1,0:T(8,128)} %bitcast.18), channel_id=1, source_target_pairs={{0,128},{128,0},{1,129},{129,1},{2,130},{130,2},{3,131},{131,3},{4... | collective-permute-start | bytes 12296 | tf_op jit(solution)/shard_map/ppermute | solution.py:561
  9.7 1.5 collective-permute-start
  11.2 1.4 collective-permute-start.1
  12.6 25.2 %collective-permute-start.3 = (bf16[512,768]{1,0:T(8,128)(2,1)}, bf16[512,768]{1,0:T(8,128)(2,1)S(1)}, u32[]{:S(2)}, u32[]{:S(2)}) collective-permute-start(bf16[512,768]{1,0:T(8,128)(2,1)} %bitcast.23), channel_id=1, source_target_pairs={{0,128},{128,0},{1,129},{129,1},{2,130},{130,2},{3,131},{131,3},{4... | collective-permute-start | bytes 2359304 | tf_op jit(solution)/shard_map/ppermute | solution.py:561
  13.0 24.8 %collective-permute-start.5 = (bf16[768,512]{1,0:T(8,128)(2,1)}, bf16[768,512]{1,0:T(8,128)(2,1)S(1)}, u32[]{:S(2)}, u32[]{:S(2)}) collective-permute-start(bf16[768,512]{1,0:T(8,128)(2,1)} %bitcast.34), channel_id=1, source_target_pairs={{0,128},{128,0},{1,129},{129,1},{2,130},{130,2},{3,131},{131,3},{4... | collective-permute-start | bytes 2359304 | tf_op jit(solution)/shard_map/ppermute | solution.py:561
  16.5 31.0 %all-to-all-start = ((bf16[64,32,128]{2,1,0:T(8,128)(2,1)}), bf16[64,32,128]{2,1,0:T(8,128)(2,1)S(1)}, u32[]{:S(2)}, u32[]{:S(2)}) async-start(bf16[64,32,128]{2,1,0:T(8,128)(2,1)} %get-tuple-element.56), calls=%async_computation | async-start | bytes 1048576 | tf_op jit(solution)/shard_map/all_to_all | solution.py:567
  29.2 18.3 %collective-permute-start.7 = (bf16[512,768]{1,0:T(8,128)(2,1)}, bf16[512,768]{1,0:T(8,128)(2,1)}, u32[]{:S(2)}, u32[]{:S(2)}) collective-permute-start(bf16[512,768]{1,0:T(8,128)(2,1)} %collective-permute-done.6.refs_8_.refs_12_), channel_id=1, source_target_pairs={{0,128},{1,129},{2,130},{3,131},{4,132},{5,133},{6,134},{7,135},{8... | collective-permute-start | bytes 2359304 | tf_op jit(solution)/shard_map/ppermute | solution.py:561
  34.3 13.3 %collective-permute-start.11 = (bf16[768,512]{1,0:T(8,128)(2,1)}, bf16[768,512]{1,0:T(8,128)(2,1)}, u32[]{:S(2)}, u32[]{:S(2)}) collective-permute-start(bf16[768,512]{1,0:T(8,128)(2,1)} %collective-permute-done.10.refs_12_.refs_16_), channel_id=1, source_target_pairs={{0,128},{1,129},{2,130},{3,131},{4,132},{5,133},{6,134},{7,135},{8... | collective-permute-start | bytes 2359304 | tf_op jit(solution)/shard_map/ppermute | solution.py:561
  36.5 11.0 %collective-permute-start.9 = (bf16[512,768]{1,0:T(8,128)(2,1)}, bf16[512,768]{1,0:T(8,128)(2,1)}, u32[]{:S(2)}, u32[]{:S(2)}) collective-permute-start(bf16[512,768]{1,0:T(8,128)(2,1)} %collective-permute-done.8.refs_10_.refs_14_), channel_id=1, source_target_pairs={{128,0},{129,1},{130,2},{131,3},{132,4},{133,5},{134,6},{135,7},{1... | collective-permute-start | bytes 2359304 | tf_op jit(solution)/shard_map/ppermute | solution.py:561
  42.5 21.5 %copy-start.32 = (bf16[384,512]{1,0:T(8,128)(2,1)S(1)}, bf16[384,512]{1,0:T(8,128)(2,1)}, u32[]{:S(2)}) copy-start(bf16[384,512]{1,0:T(8,128)(2,1)} %get-tuple-element.74) | copy-start | bytes 1179652
  42.5 24.2 %collective-permute-start.12 = (bf16[512,768]{1,0:T(8,128)(2,1)}, bf16[512,768]{1,0:T(8,128)(2,1)S(1)}, u32[]{:S(2)}, u32[]{:S(2)}) collective-permute-start(bf16[512,768]{1,0:T(8,128)(2,1)} %get-tuple-element.72), channel_id=1, source_target_pairs={{0,1},{1,0},{2,3},{3,2},{4,5},{5,4},{6,7},{7,6},{8,9},{9,8},{10,11... | collective-permute-start | bytes 2359304 | tf_op jit(solution)/shard_map/ppermute | solution.py:564
  52.6 18.0 %copy-start.19 = (f32[1,1024]{1,0:T(1,128)S(1)}, f32[1,1024]{1,0:T(1,128)}, u32[]{:S(2)}) copy-start(f32[1,1024]{1,0:T(1,128)} %param.10) | copy-start | bytes 12292
  52.6 18.0 %copy-start.31 = (f32[8,128]{1,0:T(8,128)S(1)}, f32[8,128]{1,0:T(8,128)}, u32[]{:S(2)}) copy-start(f32[8,128]{1,0:T(8,128)} %copy-done.30) | copy-start | bytes 12292
  52.6 24.1 %all-to-all-start.1 = ((bf16[64,16,128]{2,1,0:T(8,128)(2,1)}), bf16[64,16,128]{2,1,0:T(8,128)(2,1)S(1)}, u32[]{:S(2)}, u32[]{:S(2)}) async-start(bf16[64,16,128]{2,1,0:T(8,128)(2,1)} %get-tuple-element.57), calls=%async_computation.1 | async-start | bytes 524288 | tf_op jit(solution)/shard_map/all_to_all | solution.py:567
  64.0 26.0 %collective-permute-start.14 = (bf16[384,512]{1,0:T(8,128)(2,1)S(1)}, bf16[384,512]{1,0:T(8,128)(2,1)S(1)}, u32[]{:S(2)}, u32[]{:S(2)}) collective-permute-start(bf16[384,512]{1,0:T(8,128)(2,1)S(1)} %copy-done.32), channel_id=1, source_target_pairs={{0,1},{1,0},{2,3},{3,2},{4,5},{5,4},{6,7},{7,6},{8,9},{9,8},{10,11... | collective-permute-start | bytes 1179656 | tf_op jit(solution)/shard_map/ppermute | solution.py:564
  66.8 13.1 %copy-start.26 = (bf16[512,768]{1,0:T(8,128)(2,1)}, bf16[512,768]{1,0:T(8,128)(2,1)S(1)}, u32[]{:S(2)}) copy-start(bf16[512,768]{1,0:T(8,128)(2,1)S(1)} %collective-permute-done.12.refs_11_) | copy-start | bytes 2359300
  66.8 25.3 %collective-permute-start.13 = (bf16[512,768]{1,0:T(8,128)(2,1)S(1)}, bf16[512,768]{1,0:T(8,128)(2,1)S(1)}, u32[]{:S(2)}, u32[]{:S(2)}) collective-permute-start(bf16[512,768]{1,0:T(8,128)(2,1)S(1)} %collective-permute-done.12.refs_11_), channel_id=1, source_target_pairs={{0,128},{128,0},{1,129},{129,1},{2,130},{130,2},{3,131},{131,3},{4... | collective-permute-start | bytes 2359304 | tf_op jit(solution)/shard_map/ppermute | solution.py:561
  79.9 22.7 %all-to-all-start.2 = ((bf16[64,16,128]{2,1,0:T(8,128)(2,1)}), bf16[64,16,128]{2,1,0:T(8,128)(2,1)S(1)}, u32[]{:S(2)}, u32[]{:S(2)}) async-start(bf16[64,16,128]{2,1,0:T(8,128)(2,1)} %get-tuple-element.68), calls=%async_computation.2 | async-start | bytes 524288 | tf_op jit(solution)/shard_map/all_to_all | solution.py:567
  90.1 12.5 %copy-start.28 = (bf16[384,512]{1,0:T(8,128)(2,1)}, bf16[384,512]{1,0:T(8,128)(2,1)S(1)}, u32[]{:S(2)}) copy-start(bf16[384,512]{1,0:T(8,128)(2,1)S(1)} %collective-permute-done.14.refs_13_) | copy-start | bytes 1179652
  90.1 2.0 collective-permute-start.15
  110.4 26.5 %copy-start.2 = (bf16[128,2048]{1,0:T(8,128)(2,1)S(1)}, bf16[128,2048]{1,0:T(8,128)(2,1)}, u32[]{:S(2)}) copy-start(bf16[128,2048]{1,0:T(8,128)(2,1)} %get-tuple-element.101.refs_9_) | copy-start | bytes 1572868
  131.2 22.7 %all-to-all-start.4 = ((bf16[64,32,128]{2,1,0:T(8,128)(2,1)}), bf16[64,32,128]{2,1,0:T(8,128)(2,1)S(1)}, u32[]{:S(2)}, u32[]{:S(2)}) async-start(bf16[64,32,128]{2,1,0:T(8,128)(2,1)} %get-tuple-element.79), calls=%async_computation.4 | async-start | bytes 1048576 | tf_op jit(solution)/shard_map/all_to_all | solution.py:567
  136.9 54.0 %collective-permute-start.26 = (bf16[128,2048]{1,0:T(8,128)(2,1)S(1)}, bf16[128,2048]{1,0:T(8,128)(2,1)S(1)}, u32[]{:S(2)}, u32[]{:S(2)}) collective-permute-start(bf16[128,2048]{1,0:T(8,128)(2,1)S(1)} %copy-done.2), channel_id=1, source_target_pairs={{0,128},{1,129},{2,130},{3,131},{4,132},{5,133},{6,134},{7,135},{8... | collective-permute-start | bytes 1572872 | tf_op jit(solution)/shard_map/ppermute | solution.py:561
  154.8 12.4 %copy-start.34 = (bf16[128,1280]{1,0:T(8,128)(2,1)S(1)}, bf16[128,1280]{1,0:T(8,128)(2,1)}, u32[]{:S(2)}) copy-start(bf16[128,1280]{1,0:T(8,128)(2,1)} %get-tuple-element.96) | copy-start | bytes 983044
  154.8 12.5 %copy-start.33 = (bf16[128,1280]{1,0:T(8,128)(2,1)S(1)}, bf16[128,1280]{1,0:T(8,128)(2,1)}, u32[]{:S(2)}) copy-start(bf16[128,1280]{1,0:T(8,128)(2,1)} %get-tuple-element.97) | copy-start | bytes 983044
  154.8 15.9 %copy-start.11 = (bf16[128,128]{1,0:T(8,128)(2,1)S(1)}, bf16[128,128]{1,0:T(8,128)(2,1)}, u32[]{:S(2)}) copy-start(bf16[128,128]{1,0:T(8,128)(2,1)} %get-tuple-element.67.x_ref.first) | copy-start | bytes 98308
  154.8 15.9 %copy-start.18 = (s32[2]{0:T(128)S(1)}, s32[2]{0:T(128)}, u32[]{:S(2)}) copy-start(s32[2]{0:T(128)} %pad_add_fusion.refs_0_.place_ref) | copy-start | bytes 28
  161.1 28.5 %copy-start.3 = (bf16[128,2048]{1,0:T(8,128)(2,1)S(1)}, bf16[128,2048]{1,0:T(8,128)(2,1)}, u32[]{:S(2)}) copy-start(bf16[128,2048]{1,0:T(8,128)(2,1)} %get-tuple-element.99.refs_5_) | copy-start | bytes 1572868
  161.1 36.4 %copy-start.15 = (bf16[128,128]{1,0:T(8,128)(2,1)S(1)}, bf16[128,128]{1,0:T(8,128)(2,1)}, u32[]{:S(2)}) copy-start(bf16[128,128]{1,0:T(8,128)(2,1)} %get-tuple-element.58.x_ref.refs_2_) | copy-start | bytes 98308
  161.1 50.7 %copy-start.4 = (bf16[128,1280]{1,0:T(8,128)(2,1)S(1)}, bf16[128,1280]{1,0:T(8,128)(2,1)}, u32[]{:S(2)}) copy-start(bf16[128,1280]{1,0:T(8,128)(2,1)} %get-tuple-element.95.refs_1_) | copy-start | bytes 983044
  161.1 36.3 %all-to-all-start.5 = ((bf16[64,32,128]{2,1,0:T(8,128)(2,1)}), bf16[64,32,128]{2,1,0:T(8,128)(2,1)S(1)}, u32[]{:S(2)}, u32[]{:S(2)}) async-start(bf16[64,32,128]{2,1,0:T(8,128)(2,1)} %get-tuple-element.87), calls=%async_computation.5 | async-start | bytes 1048576 | tf_op jit(solution)/shard_map/all_to_all | solution.py:567
  167.2 7.7 %collective-permute-start.20 = (bf16[128,1280]{1,0:T(8,128)(2,1)S(1)}, bf16[128,1280]{1,0:T(8,128)(2,1)S(1)}, u32[]{:S(2)}, u32[]{:S(2)}) collective-permute-start(bf16[128,1280]{1,0:T(8,128)(2,1)S(1)} %copy-done.34), channel_id=1, source_target_pairs={{0,128},{128,0},{1,129},{129,1},{2,130},{130,2},{3,131},{131,3},{4... | collective-permute-start | bytes 983048 | tf_op jit(solution)/shard_map/ppermute | solution.py:561
  167.3 14.9 %collective-permute-start.21 = (bf16[128,1280]{1,0:T(8,128)(2,1)S(1)}, bf16[128,1280]{1,0:T(8,128)(2,1)S(1)}, u32[]{:S(2)}, u32[]{:S(2)}) collective-permute-start(bf16[128,1280]{1,0:T(8,128)(2,1)S(1)} %copy-done.33), channel_id=1, source_target_pairs={{0,1},{1,0},{2,3},{3,2},{4,5},{5,4},{6,7},{7,6},{8,9},{9,8},{10,11... | collective-permute-start | bytes 983048 | tf_op jit(solution)/shard_map/ppermute | solution.py:564
  167.4 21.4 %collective-permute-start.22 = (bf16[128,1280]{1,0:T(8,128)(2,1)}, bf16[128,1280]{1,0:T(8,128)(2,1)S(1)}, u32[]{:S(2)}, u32[]{:S(2)}) collective-permute-start(bf16[128,1280]{1,0:T(8,128)(2,1)} %get-tuple-element.98), channel_id=1, source_target_pairs={{0,129},{1,128},{2,131},{3,130},{4,133},{5,132},{6,135},{7,134},{8... | collective-permute-start | bytes 983048 | tf_op jit(solution)/shard_map/ppermute | solution.py:564
  174.4 17.7 %collective-permute-start.16 = (bf16[128,128]{1,0:T(8,128)(2,1)S(1)}, bf16[128,128]{1,0:T(8,128)(2,1)S(1)}, u32[]{:S(2)}, u32[]{:S(2)}) collective-permute-start(bf16[128,128]{1,0:T(8,128)(2,1)S(1)} %get-tuple-element.83), channel_id=1, source_target_pairs={{0,128},{128,0},{1,129},{129,1},{2,130},{130,2},{3,131},{131,3},{4... | collective-permute-start | bytes 98312 | tf_op jit(solution)/shard_map/ppermute | solution.py:561
  175.6 24.5 %collective-permute-start.28 = (bf16[128,2048]{1,0:T(8,128)(2,1)}, bf16[128,2048]{1,0:T(8,128)(2,1)S(1)}, u32[]{:S(2)}, u32[]{:S(2)}) collective-permute-start(bf16[128,2048]{1,0:T(8,128)(2,1)} %get-tuple-element.102), channel_id=1, source_target_pairs={{0,129},{1,128},{2,131},{3,130},{4,133},{5,132},{6,135},{7,134},{8... | collective-permute-start | bytes 1572872 | tf_op jit(solution)/shard_map/ppermute | solution.py:564
  182.9 19.6 %collective-permute-start.27 = (bf16[128,2048]{1,0:T(8,128)(2,1)}, bf16[128,2048]{1,0:T(8,128)(2,1)S(1)}, u32[]{:S(2)}, u32[]{:S(2)}) collective-permute-start(bf16[128,2048]{1,0:T(8,128)(2,1)} %get-tuple-element.102), channel_id=1, source_target_pairs={{128,129},{129,128},{130,131},{131,130},{132,133},{133,132},{134,1... | collective-permute-start | bytes 1572872 | tf_op jit(solution)/shard_map/ppermute | solution.py:564
  189.6 14.9 %collective-permute-start.23 = (bf16[128,2048]{1,0:T(8,128)(2,1)S(1)}, bf16[128,2048]{1,0:T(8,128)(2,1)}, u32[]{:S(2)}, u32[]{:S(2)}) collective-permute-start(bf16[128,2048]{1,0:T(8,128)(2,1)S(1)} %copy-done.3), channel_id=1, source_target_pairs={{128,0},{129,1},{130,2},{131,3},{132,4},{133,5},{134,6},{135,7},{1... | collective-permute-start | bytes 1572872 | tf_op jit(solution)/shard_map/ppermute | solution.py:561
  190.9 20.6 %collective-permute-start.25 = (bf16[128,2048]{1,0:T(8,128)(2,1)}, bf16[128,2048]{1,0:T(8,128)(2,1)}, u32[]{:S(2)}, u32[]{:S(2)}) collective-permute-start(bf16[128,2048]{1,0:T(8,128)(2,1)} %get-tuple-element.100), channel_id=1, source_target_pairs={{128,1},{129,0},{130,3},{131,2},{132,5},{133,4},{134,7},{135,6},{1... | collective-permute-start | bytes 1572872 | tf_op jit(solution)/shard_map/ppermute | solution.py:564
  192.2 19.6 %collective-permute-start.24 = (bf16[128,2048]{1,0:T(8,128)(2,1)}, bf16[128,2048]{1,0:T(8,128)(2,1)}, u32[]{:S(2)}, u32[]{:S(2)}) collective-permute-start(bf16[128,2048]{1,0:T(8,128)(2,1)} %get-tuple-element.100), channel_id=1, source_target_pairs={{0,1},{1,0},{2,3},{3,2},{4,5},{5,4},{6,7},{7,6},{8,9},{9,8},{10,11... | collective-permute-start | bytes 1572872 | tf_op jit(solution)/shard_map/ppermute | solution.py:564
  200.2 19.5 %collective-permute-start.19 = (f32[16,128]{1,0:T(8,128)S(1)}, f32[16,128]{1,0:T(8,128)S(1)}, u32[]{:S(2)}, u32[]{:S(2)}) collective-permute-start(f32[16,128]{1,0:T(8,128)S(1)} %get-tuple-element.92.refs_4_), channel_id=1, source_target_pairs={{0,129},{1,128},{2,131},{3,130},{4,133},{5,132},{6,135},{7,134},{8... | collective-permute-start | bytes 24584 | tf_op jit(solution)/shard_map/ppermute | solution.py:564
  202.5 17.2 %collective-permute-start.18 = (f32[16,128]{1,0:T(8,128)S(1)}, f32[16,128]{1,0:T(8,128)S(1)}, u32[]{:S(2)}, u32[]{:S(2)}) collective-permute-start(f32[16,128]{1,0:T(8,128)S(1)} %get-tuple-element.92.refs_4_), channel_id=1, source_target_pairs={{0,1},{1,0},{2,3},{3,2},{4,5},{5,4},{6,7},{7,6},{8,9},{9,8},{10,11... | collective-permute-start | bytes 24584 | tf_op jit(solution)/shard_map/ppermute | solution.py:564
  204.4 15.2 %collective-permute-start.17 = (f32[144,128]{1,0:T(8,128)S(1)}, f32[144,128]{1,0:T(8,128)S(1)}, u32[]{:S(2)}, u32[]{:S(2)}) collective-permute-start(f32[144,128]{1,0:T(8,128)S(1)} %get-tuple-element.91), channel_id=1, source_target_pairs={{0,128},{128,0},{1,129},{129,1},{2,130},{130,2},{3,131},{131,3},{4... | collective-permute-start | bytes 221192 | tf_op jit(solution)/shard_map/ppermute | solution.py:561
  (23 other events, 45.2 us)
